TPU v7x, 256 devices: a whole 4x4x8 slice. The times are simulated.
256 devices in a mesh: space: 64 (over y, z, core), chan: 4 (over x).
Axes of the slice: x: 4, y: 4, z: 8, core: 2. Of those that a mesh axis runs over, the one named last changes fastest.
Arguments:
- volume: bfloat16 [16, 256, 128, 128], P(None, 'space', 'chan'), may hold values from -6 to 6
- kernel: bfloat16 [27, 128, 128], P(None, None, 'chan'), may hold values from -0.109375 to 0.109375
- bias: float32 [128], P('chan'), may hold values from -3 to 3
- cotangent: bfloat16 [16, 256, 128, 128], P(None, 'space', 'chan'), may hold values from -6 to 6
Outputs:
- output: bfloat16 [16, 256, 128, 128], P(None, 'space', 'chan')
- volume_grad: bfloat16 [16, 256, 128, 128], P(None, 'space', 'chan')
All inputs are finite; a program needn't handle non-finite values.
Results may differ from a plain program's by a relative error of at most 0.001.
Values may be sent and summed in bfloat16 or wider, within the bound.
No kernel may reach another device: no remote copies, remote signals or barrier semaphores. Data moves between devices by JAX's collectives and lax.ppermute only.
A program may use at most 128 MiB of HBM per device.

v0:
```python
import jax
import jax.numpy as jnp
from jax import lax
from jax.sharding import PartitionSpec as P


def in_order(tiles, dim):
    tiles = jnp.moveaxis(tiles, 0, dim)
    dims = tiles.shape
    return tiles.reshape(*dims[:dim], dims[dim] * dims[dim + 1], *dims[dim + 2 :])


def sent_to_all(x, axis):
    copies = jnp.broadcast_to(x, (lax.axis_size(axis), *x.shape))
    return lax.all_to_all(copies, axis, split_axis=0, concat_axis=0, tiled=True)


def collect(x, axis, dim):
    return in_order(sent_to_all(x, axis), dim)


def with_halo(block, sides, width):
    for axis, dim in sides:
        count = lax.axis_size(axis)
        forward = [(i, i + 1) for i in range(count - 1)]
        backward = [(target, source) for source, target in forward]
        low = lax.ppermute(
            lax.slice_in_dim(block, block.shape[dim] - width, None, axis=dim), axis, forward
        )
        high = lax.ppermute(lax.slice_in_dim(block, 0, width, axis=dim), axis, backward)
        block = jnp.concatenate([low, block, high], axis=dim)
    return block


def in_blocks(x, dim, size):
    dims = x.shape
    tiles = x.reshape(*dims[:dim], size, dims[dim] // size, *dims[dim + 1 :])
    return jnp.moveaxis(tiles, dim, 0)


def sum_at_owner(x, axis, dim):
    size = lax.axis_size(axis)
    tiles = lax.all_to_all(in_blocks(x, dim, size), axis, 0, 0, tiled=True)
    return jnp.sum(tiles, axis=0)


def shifted_terms(padded, weights, forward, total):
    planes = padded.shape[0] - 2
    rows = padded.shape[1] - 2
    columns = padded.shape[3] - 2
    channels = padded.shape[2]
    group = 9 if channels < 128 else 1
    for first in range(0, 27, group):
        windows = []
        weight_list = []
        for offset in range(first, first + group):
            steps_at = (offset // 9, offset // 3 % 3, offset % 3)
            if not forward:
                steps_at = (2 - steps_at[0], 2 - steps_at[1], 2 - steps_at[2])
            windows.append(
                padded[
                    steps_at[0] : steps_at[0] + planes,
                    steps_at[1] : steps_at[1] + rows,
                    :,
                    steps_at[2] : steps_at[2] + columns,
                ]
            )
            weight_list.append(weights[offset])
        if group == 1:
            stacked = windows[0]
        else:
            stacked = jnp.concatenate(windows, axis=2)
        if forward:
            weight_now = weight_list[0]
            total = total + jnp.einsum(
                "xyiz,io->xyoz", stacked, weight_now, preferred_element_type=jnp.float32
            )
        else:
            weight_now = jnp.concatenate(weight_list, axis=1)
            total = total + jnp.einsum(
                "xyoz,io->xyiz", stacked, weight_now, preferred_element_type=jnp.float32
            )
    return total


def pad_sides(field):
    return jnp.pad(field, ((1, 1), (0, 0), (0, 0), (1, 1)))


def per_device(volume, kernel, bias, cotangent):
    start_sum = jnp.zeros(volume.shape, jnp.float32) + bias[None, None, :, None]
    whole = collect(volume, "chan", 2)
    with_rows = with_halo(whole, (("space", 1),), 1)
    forward_sum = shifted_terms(pad_sides(with_rows), kernel, True, start_sum)
    output = forward_sum.astype(jnp.bfloat16)
    grad_rows = with_halo(cotangent, (("space", 1),), 1)
    empty = jnp.zeros(
        (volume.shape[0], volume.shape[1], kernel.shape[1], volume.shape[3]), jnp.float32
    )
    partials = shifted_terms(pad_sides(grad_rows), kernel, False, empty)
    volume_grad = sum_at_owner(partials, "chan", 2)
    return (output, volume_grad.astype(jnp.bfloat16))


def solution(mesh):
    return jax.shard_map(
        per_device,
        mesh=mesh,
        in_specs=(
            P(None, "space", "chan", None),
            P(None, None, "chan"),
            P("chan"),
            P(None, "space", "chan", None),
        ),
        out_specs=(P(None, "space", "chan", None), P(None, "space", "chan", None)),
        check_vma=False,
    )
```

profile of v0, /device:TPU:65, one launch (start us, length us, event | category | flops | bytes accessed | tf_op | source)
XLA Modules:
  0.0 118.2 jit_solution(14159355303752064773)
XLA Ops:
  0.6 1.1 fusion.247
  1.7 4.1 %collective-permute-start.2 = (bf16[16,1,32,128]{3,2,1,0:T(8,128)(2,1)S(1)}, bf16[16,1,32,128]{3,2,1,0:T(8,128)(2,1)S(1)}, u32[]{:S(2)}, u32[]{:S(2)}) collective-permute-start(bf16[16,1,32,128]{3,2,1,0:T(8,128)(2,1)S(1)} %get-tuple-element.26), channel_id=1, source_target_pairs={{0,4},{4,8},{8,12},{12,16},{16,20},{20,24},{24,28},{28,32},{32,36}... | collective-permute-start | bytes 393224 | tf_op jit(solution)/shard_map/ppermute | solution.py:27
  5.8 1.9 %collective-permute-start.3 = (bf16[16,1,32,128]{3,2,1,0:T(8,128)(2,1)S(1)}, bf16[16,1,32,128]{3,2,1,0:T(8,128)(2,1)S(1)}, u32[]{:S(2)}, u32[]{:S(2)}) collective-permute-start(bf16[16,1,32,128]{3,2,1,0:T(8,128)(2,1)S(1)} %get-tuple-element.27), channel_id=1, source_target_pairs={{4,0},{8,4},{12,8},{16,12},{20,16},{24,20},{28,24},{32,28},{36,32}... | collective-permute-start | bytes 393224 | tf_op jit(solution)/shard_map/ppermute | solution.py:30
  7.8 2.9 %broadcast_in_dim.4 = bf16[4,16,4,32,128]{4,3,2,1,0:T(8,128)(2,1)} broadcast(bf16[16,4,32,128]{3,2,1,0:T(8,128)(2,1)} %param.4), dimensions={1,2,3,4} | broadcast | bytes 2621440 | tf_op jit(solution)/shard_map/broadcast_in_dim | solution.py:14
  10.6 4.0 %all-to-all-start = ((bf16[4,16,4,32,128]{4,3,2,1,0:T(8,128)(2,1)}), bf16[4,16,4,32,128]{4,3,2,1,0:T(8,128)(2,1)S(1)}, u32[]{:S(2)}, u32[]{:S(2)}) async-start(bf16[4,16,4,32,128]{4,3,2,1,0:T(8,128)(2,1)} %broadcast_in_dim.4), calls=%async_computation | async-start | bytes 4194304 | tf_op jit(solution)/shard_map/all_to_all | solution.py:15
  14.8 1.1 select_maximum_fusion.2
  20.0 0.9 slice_dynamic-update-slice_fusion.10
  21.8 3.4 %fusion.187 = f32[128,16,4,128]{3,0,2,1:T(8,128)} fusion(bf16[16,4,288,128]{3,2,1,0:T(8,128)(2,1)S(1)} %get-tuple-element.6, bf16[128,288]{0,1:T(8,128)(2,1)S(1)} %get-tuple-element.30), kind=kOutput, calls=%fused_computation.179 | convolution fusion | flops 603979776 | bytes 8986624 | tf_op jit(solution)/shard_map/xyoz,io->xyiz/dot_general | solution.py:80
  25.2 3.3 %fusion.184 = f32[128,16,4,128]{3,0,2,1:T(8,128)} fusion(bf16[16,4,288,128]{3,2,1,0:T(8,128)(2,1)S(1)} %slice_dynamic-update-slice_fusion, bf16[128,288]{0,1:T(8,128)(2,1)S(1)} %constant_dynamic-update-slice_fusion.19), kind=kOutput, calls=%fused_computation.176 | convolution fusion | flops 603979776 | bytes 8986624 | tf_op jit(solution)/shard_map/xyoz,io->xyiz/dot_general | solution.py:80
  28.5 12.1 %all-to-all-done = bf16[4,16,4,32,128]{4,3,2,1,0:T(8,128)(2,1)S(1)} async-done(((bf16[4,16,4,32,128]{4,3,2,1,0:T(8,128)(2,1)}), bf16[4,16,4,32,128]{4,3,2,1,0:T(8,128)(2,1)S(1)}, u32[]{:S(2)}, u32[]{:S(2)}) %all-to-all-start) | async-done | bytes 2097184 | tf_op jit(solution)/shard_map/all_to_all | solution.py:15
  40.6 1.3 %copy-done.2 = bf16[4,16,4,32,128]{4,3,2,1,0:T(8,128)(2,1)} copy-done((bf16[4,16,4,32,128]{4,3,2,1,0:T(8,128)(2,1)}, bf16[4,16,4,32,128]{4,3,2,1,0:T(8,128)(2,1)S(1)}, u32[]{:S(2)}) %copy-start.2) | copy-done | bytes 2097176
  41.9 2.3 %copy.6 = bf16[16,4,4,32,128]{4,3,2,1,0:T(8,128)(2,1)S(1)} copy(bf16[16,4,4,32,128]{4,3,1,0,2:T(8,128)(2,1)} %bitcast.298) | data formatting | bytes 4194304 | tf_op jit(solution)/shard_map/transpose | solution.py:8
  44.2 1.1 fusion.246
  45.3 5.5 %collective-permute-start = (bf16[16,1,128,128]{3,2,1,0:T(8,128)(2,1)}, bf16[16,1,128,128]{3,2,1,0:T(8,128)(2,1)S(1)}, u32[]{:S(2)}, u32[]{:S(2)}) collective-permute-start(bf16[16,1,128,128]{3,2,1,0:T(8,128)(2,1)} %get-tuple-element.2), channel_id=1, source_target_pairs={{0,4},{4,8},{8,12},{12,16},{16,20},{20,24},{24,28},{28,32},{32,36}... | collective-permute-start | bytes 1572872 | tf_op jit(solution)/shard_map/ppermute | solution.py:27
  50.8 1.9 %collective-permute-start.1 = (bf16[16,1,128,128]{3,2,1,0:T(8,128)(2,1)}, bf16[16,1,128,128]{3,2,1,0:T(8,128)(2,1)S(1)}, u32[]{:S(2)}, u32[]{:S(2)}) collective-permute-start(bf16[16,1,128,128]{3,2,1,0:T(8,128)(2,1)} %get-tuple-element.3), channel_id=1, source_target_pairs={{4,0},{8,4},{12,8},{16,12},{20,16},{24,20},{28,24},{32,28},{36,32}... | collective-permute-start | bytes 1572872 | tf_op jit(solution)/shard_map/ppermute | solution.py:30
  52.7 4.9 %add_add_fusion = f32[128,16,4,128]{3,0,2,1:T(8,128)S(1)} fusion(f32[128,16,4,128]{3,0,2,1:T(8,128)} %fusion.184, f32[128,16,4,128]{3,0,2,1:T(8,128)S(1)} %copy-done, bf16[16,4,288,128]{3,2,1,0:T(8,128)(2,1)} %copy-done.3, bf16[128,288]{0,1:T(8,128)(2,1)S(1)} %get-tuple-element.28), kind=kOutput, calls=%fused_computation.17 | convolution fusion | flops 606076928 | bytes 17375232 | tf_op jit(solution)/shard_map/xyoz,io->xyiz/dot_general | solution.py:80
  57.6 2.7 %copy.39 = f32[16,4,4,32,128]{4,3,1,0,2:T(8,128)} copy(f32[16,4,4,32,128]{4,3,2,1,0:T(8,128)S(1)} %bitcast.297) | data formatting | bytes 8388608 | tf_op jit(solution)/shard_map/reshape | solution.py:37
  60.3 4.9 %all-to-all-start.1 = ((f32[4,16,4,32,128]{4,3,2,1,0:T(8,128)}), f32[4,16,4,32,128]{4,3,2,1,0:T(8,128)}, u32[]{:S(2)}, u32[]{:S(2)}) async-start(f32[4,16,4,32,128]{4,3,2,1,0:T(8,128)} %bitcast.296), calls=%async_computation.1 | async-start | bytes 8388608 | tf_op jit(solution)/shard_map/all_to_all | solution.py:43
  65.6 4.3 %select_maximum_fusion = bf16[18,6,128,130]{3,2,1,0:T(8,128)(2,1)S(1)} fusion(bf16[16,1,128,128]{3,2,1,0:T(8,128)(2,1)S(1)} %collective-permute-done.1, bf16[16,4,128,128]{3,2,1,0:T(8,128)(2,1)S(1)} %bitcast.293, bf16[16,1,128,128]{3,2,1,0:T(8,128)(2,1)S(1)} %collective-permute-done), kind=kLoop, calls=%fused_computation.7 | loop fusion | flops 34145280 | bytes 6739968 | tf_op jit(solution)/shard_map/concatenate | solution.py:31
  83.2 1.1 fusion.89
  86.5 1.5 %fusion.161 = f32[16,4,128,32]{2,3,1,0:T(8,128)S(1)} fusion(f32[16,4,128,32]{2,3,1,0:T(8,128)S(1)} %fusion.202, f32[16,4,128,32]{2,3,1,0:T(8,128)S(1)} %fusion.35, f32[16,4,128,32]{2,3,1,0:T(8,128)S(1)} %fusion.37, f32[16,4,128,32]{2,3,1,0:T(8,128)S(1)} %fusion.39, f32[16,4,128,32]{2,3,1,0:T(8,128)S(1)} %fusion.41, f32[16,4,128,32]{2,3,1,0:T(8,128)S(1)} %fusion.43, ...), kind=kOutput, calls=%fused_computation.113 | convolution fusion | flops 70778880 | bytes 16785920 | tf_op jit(solution)/shard_map/xyiz,io->xyoz/dot_general | solution.py:75
  88.0 2.4 %fusion.179 = bf16[16,4,32,128]{3,2,1,0:T(8,128)(2,1)} fusion(f32[16,4,32,128]{3,2,1,0:T(8,128)S(1)} %fusion.107, f32[16,4,32,128]{3,2,1,0:T(8,128)S(1)} %fusion.104, f32[16,4,32,128]{3,2,1,0:T(8,128)S(1)} %fusion.101, f32[16,4,32,128]{3,2,1,0:T(8,128)S(1)} %fusion.98, f32[16,4,32,128]{3,2,1,0:T(8,128)S(1)} %fusion.95, f32[16,4,32,128]{3,2,1,0:T(8,128)S(1)} %fusion.92, ...), kind=kOutput, calls=%fused_computation.119 | convolution fusion | flops 70778880 | bytes 16261120 | tf_op jit(solution)/shard_map/xyiz,io->xyoz/dot_general | solution.py:75
  90.4 24.1 %all-to-all-done.1 = f32[4,16,4,32,128]{4,3,2,1,0:T(8,128)} async-done(((f32[4,16,4,32,128]{4,3,2,1,0:T(8,128)}), f32[4,16,4,32,128]{4,3,2,1,0:T(8,128)}, u32[]{:S(2)}, u32[]{:S(2)}) %all-to-all-start.1) | async-done | bytes 4194336 | tf_op jit(solution)/shard_map/all_to_all | solution.py:43
  114.6 3.6 %reduce_sum.9 = bf16[16,4,32,128]{3,2,1,0:T(8,128)(2,1)} reduce(f32[4,16,4,32,128]{4,3,2,1,0:T(8,128)} %all-to-all-done.1, f32[]{:T(128)} %constant.4.clone.1), dimensions={0}, to_apply=%region_0.1 | reduce | flops 786432 | bytes 4718596 | tf_op jit(solution)/shard_map/reduce_sum | solution.py:44
  (62 shorter events, 20.9 us)
Async XLA Ops:
  0.6 14.2 %copy-start.1 = (bf16[16,4,32,128]{3,2,1,0:T(8,128)(2,1)S(1)}, bf16[16,4,32,128]{3,2,1,0:T(8,128)(2,1)}, u32[]{:S(2)}) copy-start(bf16[16,4,32,128]{3,2,1,0:T(8,128)(2,1)} %param.7) | copy-start | bytes 1572868
  0.6 14.0 %copy-start.4 = (bf16[27,128,32]{1,2,0:T(8,128)(2,1)S(1)}, bf16[27,128,32]{1,2,0:T(8,128)(2,1)}, u32[]{:S(2)}) copy-start(bf16[27,128,32]{1,2,0:T(8,128)(2,1)} %param.5) | copy-start | bytes 663556
  1.7 13.1 %collective-permute-start.2 = (bf16[16,1,32,128]{3,2,1,0:T(8,128)(2,1)S(1)}, bf16[16,1,32,128]{3,2,1,0:T(8,128)(2,1)S(1)}, u32[]{:S(2)}, u32[]{:S(2)}) collective-permute-start(bf16[16,1,32,128]{3,2,1,0:T(8,128)(2,1)S(1)} %get-tuple-element.26), channel_id=1, source_target_pairs={{0,4},{4,8},{8,12},{12,16},{16,20},{20,24},{24,28},{28,32},{32,36}... | collective-permute-start | bytes 393224 | tf_op jit(solution)/shard_map/ppermute | solution.py:27
  5.8 9.0 %collective-permute-start.3 = (bf16[16,1,32,128]{3,2,1,0:T(8,128)(2,1)S(1)}, bf16[16,1,32,128]{3,2,1,0:T(8,128)(2,1)S(1)}, u32[]{:S(2)}, u32[]{:S(2)}) collective-permute-start(bf16[16,1,32,128]{3,2,1,0:T(8,128)(2,1)S(1)} %get-tuple-element.27), channel_id=1, source_target_pairs={{4,0},{8,4},{12,8},{16,12},{20,16},{24,20},{28,24},{32,28},{36,32}... | collective-permute-start | bytes 393224 | tf_op jit(solution)/shard_map/ppermute | solution.py:30
  10.6 29.9 %all-to-all-start = ((bf16[4,16,4,32,128]{4,3,2,1,0:T(8,128)(2,1)}), bf16[4,16,4,32,128]{4,3,2,1,0:T(8,128)(2,1)S(1)}, u32[]{:S(2)}, u32[]{:S(2)}) async-start(bf16[4,16,4,32,128]{4,3,2,1,0:T(8,128)(2,1)} %broadcast_in_dim.4), calls=%async_computation | async-start | bytes 4194304 | tf_op jit(solution)/shard_map/all_to_all | solution.py:15
  21.6 3.5 %copy-start.3 = (bf16[16,4,288,128]{3,2,1,0:T(8,128)(2,1)}, bf16[16,4,288,128]{3,2,1,0:T(8,128)(2,1)S(1)}, u32[]{:S(2)}) copy-start(bf16[16,4,288,128]{3,2,1,0:T(8,128)(2,1)S(1)} %get-tuple-element.4) | copy-start | bytes 14155780
  40.6 1.3 %copy-start.2 = (bf16[4,16,4,32,128]{4,3,2,1,0:T(8,128)(2,1)}, bf16[4,16,4,32,128]{4,3,2,1,0:T(8,128)(2,1)S(1)}, u32[]{:S(2)}) copy-start(bf16[4,16,4,32,128]{4,3,2,1,0:T(8,128)(2,1)S(1)} %all-to-all-done) | copy-start | bytes 6291460
  41.9 10.8 %copy-start = (f32[128,16,4,128]{3,0,2,1:T(8,128)S(1)}, f32[128,16,4,128]{3,0,2,1:T(8,128)}, u32[]{:S(2)}) copy-start(f32[128,16,4,128]{3,0,2,1:T(8,128)} %fusion.187) | copy-start | bytes 12582916
  45.3 20.3 %collective-permute-start = (bf16[16,1,128,128]{3,2,1,0:T(8,128)(2,1)}, bf16[16,1,128,128]{3,2,1,0:T(8,128)(2,1)S(1)}, u32[]{:S(2)}, u32[]{:S(2)}) collective-permute-start(bf16[16,1,128,128]{3,2,1,0:T(8,128)(2,1)} %get-tuple-element.2), channel_id=1, source_target_pairs={{0,4},{4,8},{8,12},{12,16},{16,20},{20,24},{24,28},{28,32},{32,36}... | collective-permute-start | bytes 1572872 | tf_op jit(solution)/shard_map/ppermute | solution.py:27
  50.8 14.8 %collective-permute-start.1 = (bf16[16,1,128,128]{3,2,1,0:T(8,128)(2,1)}, bf16[16,1,128,128]{3,2,1,0:T(8,128)(2,1)S(1)}, u32[]{:S(2)}, u32[]{:S(2)}) collective-permute-start(bf16[16,1,128,128]{3,2,1,0:T(8,128)(2,1)} %get-tuple-element.3), channel_id=1, source_target_pairs={{4,0},{8,4},{12,8},{16,12},{20,16},{24,20},{28,24},{32,28},{36,32}... | collective-permute-start | bytes 1572872 | tf_op jit(solution)/shard_map/ppermute | solution.py:30
  60.3 54.3 %all-to-all-start.1 = ((f32[4,16,4,32,128]{4,3,2,1,0:T(8,128)}), f32[4,16,4,32,128]{4,3,2,1,0:T(8,128)}, u32[]{:S(2)}, u32[]{:S(2)}) async-start(f32[4,16,4,32,128]{4,3,2,1,0:T(8,128)} %bitcast.296), calls=%async_computation.1 | async-start | bytes 8388608 | tf_op jit(solution)/shard_map/all_to_all | solution.py:43
  84.3 2.2 %copy-start.5 = (f32[32]{0:T(128)S(1)}, f32[32]{0:T(128)}, u32[]{:S(2)}) copy-start(f32[32]{0:T(128)} %param.6) | copy-start | bytes 388
where the time goes:
time: 119 us; the launch traced here: 118 us
  waiting for transfers between devices  36.3 us (31%)
  matrix products  32.5 us (27%)
  starting transfers between devices  22.3 us (19%)
  local copies, waits for them, and re-layouts  17.1 us (14%)
  other arithmetic  9.13 us (8%)
    all_to_all x1, waiting for transfers between devices, sum_at_owner(): tiles = lax.all_to_all(in_blocks(x, dim, size), axis, 0, 0, tiled=True)  24.1 us
    dot_general x27, matrix products, shifted_terms(): jnp.einsum('xyiz,io->xyoz', stacked, weight_now, preferred_element_type=j...  20.9 us
    all_to_all x1, waiting for transfers between devices, sent_to_all(): return lax.all_to_all(copies, axis, split_axis=0, concat_axis=0, tiled=True)  12.1 us
    dot_general x3, matrix products, shifted_terms(): jnp.einsum('xyoz,io->xyiz', stacked, weight_now, preferred_element_type=j...  11.6 us
    ppermute x2, starting transfers between devices, with_halo(): lax.ppermute(lax.slice_in_dim(block, block.shape[dim] - width, None, axis...  9.56 us
    unnamed x30, local copies, waits for them, and re-layouts  6.3 us
    concatenate x2, other arithmetic, with_halo(): block = jnp.concatenate([low, block, high], axis=dim)  5.32 us
    all_to_all x1, starting transfers between devices, sum_at_owner(): tiles = lax.all_to_all(in_blocks(x, dim, size), axis, 0, 0, tiled=True)  4.86 us
  transfers between devices with their start and end apart: 6, of which 2 were waited for; matrix products, arithmetic and copies ran while one was open for 42% of the time, Pallas kernels for 0%

commit v1 on v0

v1 whole, which is shorter than its diff:
```python
import jax
import jax.numpy as jnp
from jax import lax
from jax.experimental import pallas as pl
from jax.experimental.pallas import tpu as pltpu
from jax.sharding import PartitionSpec as P


MIB = 1024 * 1024
BF16 = jnp.bfloat16
ANY = pl.BlockSpec(memory_space=pl.ANY)
HBM = pl.BlockSpec(memory_space=pltpu.HBM)
VMEM = pl.BlockSpec(memory_space=pltpu.VMEM)
SMEM = pl.BlockSpec(memory_space=pltpu.SMEM)


def shifted(x, steps):
    count = lax.axis_size("chan")
    return lax.ppermute(x, "chan", [(i, (i + steps) % count) for i in range(count)])


def swapped_rows(on_chip, off_chip):
    count = lax.axis_size("space")
    near = [(i, i ^ 1) for i in range(count)]
    far = [(i, i - 1 if i % 2 == 0 else i + 1) for i in range(1, count - 1)]
    return lax.ppermute(on_chip, "space", near), lax.ppermute(off_chip, "space", far)


def copies(plan, sems):
    started = []
    for n, (source, target) in enumerate(plan):
        copy = pltpu.make_async_copy(source, target, sems.at[n])
        copy.start()
        started.append(copy)
    return started


def pack_own(volume, cotangent):
    planes, rows, part, cells = volume.shape

    def body(v, c, ev, ec, sems):
        plan = []
        for x, edge in ((v, ev), (c, ec)):
            plan.append((x.at[:, 0], edge.at[0]))
            plan.append((x.at[:, rows - 1], edge.at[1]))
        for copy in copies(plan, sems):
            copy.wait()

    out = jax.ShapeDtypeStruct((2, planes, part, cells), BF16)
    return pl.pallas_call(
        body,
        out_shape=(out, out),
        in_specs=[HBM, HBM],
        out_specs=[VMEM] * 2,
        scratch_shapes=[pltpu.SemaphoreType.DMA((4,))],
        compiler_params=pltpu.CompilerParams(vmem_limit_bytes=2 * MIB),
        name="pack_own",
    )(volume, cotangent)


def pack_near(core, volume, cotangent, vol_near, cot_near):
    planes, rows, part, cells = volume.shape
    inside = rows - 2

    def body(core_ref, v, c, vn, cn, ev, ec, m_up, m_down, on_chip, off_chip, sems):
        inner = jnp.where(core_ref[0] == 0, rows - 1, 0)
        outer = rows - 1 - inner
        plan = []
        for x, edge in ((vn, ev), (cn, ec)):
            plan.append((x.at[:, 0], edge.at[0]))
            plan.append((x.at[:, rows - 1], edge.at[1]))
        for r in range(inside):
            for n, x in enumerate((c, vn)):
                plan.append((x.at[:, 1 + r], m_up.at[n * inside + r]))
            for n, x in enumerate((v, cn)):
                plan.append((x.at[:, 1 + r], m_down.at[n * inside + r]))
        for n, x in enumerate((v, c, vn, cn)):
            plan.append((x.at[:, inner], on_chip.at[n]))
            plan.append((x.at[:, outer], off_chip.at[n]))
        for copy in copies(plan, sems):
            copy.wait()

    def out(n):
        return jax.ShapeDtypeStruct((n, planes, part, cells), BF16)

    return pl.pallas_call(
        body,
        out_shape=(out(2), out(2), out(2 * inside), out(2 * inside), out(4), out(4)),
        in_specs=[SMEM, HBM, HBM, ANY, ANY],
        out_specs=[VMEM] * 6,
        scratch_shapes=[pltpu.SemaphoreType.DMA((12 + 4 * inside,))],
        compiler_params=pltpu.CompilerParams(vmem_limit_bytes=6 * MIB),
        name="pack_near",
    )(core, volume, cotangent, vol_near, cot_near)


def pack_far(core, blocks):
    _, planes, part, cells = blocks[0].shape
    count = len(blocks)

    def body(core_ref, *refs):
        *held, on_chip, off_chip, sems = refs
        side = jnp.where(core_ref[0] == 0, 1, 0)
        plan = []
        for n, x in enumerate(held):
            plan.append((x.at[side], on_chip.at[n]))
            plan.append((x.at[1 - side], off_chip.at[n]))
        for copy in copies(plan, sems):
            copy.wait()

    out = jax.ShapeDtypeStruct((count, planes, part, cells), BF16)
    return pl.pallas_call(
        body,
        out_shape=(out, out),
        in_specs=[SMEM, *[ANY] * count],
        out_specs=[VMEM] * 2,
        scratch_shapes=[pltpu.SemaphoreType.DMA((2 * count,))],
        compiler_params=pltpu.CompilerParams(vmem_limit_bytes=4 * MIB),
        name="pack_far",
    )(core, *blocks)


def pack_taps(own, size):
    taps, outs, chans = own.shape
    part = chans // size
    groups = -(-taps // size)

    def body(own_ref, send_ref):
        empty = jnp.zeros((outs, part), jnp.float32)
        for g in range(groups):
            quad = [
                own_ref[taps - 1 - t].astype(jnp.float32) if t < taps else None
                for t in range(g * size, (g + 1) * size)
            ]
            for j in range(size):
                pieces = [empty if q is None else q[:, j * part : (j + 1) * part] for q in quad]
                send_ref[j, g] = jnp.concatenate(pieces, axis=1).astype(BF16)

    return pl.pallas_call(
        body,
        out_shape=jax.ShapeDtypeStruct((size, groups, outs, chans), BF16),
        in_specs=[VMEM],
        out_specs=VMEM,
        compiler_params=pltpu.CompilerParams(vmem_limit_bytes=4 * MIB),
        name="pack_taps",
    )(own)


def weights(own, received, turns):
    taps, outs, chans = own.shape
    size, groups = received.shape[:2]
    part = chans // size
    half = chans // 2

    def body(turn_ref, own_ref, got_ref, ahead_a, ahead_b, back_a, back_b):
        low = lax.broadcasted_iota(jnp.int32, (outs, chans), 1) < half

        def put(refs, tiles):
            for at in range(0, 9, 2):
                for c in range(3):
                    here = slice(c * outs, (c + 1) * outs)
                    even = tiles[3 * at + c]
                    if at == 8:
                        refs[0][here, at * half :] = even[:, :half].astype(BF16)
                        refs[1][here, at * half :] = even[:, half:].astype(BF16)
                        continue
                    odd = tiles[3 * at + 3 + c]
                    both = slice(at * half, (at + 2) * half)
                    first = jnp.where(low, even, pltpu.roll(odd, half, 1))
                    second = jnp.where(low, pltpu.roll(even, half, 1), odd)
                    refs[0][here, both] = first.astype(BF16)
                    refs[1][here, both] = second.astype(BF16)

        tiles = [pltpu.roll(own_ref[t].astype(jnp.float32), turn_ref[0], 1) for t in range(taps)]
        put((ahead_a, ahead_b), tiles)
        tiles = []
        for g in range(groups):
            tile = jnp.concatenate([got_ref[s, g] for s in range(size)], axis=0)
            tile = pltpu.roll(tile.astype(jnp.float32).T, turn_ref[1], 1)
            tiles += [tile[t * part : (t + 1) * part] for t in range(size)]
        put((back_a, back_b), tiles)

    out = jax.ShapeDtypeStruct((3 * outs, 9 * half), BF16)
    return pl.pallas_call(
        body,
        out_shape=(out,) * 4,
        in_specs=[SMEM, VMEM, VMEM],
        out_specs=[VMEM] * 4,
        compiler_params=pltpu.CompilerParams(vmem_limit_bytes=6 * MIB),
        name="weights",
    )(turns, own, received)


def convolve(x_ref, w_ref, start, o_ref):
    planes, rows, outs, cells = o_ref.shape
    chans = x_ref.shape[1] // (rows + 2)
    wide = 2 * cells
    lane = lax.broadcasted_iota(jnp.int32, (outs, wide), 1) % cells
    first = lane == 0
    last = lane == cells - 1

    def plane(p, carry):
        for r in range(0, rows, 2):
            halves = []
            for rr in (r, r + 1):
                stack = [x_ref[p + a, rr * chans : (rr + 3) * chans] for a in range(3)]
                halves.append(jnp.concatenate(stack, axis=0))
            data = jnp.concatenate(halves, axis=1)
            sums = jnp.dot(w_ref[...], data, preferred_element_type=jnp.float32)
            total = sums[outs : 2 * outs]
            total = total + jnp.where(first, 0.0, pltpu.roll(sums[:outs], 1, 1))
            total = total + jnp.where(last, 0.0, pltpu.roll(sums[2 * outs :], wide - 1, 1))
            for n in range(2):
                part = total[:, n * cells : (n + 1) * cells]
                if start is not None:
                    part = part + start(p, r + n)
                o_ref[p, r + n] = part.astype(o_ref.dtype)
        return carry

    lax.fori_loop(0, planes, plane, 0, unroll=8)


def stage(core, parts, tables, starts, dtype, shape, fixed=()):
    planes, rows, part, cells = shape
    operands = []
    for plan in parts:
        for block in plan:
            for x, _ in block:
                if not any(x is y for y in operands):
                    operands.append(x)
    count = len(parts[0])
    chans = count * part

    def place(x):
        return [i for i, y in enumerate(operands) if y is x][0]

    def body(core_ref, *refs):
        held = refs[: len(operands)]
        w_refs = refs[len(operands) : len(operands) + 2]
        s_refs = refs[len(operands) + 2 : len(operands) + 2 + len(starts)]
        o_refs = refs[len(operands) + 2 + len(starts) :][:2]
        *x_refs, sems = refs[len(operands) + 4 + len(starts) :]
        upper = core_ref[0] == 0
        inner = jnp.where(upper, rows + 1, 0)
        outer = rows + 1 - inner
        pending = []
        for n, (x_ref, plan) in enumerate(zip(x_refs, parts)):
            work = []
            for s in range(count):
                for r, (x, index) in enumerate(plan[s]):
                    at = [inner, outer, *range(1, rows + 1)][r]
                    base = at * chans + s * part
                    if r < 2:
                        base = pl.multiple_of(base, part)
                    target = x_ref.at[pl.ds(1, planes), pl.ds(base, part)]
                    work.append((held[place(x)].at[index], target))
            pending.append(copies(work, sems.at[n]))
        zero = jnp.zeros((x_refs[0].shape[1], cells), BF16)
        for x_ref in x_refs:
            x_ref[0] = zero
            x_ref[planes + 1] = zero
        for n in range(2):
            for copy in pending[n]:
                copy.wait()
            begin = None
            if n < len(starts):
                if len(starts) == 1:
                    begin = lambda p, r: s_refs[0][...]
                else:
                    begin = lambda p, r, n=n: s_refs[n][p, r]
            convolve(x_refs[n], w_refs[n], begin, o_refs[n])

    out = jax.ShapeDtypeStruct(shape, dtype)
    padded = pltpu.VMEM((planes + 2, (rows + 2) * chans, cells), BF16)
    places = [HBM if any(x is y for y in fixed) else ANY for x in operands]
    return pl.pallas_call(
        body,
        out_shape=(out, out),
        in_specs=[SMEM, *places, *[VMEM] * (2 + len(starts))],
        out_specs=[VMEM, VMEM],
        scratch_shapes=[padded, padded, pltpu.SemaphoreType.DMA((2, count * (rows + 2)))],
        compiler_params=pltpu.CompilerParams(vmem_limit_bytes=12 * MIB),
        cost_estimate=pl.CostEstimate(
            flops=4 * 27 * chans * part * planes * rows * cells,
            bytes_accessed=6 * MIB,
            transcendentals=0,
        ),
    )(core, *operands, *tables, *starts)


def per_device(volume, kernel, bias, cotangent):
    size = lax.axis_size("chan")
    me = lax.axis_index("chan")
    core = (lax.axis_index("space") % 2).astype(jnp.int32).reshape(1)
    _, rows, part, cells = volume.shape
    every = slice(None)

    vol_left = shifted(volume, 1)
    cot_right = shifted(cotangent, -1)
    vol_edge, cot_edge = pack_own(volume, cotangent)
    cot_left_edge = shifted(cot_edge, 1)
    vol_right_edge = shifted(vol_edge, -1)
    own = jnp.swapaxes(kernel, 1, 2)
    received = lax.all_to_all(pack_taps(own, size), "chan", 0, 0, tiled=True)

    vol_edge, cot_edge, mid_up, mid_down, on_chip, off_chip = pack_near(
        core, volume, cotangent, vol_left, cot_right
    )
    vol_edge, cot_edge = shifted(vol_edge, 1), shifted(cot_edge, -1)
    mid_up, mid_down = shifted(mid_up, 1), shifted(mid_down, -1)
    near = swapped_rows(on_chip, off_chip)

    turn = (size - me) % size
    turns = jnp.stack([(turn + 1) % size, turn]).astype(jnp.int32) * part
    ahead_a, ahead_b, back_a, back_b = weights(own, received, turns)

    on_chip, off_chip = pack_far(core, (vol_right_edge, cot_left_edge, vol_edge, cot_edge))
    far = swapped_rows(on_chip, off_chip)

    def whole(x, pair, n):
        return [(pair[0], n), (pair[1], n), *[(x, (every, r)) for r in range(rows)]]

    def split(edge, middle, half, pair, n):
        inner = [(middle, half * (rows - 2) + r) for r in range(rows - 2)]
        return [(pair[0], n), (pair[1], n), (edge, 0), *inner, (edge, 1)]

    wide = jnp.broadcast_to(bias[:, None], (bias.shape[0], cells))
    sums = stage(
        core,
        [
            [whole(vol_left, near, 2), whole(volume, near, 0)],
            [whole(cotangent, near, 1), whole(cot_right, near, 3)],
        ],
        (ahead_a, back_a),
        (wide,),
        jnp.float32,
        volume.shape,
        (volume, cotangent),
    )
    return stage(
        core,
        [
            [split(vol_right_edge, mid_down, 0, far, 0), split(vol_edge, mid_up, 1, far, 2)],
            [split(cot_edge, mid_down, 1, far, 3), split(cot_left_edge, mid_up, 0, far, 1)],
        ],
        (ahead_b, back_b),
        sums,
        BF16,
        volume.shape,
    )


def solution(mesh):
    spec = P(None, "space", "chan", None)

    return jax.shard_map(
        per_device,
        mesh=mesh,
        in_specs=(spec, P(None, None, "chan"), P("chan"), spec),
        out_specs=(spec, spec),
        check_vma=False,
    )
```

time: 119 us -> 77.9 us (0.65)
  the two profiles are of different devices: /device:TPU:65 before, /device:TPU:24 now
where the time goes in v1:
time: 77.9 us; the launch traced here: 77.5 us
  starting transfers between devices  30.9 us (40%)
  waiting for transfers between devices  21.7 us (28%)
  Pallas kernels  19.1 us (25%)
  local copies, waits for them, and re-layouts  4.68 us (6%)
  between operations  1 us (1%)
    ppermute x8, waiting for transfers between devices, shifted(): lax.ppermute(x, 'chan', [(i, (i + steps) % count) for i in range(count)])  15.3 us
    ppermute x8, starting transfers between devices, shifted(): lax.ppermute(x, 'chan', [(i, (i + steps) % count) for i in range(count)])  13.4 us
    pallas_call x2, Pallas kernels, stage(): pl.pallas_call(body, out_shape=(out, out), in_specs=[SMEM, *places, *[VME...  12.9 us
    ppermute x2, starting transfers between devices, swapped_rows(): lax.ppermute(off_chip, 'space', far)  12.8 us
    all_to_all x1, waiting for transfers between devices, per_device(): received = lax.all_to_all(pack_taps(own, size), 'chan', 0, 0, tiled=True)  6.43 us
    all_to_all x1, starting transfers between devices, per_device(): received = lax.all_to_all(pack_taps(own, size), 'chan', 0, 0, tiled=True)  4.61 us
    unnamed x20, local copies, waits for them, and re-layouts  4.61 us
    pallas_call x1, Pallas kernels, pack_far(): pl.pallas_call(body, out_shape=(out, out), in_specs=[SMEM, *[ANY] * count...  2.4 us
  transfers between devices with their start and end apart: 13, of which 3 were waited for; matrix products, arithmetic and copies ran while one was open for 0% of the time, Pallas kernels for 13%

profile of v1, /device:TPU:24, one launch (start us, length us, event | category | flops | bytes accessed | tf_op | source)
XLA Modules:
  0.0 77.5 jit_solution(2441827109032913923)
XLA Ops:
  0.6 1.6 %collective-permute-start.2 = (bf16[16,4,32,128]{3,2,1,0:T(8,128)(2,1)}, bf16[16,4,32,128]{3,2,1,0:T(8,128)(2,1)S(1)}, u32[]{:S(2)}, u32[]{:S(2)}) collective-permute-start(bf16[16,4,32,128]{3,2,1,0:T(8,128)(2,1)} %refs_3_.1), channel_id=1, source_target_pairs={{0,1},{1,2},{2,3},{3,0},{4,5},{5,6},{6,7},{7,4},{8,9},{9,10},{10,1... | collective-permute-start | bytes 1572872 | tf_op jit(solution)/shard_map/ppermute | solution.py:19
  2.2 1.7 %collective-permute-start.3 = (bf16[16,4,32,128]{3,2,1,0:T(8,128)(2,1)}, bf16[16,4,32,128]{3,2,1,0:T(8,128)(2,1)S(1)}, u32[]{:S(2)}, u32[]{:S(2)}) collective-permute-start(bf16[16,4,32,128]{3,2,1,0:T(8,128)(2,1)} %refs_4_.1), channel_id=1, source_target_pairs={{0,3},{1,0},{2,1},{3,2},{4,7},{5,4},{6,5},{7,6},{8,11},{9,8},{10,9... | collective-permute-start | bytes 1572872 | tf_op jit(solution)/shard_map/ppermute | solution.py:19
  3.9 11.8 %collective-permute-done.2.vn.refs_2_ = bf16[16,4,32,128]{3,2,1,0:T(8,128)(2,1)S(1)} collective-permute-done((bf16[16,4,32,128]{3,2,1,0:T(8,128)(2,1)}, bf16[16,4,32,128]{3,2,1,0:T(8,128)(2,1)S(1)}, u32[]{:S(2)}, u32[]{:S(2)}) %collective-permute-start.2) | collective-permute-done | bytes 524320 | tf_op jit(solution)/shard_map/ppermute | solution.py:19
  15.8 1.0 %copy-done = bf16[16,4,32,128]{3,2,1,0:T(8,128)(2,1)S(1)} copy-done((bf16[16,4,32,128]{3,2,1,0:T(8,128)(2,1)S(1)}, bf16[16,4,32,128]{3,2,1,0:T(8,128)(2,1)}, u32[]{:S(2)}) %copy-start) | copy-done | bytes 524312
  16.8 1.0 %copy-done.2 = bf16[16,4,32,128]{3,2,1,0:T(8,128)(2,1)S(1)} copy-done((bf16[16,4,32,128]{3,2,1,0:T(8,128)(2,1)S(1)}, bf16[16,4,32,128]{3,2,1,0:T(8,128)(2,1)}, u32[]{:S(2)}) %copy-start.2) | copy-done | bytes 524312
  17.9 1.7 %pack_near.1 = (bf16[2,16,32,128]{3,2,1,0:T(8,128)(2,1)S(1)}, bf16[2,16,32,128]{3,2,1,0:T(8,128)(2,1)S(1)}, bf16[4,16,32,128]{3,2,1,0:T(8,128)(2,1)}, bf16[4,16,...) custom-call(s32[1]{0:T(128)} %bitcast.core_ref, ...), custom_call_target="tpu_custom_call" | custom-call | tf_op jit(solution)/shard_map/pack_near/pallas_call | solution.py:86
  19.7 0.1 pack_own.1
  19.9 3.0 %collective-permute-start = (bf16[2,16,32,128]{3,2,1,0:T(8,128)(2,1)S(1)}, bf16[2,16,32,128]{3,2,1,0:T(8,128)(2,1)S(1)}, u32[]{:S(2)}, u32[]{:S(2)}) collective-permute-start(bf16[2,16,32,128]{3,2,1,0:T(8,128)(2,1)S(1)} %get-tuple-element.18), channel_id=1, source_target_pairs={{0,3},{1,0},{2,1},{3,2},{4,7},{5,4},{6,5},{7,6},{8,11},{9,8},{10,9... | collective-permute-start | bytes 786440 | tf_op jit(solution)/shard_map/ppermute | solution.py:19
  22.9 0.6 collective-permute-start.4
  23.5 2.7 %collective-permute-start.5 = (bf16[2,16,32,128]{3,2,1,0:T(8,128)(2,1)S(1)}, bf16[2,16,32,128]{3,2,1,0:T(8,128)(2,1)S(1)}, u32[]{:S(2)}, u32[]{:S(2)}) collective-permute-start(bf16[2,16,32,128]{3,2,1,0:T(8,128)(2,1)S(1)} %get-tuple-element.21), channel_id=1, source_target_pairs={{0,3},{1,0},{2,1},{3,2},{4,7},{5,4},{6,5},{7,6},{8,11},{9,8},{10,9... | collective-permute-start | bytes 786440 | tf_op jit(solution)/shard_map/ppermute | solution.py:19
  26.2 3.4 %collective-permute-done.refs_0_.refs_2_ = bf16[2,16,32,128]{3,2,1,0:T(8,128)(2,1)S(1)} collective-permute-done((bf16[2,16,32,128]{3,2,1,0:T(8,128)(2,1)S(1)}, bf16[2,16,32,128]{3,2,1,0:T(8,128)(2,1)S(1)}, u32[]{:S(2)}, u32[]{:S(2)}) %collective-permute-start) | collective-permute-done | bytes 262176 | tf_op jit(solution)/shard_map/ppermute | solution.py:19
  29.6 6.7 %collective-permute-start.11 = (bf16[4,16,32,128]{3,2,1,0:T(8,128)(2,1)}, bf16[4,16,32,128]{3,2,1,0:T(8,128)(2,1)}, u32[]{:S(2)}, u32[]{:S(2)}) collective-permute-start(bf16[4,16,32,128]{3,2,1,0:T(8,128)(2,1)} %get-tuple-element.29), channel_id=1, source_target_pairs={{4,8},{8,4},{12,16},{16,12},{20,24},{24,20},{28,32},{32,28},{36,40... | collective-permute-start | bytes 1572872 | tf_op jit(solution)/shard_map/ppermute | solution.py:26
  36.3 3.8 %collective-permute-start.8 = (bf16[4,16,32,128]{3,2,1,0:T(8,128)(2,1)}, bf16[4,16,32,128]{3,2,1,0:T(8,128)(2,1)}, u32[]{:S(2)}, u32[]{:S(2)}) collective-permute-start(bf16[4,16,32,128]{3,2,1,0:T(8,128)(2,1)} %get-tuple-element.24), channel_id=1, source_target_pairs={{0,3},{1,0},{2,1},{3,2},{4,7},{5,4},{6,5},{7,6},{8,11},{9,8},{10,9... | collective-permute-start | bytes 1572872 | tf_op jit(solution)/shard_map/ppermute | solution.py:19
  40.1 2.4 %pack_far.1 = (bf16[4,16,32,128]{3,2,1,0:T(8,128)(2,1)}, bf16[4,16,32,128]{3,2,1,0:T(8,128)(2,1)}) custom-call(s32[1]{0:T(128)} %bitcast.core_ref, bf16[2,16,32,128]{3,2,1,0:T(8,128)(2,1)S(1)} %collective-permute-done.refs_0_.refs_2_, bf16[2,16,32,128]{3,2,1,0:T(8,128)(2,1)S(1)} %collective-permute-done.1.refs_1_.refs_7_, ...), custom_call_target="tpu_custom_call" | custom-call | tf_op jit(solution)/shard_map/pack_far/pallas_call | solution.py:112
  42.6 0.8 %copy-done.7 = bf16[4,16,32,128]{3,2,1,0:T(8,128)(2,1)} copy-done((bf16[4,16,32,128]{3,2,1,0:T(8,128)(2,1)}, bf16[4,16,32,128]{3,2,1,0:T(8,128)(2,1)S(1)}, u32[]{:S(2)}) %copy-start.7) | copy-done | bytes 524312
  43.4 6.1 %collective-permute-start.7 = (bf16[4,16,32,128]{3,2,1,0:T(8,128)(2,1)}, bf16[4,16,32,128]{3,2,1,0:T(8,128)(2,1)}, u32[]{:S(2)}, u32[]{:S(2)}) collective-permute-start(bf16[4,16,32,128]{3,2,1,0:T(8,128)(2,1)} %get-tuple-element.23), channel_id=1, source_target_pairs={{4,8},{8,4},{12,16},{16,12},{20,24},{24,20},{28,32},{32,28},{36,40... | collective-permute-start | bytes 1572872 | tf_op jit(solution)/shard_map/ppermute | solution.py:26
  49.6 0.9 %pack_taps.1 = bf16[4,7,32,128]{3,2,1,0:T(8,128)(2,1)} custom-call(bf16[27,32,128]{2,1,0:T(8,128)(2,1)S(1)} %bitcast.4), custom_call_target="tpu_custom_call" | custom-call | tf_op jit(solution)/shard_map/pack_taps/pallas_call | solution.py:139
  50.5 4.6 %all-to-all-start = ((bf16[4,7,32,128]{3,2,1,0:T(8,128)(2,1)}), bf16[4,7,32,128]{3,2,1,0:T(8,128)(2,1)S(1)}, u32[]{:S(2)}, u32[]{:S(2)}) async-start(bf16[4,7,32,128]{3,2,1,0:T(8,128)(2,1)} %pack_taps.1), calls=%async_computation | async-start | bytes 458752 | tf_op jit(solution)/shard_map/all_to_all | solution.py:304
  55.2 6.4 %all-to-all-done.got_ref = bf16[4,7,32,128]{3,2,1,0:T(8,128)(2,1)S(1)} async-done(((bf16[4,7,32,128]{3,2,1,0:T(8,128)(2,1)}), bf16[4,7,32,128]{3,2,1,0:T(8,128)(2,1)S(1)}, u32[]{:S(2)}, u32[]{:S(2)}) %all-to-all-start) | async-done | bytes 229408 | tf_op jit(solution)/shard_map/all_to_all | solution.py:304
  61.6 1.0 %weights.1 = (bf16[96,576]{1,0:T(8,128)(2,1)S(1)}, bf16[96,576]{1,0:T(8,128)(2,1)S(1)}, bf16[96,576]{1,0:T(8,128)(2,1)S(1)}, bf16[96,576]{1,0:T(8,128)(2,1)S(1)}) custom-call(s32[2]{0:T(128)S(1)} %add_multiply_fusion.turn_ref, bf16[27,32,128]{2,1,0:T(8,128)(2,1)S(1)} %bitcast.5, bf16[4,7,32,128]{3,2,1,0:T(8,128)(2,1)S(1)} %all-to-all-done.got_ref), custom_call_target="tpu_custom_call" | custom-call | tf_op jit(solution)/shard_map/weights/pallas_call | solution.py:184
  62.6 0.6 copy-done.9
  63.4 1.0 %copy-done.8 = bf16[4,16,32,128]{3,2,1,0:T(8,128)(2,1)S(1)} copy-done((bf16[4,16,32,128]{3,2,1,0:T(8,128)(2,1)S(1)}, bf16[4,16,32,128]{3,2,1,0:T(8,128)(2,1)}, u32[]{:S(2)}) %copy-start.8) | copy-done | bytes 524312
  64.4 5.8 %shard_map.59 = (f32[16,4,32,128]{3,2,1,0:T(8,128)S(1)}, f32[16,4,32,128]{3,2,1,0:T(8,128)S(1)}) custom-call(s32[1]{0:T(128)} %bitcast.core_ref, bf16[4,16,32,128]{3,2,1,0:T(8,128)(2,1)S(1)} %copy-done.8, bf16[4,16,32,128]{3,2,1,0:T(8,128)(2,1)} %collective-permute-done.11.refs_1_, bf16[16,4,32,128]{3,2,1,0:T(8,128)(2,1)S(1)} %collective-permute-done.2.vn.refs_2_, ...), custom_call_target="tpu_custom_call" | custom-call | flops 1811939328 | bytes 6291456 | tf_op jit(solution)/shard_map/pallas_call | solution.py:276
  70.3 7.0 %shard_map.60 = (bf16[16,4,32,128]{3,2,1,0:T(8,128)(2,1)}, bf16[16,4,32,128]{3,2,1,0:T(8,128)(2,1)}) custom-call(s32[1]{0:T(128)} %bitcast.core_ref, bf16[4,16,32,128]{3,2,1,0:T(8,128)(2,1)} %collective-permute-done.6.refs_0_, bf16[4,16,32,128]{3,2,1,0:T(8,128)(2,1)} %collective-permute-done.7.refs_1_, ...), custom_call_target="tpu_custom_call" | custom-call | flops 1811939328 | bytes 6291456 | tf_op jit(solution)/shard_map/pallas_call | solution.py:276
  (31 shorter events, 0.4 us)
Async XLA Ops:
  0.6 15.2 %collective-permute-start.2 = (bf16[16,4,32,128]{3,2,1,0:T(8,128)(2,1)}, bf16[16,4,32,128]{3,2,1,0:T(8,128)(2,1)S(1)}, u32[]{:S(2)}, u32[]{:S(2)}) collective-permute-start(bf16[16,4,32,128]{3,2,1,0:T(8,128)(2,1)} %refs_3_.1), channel_id=1, source_target_pairs={{0,1},{1,2},{2,3},{3,0},{4,5},{5,6},{6,7},{7,4},{8,9},{9,10},{10,1... | collective-permute-start | bytes 1572872 | tf_op jit(solution)/shard_map/ppermute | solution.py:19
  2.2 13.6 %collective-permute-start.3 = (bf16[16,4,32,128]{3,2,1,0:T(8,128)(2,1)}, bf16[16,4,32,128]{3,2,1,0:T(8,128)(2,1)S(1)}, u32[]{:S(2)}, u32[]{:S(2)}) collective-permute-start(bf16[16,4,32,128]{3,2,1,0:T(8,128)(2,1)} %refs_4_.1), channel_id=1, source_target_pairs={{0,3},{1,0},{2,1},{3,2},{4,7},{5,4},{6,5},{7,6},{8,11},{9,8},{10,9... | collective-permute-start | bytes 1572872 | tf_op jit(solution)/shard_map/ppermute | solution.py:19
  15.8 1.0 %copy-start = (bf16[16,4,32,128]{3,2,1,0:T(8,128)(2,1)S(1)}, bf16[16,4,32,128]{3,2,1,0:T(8,128)(2,1)}, u32[]{:S(2)}) copy-start(bf16[16,4,32,128]{3,2,1,0:T(8,128)(2,1)} %refs_3_.1) | copy-start | bytes 1572868
  16.8 1.0 %copy-start.2 = (bf16[16,4,32,128]{3,2,1,0:T(8,128)(2,1)S(1)}, bf16[16,4,32,128]{3,2,1,0:T(8,128)(2,1)}, u32[]{:S(2)}) copy-start(bf16[16,4,32,128]{3,2,1,0:T(8,128)(2,1)} %refs_4_.1) | copy-start | bytes 1572868
  19.6 23.0 %collective-permute-start.10 = (bf16[4,16,32,128]{3,2,1,0:T(8,128)(2,1)S(1)}, bf16[4,16,32,128]{3,2,1,0:T(8,128)(2,1)S(1)}, u32[]{:S(2)}, u32[]{:S(2)}) collective-permute-start(bf16[4,16,32,128]{3,2,1,0:T(8,128)(2,1)S(1)} %get-tuple-element.28), channel_id=1, source_target_pairs={{0,4},{4,0},{8,12},{12,8},{16,20},{20,16},{24,28},{28,24},{32,36},... | collective-permute-start | bytes 1572872 | tf_op jit(solution)/shard_map/ppermute | solution.py:26
  19.9 9.7 %collective-permute-start = (bf16[2,16,32,128]{3,2,1,0:T(8,128)(2,1)S(1)}, bf16[2,16,32,128]{3,2,1,0:T(8,128)(2,1)S(1)}, u32[]{:S(2)}, u32[]{:S(2)}) collective-permute-start(bf16[2,16,32,128]{3,2,1,0:T(8,128)(2,1)S(1)} %get-tuple-element.18), channel_id=1, source_target_pairs={{0,3},{1,0},{2,1},{3,2},{4,7},{5,4},{6,5},{7,6},{8,11},{9,8},{10,9... | collective-permute-start | bytes 786440 | tf_op jit(solution)/shard_map/ppermute | solution.py:19
  22.9 13.4 %collective-permute-start.1 = (bf16[2,16,32,128]{3,2,1,0:T(8,128)(2,1)S(1)}, bf16[2,16,32,128]{3,2,1,0:T(8,128)(2,1)S(1)}, u32[]{:S(2)}, u32[]{:S(2)}) collective-permute-start(bf16[2,16,32,128]{3,2,1,0:T(8,128)(2,1)S(1)} %get-tuple-element.19), channel_id=1, source_target_pairs={{0,1},{1,2},{2,3},{3,0},{4,5},{5,6},{6,7},{7,4},{8,9},{9,10},{10,1... | collective-permute-start | bytes 786440 | tf_op jit(solution)/shard_map/ppermute | solution.py:19
  22.9 17.2 %collective-permute-start.4 = (bf16[2,16,32,128]{3,2,1,0:T(8,128)(2,1)S(1)}, bf16[2,16,32,128]{3,2,1,0:T(8,128)(2,1)S(1)}, u32[]{:S(2)}, u32[]{:S(2)}) collective-permute-start(bf16[2,16,32,128]{3,2,1,0:T(8,128)(2,1)S(1)} %get-tuple-element.20), channel_id=1, source_target_pairs={{0,1},{1,2},{2,3},{3,0},{4,5},{5,6},{6,7},{7,4},{8,9},{9,10},{10,1... | collective-permute-start | bytes 786440 | tf_op jit(solution)/shard_map/ppermute | solution.py:19
  23.5 16.6 %collective-permute-start.5 = (bf16[2,16,32,128]{3,2,1,0:T(8,128)(2,1)S(1)}, bf16[2,16,32,128]{3,2,1,0:T(8,128)(2,1)S(1)}, u32[]{:S(2)}, u32[]{:S(2)}) collective-permute-start(bf16[2,16,32,128]{3,2,1,0:T(8,128)(2,1)S(1)} %get-tuple-element.21), channel_id=1, source_target_pairs={{0,3},{1,0},{2,1},{3,2},{4,7},{5,4},{6,5},{7,6},{8,11},{9,8},{10,9... | collective-permute-start | bytes 786440 | tf_op jit(solution)/shard_map/ppermute | solution.py:19
  29.6 33.0 %collective-permute-start.11 = (bf16[4,16,32,128]{3,2,1,0:T(8,128)(2,1)}, bf16[4,16,32,128]{3,2,1,0:T(8,128)(2,1)}, u32[]{:S(2)}, u32[]{:S(2)}) collective-permute-start(bf16[4,16,32,128]{3,2,1,0:T(8,128)(2,1)} %get-tuple-element.29), channel_id=1, source_target_pairs={{4,8},{8,4},{12,16},{16,12},{20,24},{24,20},{28,32},{32,28},{36,40... | collective-permute-start | bytes 1572872 | tf_op jit(solution)/shard_map/ppermute | solution.py:26
  36.3 34.0 %collective-permute-start.8 = (bf16[4,16,32,128]{3,2,1,0:T(8,128)(2,1)}, bf16[4,16,32,128]{3,2,1,0:T(8,128)(2,1)}, u32[]{:S(2)}, u32[]{:S(2)}) collective-permute-start(bf16[4,16,32,128]{3,2,1,0:T(8,128)(2,1)} %get-tuple-element.24), channel_id=1, source_target_pairs={{0,3},{1,0},{2,1},{3,2},{4,7},{5,4},{6,5},{7,6},{8,11},{9,8},{10,9... | collective-permute-start | bytes 1572872 | tf_op jit(solution)/shard_map/ppermute | solution.py:19
  40.1 9.5 %copy-start.4 = (bf16[27,128,32]{1,2,0:T(8,128)(2,1)S(1)}, bf16[27,128,32]{1,2,0:T(8,128)(2,1)}, u32[]{:S(2)}) copy-start(bf16[27,128,32]{1,2,0:T(8,128)(2,1)} %param.5) | copy-start | bytes 663556
  40.1 30.2 %collective-permute-start.9 = (bf16[4,16,32,128]{3,2,1,0:T(8,128)(2,1)}, bf16[4,16,32,128]{3,2,1,0:T(8,128)(2,1)}, u32[]{:S(2)}, u32[]{:S(2)}) collective-permute-start(bf16[4,16,32,128]{3,2,1,0:T(8,128)(2,1)} %get-tuple-element.25), channel_id=1, source_target_pairs={{0,1},{1,2},{2,3},{3,0},{4,5},{5,6},{6,7},{7,4},{8,9},{9,10},{10,1... | collective-permute-start | bytes 1572872 | tf_op jit(solution)/shard_map/ppermute | solution.py:19
  40.1 2.4 %copy-start.5 = (bf16[2,16,32,128]{3,2,1,0:T(8,128)(2,1)}, bf16[2,16,32,128]{3,2,1,0:T(8,128)(2,1)S(1)}, u32[]{:S(2)}) copy-start(bf16[2,16,32,128]{3,2,1,0:T(8,128)(2,1)S(1)} %collective-permute-done.5.refs_3_.refs_6_) | copy-start | bytes 786436
  42.5 27.8 %collective-permute-start.6 = (bf16[4,16,32,128]{3,2,1,0:T(8,128)(2,1)}, bf16[4,16,32,128]{3,2,1,0:T(8,128)(2,1)}, u32[]{:S(2)}, u32[]{:S(2)}) collective-permute-start(bf16[4,16,32,128]{3,2,1,0:T(8,128)(2,1)} %get-tuple-element.22), channel_id=1, source_target_pairs={{0,4},{4,0},{8,12},{12,8},{16,20},{20,16},{24,28},{28,24},{32,36},... | collective-permute-start | bytes 1572872 | tf_op jit(solution)/shard_map/ppermute | solution.py:26
  42.6 0.8 %copy-start.7 = (bf16[4,16,32,128]{3,2,1,0:T(8,128)(2,1)}, bf16[4,16,32,128]{3,2,1,0:T(8,128)(2,1)S(1)}, u32[]{:S(2)}) copy-start(bf16[4,16,32,128]{3,2,1,0:T(8,128)(2,1)S(1)} %collective-permute-done.10.refs_0_) | copy-start | bytes 1572868
  43.4 26.8 %collective-permute-start.7 = (bf16[4,16,32,128]{3,2,1,0:T(8,128)(2,1)}, bf16[4,16,32,128]{3,2,1,0:T(8,128)(2,1)}, u32[]{:S(2)}, u32[]{:S(2)}) collective-permute-start(bf16[4,16,32,128]{3,2,1,0:T(8,128)(2,1)} %get-tuple-element.23), channel_id=1, source_target_pairs={{4,8},{8,4},{12,16},{16,12},{20,24},{24,20},{28,32},{32,28},{36,40... | collective-permute-start | bytes 1572872 | tf_op jit(solution)/shard_map/ppermute | solution.py:26
  49.6 13.8 %copy-start.3 = (bf16[16,4,32,128]{3,2,1,0:T(8,128)(2,1)S(1)}, bf16[16,4,32,128]{3,2,1,0:T(8,128)(2,1)}, u32[]{:S(2)}) copy-start(bf16[16,4,32,128]{3,2,1,0:T(8,128)(2,1)} %refs_4_.1) | copy-start | bytes 1572868
  50.5 12.9 %copy-start.1 = (bf16[16,4,32,128]{3,2,1,0:T(8,128)(2,1)S(1)}, bf16[16,4,32,128]{3,2,1,0:T(8,128)(2,1)}, u32[]{:S(2)}) copy-start(bf16[16,4,32,128]{3,2,1,0:T(8,128)(2,1)} %refs_3_.1) | copy-start | bytes 1572868
  50.5 11.1 %all-to-all-start = ((bf16[4,7,32,128]{3,2,1,0:T(8,128)(2,1)}), bf16[4,7,32,128]{3,2,1,0:T(8,128)(2,1)S(1)}, u32[]{:S(2)}, u32[]{:S(2)}) async-start(bf16[4,7,32,128]{3,2,1,0:T(8,128)(2,1)} %pack_taps.1), calls=%async_computation | async-start | bytes 458752 | tf_op jit(solution)/shard_map/all_to_all | solution.py:304
  62.6 0.7 copy-start.9
  63.4 1.0 %copy-start.8 = (bf16[4,16,32,128]{3,2,1,0:T(8,128)(2,1)S(1)}, bf16[4,16,32,128]{3,2,1,0:T(8,128)(2,1)}, u32[]{:S(2)}) copy-start(bf16[4,16,32,128]{3,2,1,0:T(8,128)(2,1)} %copy-done.7) | copy-start | bytes 1572868
  64.4 5.9 %copy-start.6 = (bf16[2,16,32,128]{3,2,1,0:T(8,128)(2,1)S(1)}, bf16[2,16,32,128]{3,2,1,0:T(8,128)(2,1)}, u32[]{:S(2)}) copy-start(bf16[2,16,32,128]{3,2,1,0:T(8,128)(2,1)} %copy-done.5) | copy-start | bytes 786436

commit v2 on v1

v2 whole, which is shorter than its diff:
```python
import jax
import jax.numpy as jnp
from jax import lax
from jax.experimental import pallas as pl
from jax.experimental.pallas import tpu as pltpu
from jax.sharding import PartitionSpec as P


MIB = 1024 * 1024
BF16 = jnp.bfloat16
VMEM = pl.BlockSpec(memory_space=pltpu.VMEM)
SMEM = pl.BlockSpec(memory_space=pltpu.SMEM)


def shifted(x, steps):
    count = lax.axis_size("chan")
    return lax.ppermute(x, "chan", [(i, (i + steps) % count) for i in range(count)])


def swapped_rows(on_chip, off_chip):
    count = lax.axis_size("space")
    near = [(i, i ^ 1) for i in range(count)]
    far = [(i, i - 1 if i % 2 == 0 else i + 1) for i in range(1, count - 1)]
    return lax.ppermute(on_chip, "space", near), lax.ppermute(off_chip, "space", far)


def pack_own(core, me, volume, cotangent):
    planes, rows, part, cells = volume.shape

    def body(core_ref, me_ref, v, c, ev, ec):
        for x, edge in ((v, ev), (c, ec)):
            edge[0] = x[:, 0]
            edge[1] = x[:, rows - 1]

    out = jax.ShapeDtypeStruct((2, planes, part, cells), BF16)
    return pl.pallas_call(
        body,
        out_shape=(out, out),
        in_specs=[SMEM, SMEM, VMEM, VMEM],
        out_specs=[VMEM] * 2,
        compiler_params=pltpu.CompilerParams(vmem_limit_bytes=4 * MIB),
        name="pack_own",
    )(core, me, volume, cotangent)


def pack_near(core, volume, cotangent, vol_near, cot_near):
    planes, rows, part, cells = volume.shape
    inside = rows - 2

    def body(core_ref, v, c, vn, cn, ev, ec, m_up, m_down, on_chip, off_chip):
        inner = jnp.where(core_ref[0] == 0, rows - 1, 0)
        outer = rows - 1 - inner
        for x, edge in ((vn, ev), (cn, ec)):
            edge[0] = x[:, 0]
            edge[1] = x[:, rows - 1]
        for r in range(inside):
            for n, x in enumerate((c, vn)):
                m_up[n * inside + r] = x[:, 1 + r]
            for n, x in enumerate((v, cn)):
                m_down[n * inside + r] = x[:, 1 + r]
        for n, x in enumerate((v, c, vn, cn)):
            on_chip[n] = x[:, inner]
            off_chip[n] = x[:, outer]

    def out(n):
        return jax.ShapeDtypeStruct((n, planes, part, cells), BF16)

    return pl.pallas_call(
        body,
        out_shape=(out(2), out(2), out(2 * inside), out(2 * inside), out(4), out(4)),
        in_specs=[SMEM, *[VMEM] * 4],
        out_specs=[VMEM] * 6,
        compiler_params=pltpu.CompilerParams(vmem_limit_bytes=8 * MIB),
        name="pack_near",
    )(core, volume, cotangent, vol_near, cot_near)


def pack_far(core, blocks):
    _, planes, part, cells = blocks[0].shape
    count = len(blocks)

    def body(core_ref, *refs):
        *held, on_chip, off_chip = refs
        side = jnp.where(core_ref[0] == 0, 1, 0)
        for n, x in enumerate(held):
            on_chip[n] = x[side]
            off_chip[n] = x[1 - side]

    out = jax.ShapeDtypeStruct((count, planes, part, cells), BF16)
    return pl.pallas_call(
        body,
        out_shape=(out, out),
        in_specs=[SMEM, *[VMEM] * count],
        out_specs=[VMEM] * 2,
        compiler_params=pltpu.CompilerParams(vmem_limit_bytes=6 * MIB),
        name="pack_far",
    )(core, *blocks)


def pack_taps(place, own, size):
    taps, outs, chans = own.shape
    part = chans // size
    groups = -(-taps // size)

    def body(place_ref, own_ref, *send_refs):
        turn = lax.rem(size - place_ref[0], size) * part
        empty = jnp.zeros((outs, chans), jnp.float32)
        for g in range(groups):
            quad = [
                pltpu.roll(own_ref[taps - 1 - t].astype(jnp.float32), turn, 1) if t < taps else empty
                for t in range(g * size, (g + 1) * size)
            ]
            for j in range(size):
                pieces = [q[:, j * part : (j + 1) * part] for q in quad]
                send_refs[j][g] = jnp.concatenate(pieces, axis=1).astype(BF16)

    return pl.pallas_call(
        body,
        out_shape=(jax.ShapeDtypeStruct((groups, outs, chans), BF16),) * size,
        in_specs=[SMEM, VMEM],
        out_specs=[VMEM] * size,
        compiler_params=pltpu.CompilerParams(vmem_limit_bytes=4 * MIB),
        name="pack_taps",
    )(place, own)


def weights(place, own, received, bias, cells):
    taps, outs, chans = own.shape
    size, groups = len(received), received[0].shape[0]
    part = chans // size
    half = chans // 2

    def body(place_ref, own_ref, *refs):
        got_refs = refs[:size]
        bias_ref, ahead_a, ahead_b, back_a, back_b, wide_ref = refs[size:]
        turn = lax.rem(size - place_ref[0] + 1, size) * part
        shape = (outs, outs)
        same = lax.broadcasted_iota(jnp.int32, shape, 0) == lax.broadcasted_iota(jnp.int32, shape, 1)
        column = jnp.sum(jnp.where(same, bias_ref[...], 0.0), axis=1, keepdims=True)
        wide_ref[...] = jnp.broadcast_to(column, wide_ref.shape)
        low = lax.broadcasted_iota(jnp.int32, (outs, chans), 1) < half

        def put(refs, tiles):
            for at in range(0, 9, 2):
                for c in range(3):
                    here = slice(c * outs, (c + 1) * outs)
                    even = tiles[3 * at + c]
                    if at == 8:
                        refs[0][here, at * half :] = even[:, :half].astype(BF16)
                        refs[1][here, at * half :] = even[:, half:].astype(BF16)
                        continue
                    odd = tiles[3 * at + 3 + c]
                    both = slice(at * half, (at + 2) * half)
                    first = jnp.where(low, even, pltpu.roll(odd, half, 1))
                    second = jnp.where(low, pltpu.roll(even, half, 1), odd)
                    refs[0][here, both] = first.astype(BF16)
                    refs[1][here, both] = second.astype(BF16)

        tiles = [pltpu.roll(own_ref[t].astype(jnp.float32), turn, 1) for t in range(taps)]
        put((ahead_a, ahead_b), tiles)
        tiles = []
        for g in range(groups):
            tile = jnp.concatenate([got[g] for got in got_refs], axis=0)
            tile = tile.astype(jnp.float32).T
            tiles += [tile[t * part : (t + 1) * part] for t in range(size)]
        put((back_a, back_b), tiles)

    out = jax.ShapeDtypeStruct((3 * outs, 9 * half), BF16)
    return pl.pallas_call(
        body,
        out_shape=(*[out] * 4, jax.ShapeDtypeStruct((outs, cells), jnp.float32)),
        in_specs=[SMEM, *[VMEM] * (size + 2)],
        out_specs=[VMEM] * 5,
        compiler_params=pltpu.CompilerParams(vmem_limit_bytes=6 * MIB),
        name="weights",
    )(place, own, *received, bias.reshape(1, outs))


def convolve(source, w_ref, start, o_ref):
    planes, rows, outs, cells = o_ref.shape
    wide = 2 * cells
    lane = lax.broadcasted_iota(jnp.int32, (outs, wide), 1) % cells
    first = lane == 0
    last = lane == cells - 1
    step = w_ref.shape[1] // 3
    for p in range(planes):
        low, high = max(p - 1, 0), min(p + 1, planes - 1)
        table = w_ref[:, (low - p + 1) * step : (high - p + 2) * step]
        for r in range(0, rows, 2):
            halves = []
            for rr in (r, r + 1):
                stack = []
                for at in range(low, high + 1):
                    for b in range(3):
                        stack += source(at, rr + b)
                halves.append(jnp.concatenate(stack, axis=0))
            data = jnp.concatenate(halves, axis=1)
            sums = jnp.dot(table, data, preferred_element_type=jnp.float32)
            total = sums[outs : 2 * outs]
            total = total + jnp.where(first, 0.0, pltpu.roll(sums[:outs], 1, 1))
            total = total + jnp.where(last, 0.0, pltpu.roll(sums[2 * outs :], wide - 1, 1))
            for n in range(2):
                piece = total[:, n * cells : (n + 1) * cells]
                if start is not None:
                    piece = piece + start(p, r + n)
                o_ref[p, r + n] = piece.astype(o_ref.dtype)


def stage(core, parts, tables, starts, dtype, shape):
    planes, rows, part, cells = shape
    operands = []
    for plan in parts:
        for on_chip, off_chip, _, inner in plan:
            for x in (on_chip, off_chip, *[x for x, _, _ in inner]):
                if not any(x is y for y in operands):
                    operands.append(x)
    count = len(parts[0])

    def place(x):
        return [i for i, y in enumerate(operands) if y is x][0]

    def body(core_ref, *refs):
        held = refs[: len(operands)]
        w_refs = refs[len(operands) : len(operands) + 2]
        s_refs = refs[len(operands) + 2 : len(operands) + 2 + len(starts)]
        o_refs = refs[len(operands) + 2 + len(starts) :][:2]
        low_ref, high_ref = refs[len(operands) + 4 + len(starts) :]
        places = [(block[0], block[1], block[2]) for plan in parts for block in plan]

        @pl.when(core_ref[0] == 0)
        def _():
            for i, (on_chip, off_chip, n) in enumerate(places):
                high_ref[i] = held[place(on_chip)][n]
                low_ref[i] = held[place(off_chip)][n]

        @pl.when(core_ref[0] != 0)
        def _():
            for i, (on_chip, off_chip, n) in enumerate(places):
                low_ref[i] = held[place(on_chip)][n]
                high_ref[i] = held[place(off_chip)][n]

        for n in range(2):

            def source(p, r, n=n):
                if r == 0:
                    return [low_ref[n * count + s, p] for s in range(count)]
                if r == rows + 1:
                    return [high_ref[n * count + s, p] for s in range(count)]
                found = []
                for s in range(count):
                    x, before, at = parts[n][s][3][r - 1]
                    ref = held[place(x)]
                    found.append(ref[at, p] if before else ref[p, at])
                return found

            begin = None
            if n < len(starts):
                if len(starts) == 1:
                    begin = lambda p, r: s_refs[0][...]
                else:
                    begin = lambda p, r, n=n: s_refs[n][p, r]
            convolve(source, w_refs[n], begin, o_refs[n])

    out = jax.ShapeDtypeStruct(shape, dtype)
    edge = pltpu.VMEM((2 * count, planes, part, cells), BF16)
    return pl.pallas_call(
        body,
        out_shape=(out, out),
        in_specs=[SMEM, *[VMEM] * (len(operands) + 2 + len(starts))],
        out_specs=[VMEM, VMEM],
        scratch_shapes=[edge, edge],
        compiler_params=pltpu.CompilerParams(vmem_limit_bytes=14 * MIB),
        cost_estimate=pl.CostEstimate(
            flops=4 * 27 * count * part * part * planes * rows * cells,
            bytes_accessed=6 * MIB,
            transcendentals=0,
        ),
    )(core, *operands, *tables, *starts)


def per_device(volume, kernel, bias, cotangent):
    size = lax.axis_size("chan")
    me = lax.axis_index("chan").astype(jnp.int32).reshape(1)
    core = (lax.axis_index("space") % 2).astype(jnp.int32).reshape(1)
    _, rows, _, cells = volume.shape

    vol_left = shifted(volume, 1)
    cot_right = shifted(cotangent, -1)
    vol_edge, cot_edge = pack_own(core, me, volume, cotangent)
    cot_left_edge = shifted(cot_edge, 1)
    vol_right_edge = shifted(vol_edge, -1)
    own = jnp.swapaxes(kernel, 1, 2)
    sent = pack_taps(me, own, size)
    received = [sent[0], *[shifted(sent[size - d], -d) for d in range(1, size)]]

    vol_edge, cot_edge, mid_up, mid_down, on_chip, off_chip = pack_near(core, volume, cotangent, vol_left, cot_right)
    vol_edge, cot_edge = shifted(vol_edge, 1), shifted(cot_edge, -1)
    mid_up, mid_down = shifted(mid_up, 1), shifted(mid_down, -1)
    near = swapped_rows(on_chip, off_chip)

    ahead_a, ahead_b, back_a, back_b, wide = weights(me, own, received, bias, cells)

    on_chip, off_chip = pack_far(core, (vol_right_edge, cot_left_edge, vol_edge, cot_edge))
    far = swapped_rows(on_chip, off_chip)

    def whole(x, pair, n):
        return (*pair, n, [(x, False, r) for r in range(rows)])

    def split(edge, middle, half, pair, n):
        inner = [(middle, True, half * (rows - 2) + r) for r in range(rows - 2)]
        return (*pair, n, [(edge, True, 0), *inner, (edge, True, 1)])

    sums = stage(
        core,
        [[whole(vol_left, near, 2), whole(volume, near, 0)], [whole(cotangent, near, 1), whole(cot_right, near, 3)]],
        (ahead_a, back_a),
        (wide,),
        jnp.float32,
        volume.shape,
    )
    return stage(
        core,
        [
            [split(vol_right_edge, mid_down, 0, far, 0), split(vol_edge, mid_up, 1, far, 2)],
            [split(cot_edge, mid_down, 1, far, 3), split(cot_left_edge, mid_up, 0, far, 1)],
        ],
        (ahead_b, back_b),
        sums,
        BF16,
        volume.shape,
    )


def solution(mesh):
    spec = P(None, "space", "chan", None)

    return jax.shard_map(
        per_device,
        mesh=mesh,
        in_specs=(spec, P(None, None, "chan"), P("chan"), spec),
        out_specs=(spec, spec),
        check_vma=False,
    )
```

time: 77.9 us -> 65.6 us (0.84)
  the two profiles are of different devices: /device:TPU:24 before, /device:TPU:30 now
where the time goes in v2:
time: 65.6 us; the launch traced here: 65.4 us
  starting transfers between devices  25.6 us (39%)
  waiting for transfers between devices  23 us (35%)
  Pallas kernels  11.7 us (18%)
  local copies, waits for them, and re-layouts  4.27 us (7%)
  between operations  0.8 us (1%)
    ppermute x11, waiting for transfers between devices, shifted(): lax.ppermute(x, 'chan', [(i, (i + steps) % count) for i in range(count)])  21.4 us
    ppermute x11, starting transfers between devices, shifted(): lax.ppermute(x, 'chan', [(i, (i + steps) % count) for i in range(count)])  14 us
    ppermute x2, starting transfers between devices, swapped_rows(): lax.ppermute(off_chip, 'space', far)  11.6 us
    pallas_call x2, Pallas kernels, stage(): pl.pallas_call(body, out_shape=(out, out), in_specs=[SMEM, *[VMEM] * (len...  9.62 us
    unnamed x20, local copies, waits for them, and re-layouts  4.27 us
    ppermute x2, waiting for transfers between devices, swapped_rows(): lax.ppermute(off_chip, 'space', far)  1.54 us
  transfers between devices with their start and end apart: 15, of which 6 were waited for; matrix products, arithmetic and copies ran while one was open for 0% of the time, Pallas kernels for 9%

profile of v2, /device:TPU:30, one launch (start us, length us, event | category | flops | bytes accessed | tf_op | source)
XLA Modules:
  0.0 65.4 jit_solution(11879169035276129182)
XLA Ops:
  0.6 0.6 collective-permute-start.2
  1.2 1.5 %collective-permute-start.3 = (bf16[16,4,32,128]{3,2,1,0:T(8,128)(2,1)}, bf16[16,4,32,128]{3,2,1,0:T(8,128)(2,1)S(1)}, u32[]{:S(2)}, u32[]{:S(2)}) collective-permute-start(bf16[16,4,32,128]{3,2,1,0:T(8,128)(2,1)} %refs_4_.1), channel_id=1, source_target_pairs={{0,3},{1,0},{2,1},{3,2},{4,7},{5,4},{6,5},{7,6},{8,11},{9,8},{10,9... | collective-permute-start | bytes 1572872 | tf_op jit(solution)/shard_map/ppermute | solution.py:17
  2.7 11.8 %collective-permute-done.2.vn.refs_2_ = bf16[16,4,32,128]{3,2,1,0:T(8,128)(2,1)S(1)} collective-permute-done((bf16[16,4,32,128]{3,2,1,0:T(8,128)(2,1)}, bf16[16,4,32,128]{3,2,1,0:T(8,128)(2,1)S(1)}, u32[]{:S(2)}, u32[]{:S(2)}) %collective-permute-start.2) | collective-permute-done | bytes 524320 | tf_op jit(solution)/shard_map/ppermute | solution.py:17
  14.6 1.4 %collective-permute-done.3.cn.refs_5_ = bf16[16,4,32,128]{3,2,1,0:T(8,128)(2,1)S(1)} collective-permute-done((bf16[16,4,32,128]{3,2,1,0:T(8,128)(2,1)}, bf16[16,4,32,128]{3,2,1,0:T(8,128)(2,1)S(1)}, u32[]{:S(2)}, u32[]{:S(2)}) %collective-permute-start.3) | collective-permute-done | bytes 524320 | tf_op jit(solution)/shard_map/ppermute | solution.py:17
  16.0 1.0 %copy-done = bf16[16,4,32,128]{3,2,1,0:T(8,128)(2,1)S(1)} copy-done((bf16[16,4,32,128]{3,2,1,0:T(8,128)(2,1)S(1)}, bf16[16,4,32,128]{3,2,1,0:T(8,128)(2,1)}, u32[]{:S(2)}) %copy-start) | copy-done | bytes 524312
  17.0 1.0 %copy-done.2 = bf16[16,4,32,128]{3,2,1,0:T(8,128)(2,1)S(1)} copy-done((bf16[16,4,32,128]{3,2,1,0:T(8,128)(2,1)S(1)}, bf16[16,4,32,128]{3,2,1,0:T(8,128)(2,1)}, u32[]{:S(2)}) %copy-start.2) | copy-done | bytes 524312
  18.1 1.0 %pack_near.1 = (bf16[2,16,32,128]{3,2,1,0:T(8,128)(2,1)S(1)}, bf16[2,16,32,128]{3,2,1,0:T(8,128)(2,1)S(1)}, bf16[4,16,32,128]{3,2,1,0:T(8,128)(2,1)S(1)}, bf16[4...) custom-call(s32[1]{0:T(128)} %bitcast.core_ref, ...), custom_call_target="tpu_custom_call" | custom-call | tf_op jit(solution)/shard_map/pack_near/pallas_call | solution.py:68
  19.1 0.8 %copy-done.6 = bf16[4,16,32,128]{3,2,1,0:T(8,128)(2,1)} copy-done((bf16[4,16,32,128]{3,2,1,0:T(8,128)(2,1)}, bf16[4,16,32,128]{3,2,1,0:T(8,128)(2,1)S(1)}, u32[]{:S(2)}) %copy-start.6) | copy-done | bytes 524312
  19.9 0.7 %copy-done.8 = bf16[2,16,32,128]{3,2,1,0:T(8,128)(2,1)} copy-done((bf16[2,16,32,128]{3,2,1,0:T(8,128)(2,1)}, bf16[2,16,32,128]{3,2,1,0:T(8,128)(2,1)S(1)}, u32[]{:S(2)}) %copy-start.8) | copy-done | bytes 262168
  21.1 2.9 %collective-permute-start.1 = (bf16[2,16,32,128]{3,2,1,0:T(8,128)(2,1)S(1)}, bf16[2,16,32,128]{3,2,1,0:T(8,128)(2,1)S(1)}, u32[]{:S(2)}, u32[]{:S(2)}) collective-permute-start(bf16[2,16,32,128]{3,2,1,0:T(8,128)(2,1)S(1)} %get-tuple-element.24), channel_id=1, source_target_pairs={{0,1},{1,2},{2,3},{3,0},{4,5},{5,6},{6,7},{7,4},{8,9},{9,10},{10,1... | collective-permute-start | bytes 786440 | tf_op jit(solution)/shard_map/ppermute | solution.py:17
  24.0 2.0 %collective-permute-start.5 = (bf16[2,16,32,128]{3,2,1,0:T(8,128)(2,1)S(1)}, bf16[2,16,32,128]{3,2,1,0:T(8,128)(2,1)S(1)}, u32[]{:S(2)}, u32[]{:S(2)}) collective-permute-start(bf16[2,16,32,128]{3,2,1,0:T(8,128)(2,1)S(1)} %get-tuple-element.26), channel_id=1, source_target_pairs={{0,3},{1,0},{2,1},{3,2},{4,7},{5,4},{6,5},{7,6},{8,11},{9,8},{10,9... | collective-permute-start | bytes 786440 | tf_op jit(solution)/shard_map/ppermute | solution.py:17
  26.0 5.1 %collective-permute-done.refs_0_.refs_2_ = bf16[2,16,32,128]{3,2,1,0:T(8,128)(2,1)S(1)} collective-permute-done((bf16[2,16,32,128]{3,2,1,0:T(8,128)(2,1)S(1)}, bf16[2,16,32,128]{3,2,1,0:T(8,128)(2,1)S(1)}, u32[]{:S(2)}, u32[]{:S(2)}) %collective-permute-start) | collective-permute-done | bytes 262176 | tf_op jit(solution)/shard_map/ppermute | solution.py:17
  31.1 6.7 %collective-permute-start.14 = (bf16[4,16,32,128]{3,2,1,0:T(8,128)(2,1)S(1)}, bf16[4,16,32,128]{3,2,1,0:T(8,128)(2,1)S(1)}, u32[]{:S(2)}, u32[]{:S(2)}) collective-permute-start(bf16[4,16,32,128]{3,2,1,0:T(8,128)(2,1)S(1)} %copy-done.7), channel_id=1, source_target_pairs={{4,8},{8,4},{12,16},{16,12},{20,24},{24,20},{28,32},{32,28},{36,40... | collective-permute-start | bytes 1572872 | tf_op jit(solution)/shard_map/ppermute | solution.py:24
  37.9 0.6 pack_taps.1
  38.6 1.0 %collective-permute-start.11 = (bf16[7,32,128]{2,1,0:T(8,128)(2,1)S(1)}, bf16[7,32,128]{2,1,0:T(8,128)(2,1)S(1)}, u32[]{:S(2)}, u32[]{:S(2)}) collective-permute-start(bf16[7,32,128]{2,1,0:T(8,128)(2,1)S(1)} %get-tuple-element.33), channel_id=1, source_target_pairs={{0,2},{1,3},{2,0},{3,1},{4,6},{5,7},{6,4},{7,5},{8,10},{9,11},{10,... | collective-permute-start | bytes 172040 | tf_op jit(solution)/shard_map/ppermute | solution.py:17
  39.6 2.3 %collective-permute-start.12 = (bf16[7,32,128]{2,1,0:T(8,128)(2,1)S(1)}, bf16[7,32,128]{2,1,0:T(8,128)(2,1)S(1)}, u32[]{:S(2)}, u32[]{:S(2)}) collective-permute-start(bf16[7,32,128]{2,1,0:T(8,128)(2,1)S(1)} %get-tuple-element.34), channel_id=1, source_target_pairs={{0,1},{1,2},{2,3},{3,0},{4,5},{5,6},{6,7},{7,4},{8,9},{9,10},{10,1... | collective-permute-start | bytes 172040 | tf_op jit(solution)/shard_map/ppermute | solution.py:17
  42.0 2.2 %collective-permute-done.10.refs_1_ = bf16[7,32,128]{2,1,0:T(8,128)(2,1)S(1)} collective-permute-done((bf16[7,32,128]{2,1,0:T(8,128)(2,1)S(1)}, bf16[7,32,128]{2,1,0:T(8,128)(2,1)S(1)}, u32[]{:S(2)}, u32[]{:S(2)}) %collective-permute-start.10) | collective-permute-done | bytes 57376 | tf_op jit(solution)/shard_map/ppermute | solution.py:17
  44.2 0.8 %collective-permute-done.11.refs_2_ = bf16[7,32,128]{2,1,0:T(8,128)(2,1)S(1)} collective-permute-done((bf16[7,32,128]{2,1,0:T(8,128)(2,1)S(1)}, bf16[7,32,128]{2,1,0:T(8,128)(2,1)S(1)}, u32[]{:S(2)}, u32[]{:S(2)}) %collective-permute-start.11) | collective-permute-done | bytes 57376 | tf_op jit(solution)/shard_map/ppermute | solution.py:17
  45.0 3.1 %collective-permute-start.9 = (bf16[4,16,32,128]{3,2,1,0:T(8,128)(2,1)S(1)}, bf16[4,16,32,128]{3,2,1,0:T(8,128)(2,1)S(1)}, u32[]{:S(2)}, u32[]{:S(2)}) collective-permute-start(bf16[4,16,32,128]{3,2,1,0:T(8,128)(2,1)S(1)} %get-tuple-element.30), channel_id=1, source_target_pairs={{0,1},{1,2},{2,3},{3,0},{4,5},{5,6},{6,7},{7,4},{8,9},{9,10},{10,1... | collective-permute-start | bytes 1572872 | tf_op jit(solution)/shard_map/ppermute | solution.py:17
  48.1 5.0 %collective-permute-start.7 = (bf16[4,16,32,128]{3,2,1,0:T(8,128)(2,1)S(1)}, bf16[4,16,32,128]{3,2,1,0:T(8,128)(2,1)S(1)}, u32[]{:S(2)}, u32[]{:S(2)}) collective-permute-start(bf16[4,16,32,128]{3,2,1,0:T(8,128)(2,1)S(1)} %get-tuple-element.28), channel_id=1, source_target_pairs={{4,8},{8,4},{12,16},{16,12},{20,24},{24,20},{28,32},{32,28},{36,40... | collective-permute-start | bytes 1572872 | tf_op jit(solution)/shard_map/ppermute | solution.py:24
  53.1 0.6 copy-done.5
  54.2 5.0 %shard_map.59 = (f32[16,4,32,128]{3,2,1,0:T(8,128)S(1)}, f32[16,4,32,128]{3,2,1,0:T(8,128)S(1)}) custom-call(s32[1]{0:T(128)} %bitcast.core_ref, bf16[4,16,32,128]{3,2,1,0:T(8,128)(2,1)} %collective-permute-done.13.refs_0_, bf16[4,16,32,128]{3,2,1,0:T(8,128)(2,1)S(1)} %collective-permute-done.14.refs_1_, ...), custom_call_target="tpu_custom_call" | custom-call | flops 1811939328 | bytes 6291456 | tf_op jit(solution)/shard_map/pallas_call | solution.py:266
  59.2 1.5 %collective-permute-done.7.refs_1_ = bf16[4,16,32,128]{3,2,1,0:T(8,128)(2,1)S(1)} collective-permute-done((bf16[4,16,32,128]{3,2,1,0:T(8,128)(2,1)S(1)}, bf16[4,16,32,128]{3,2,1,0:T(8,128)(2,1)S(1)}, u32[]{:S(2)}, u32[]{:S(2)}) %collective-permute-start.7) | collective-permute-done | bytes 524320 | tf_op jit(solution)/shard_map/ppermute | solution.py:24
  60.8 4.6 %shard_map.60 = (bf16[16,4,32,128]{3,2,1,0:T(8,128)(2,1)}, bf16[16,4,32,128]{3,2,1,0:T(8,128)(2,1)}) custom-call(s32[1]{0:T(128)} %bitcast.core_ref, bf16[4,16,32,128]{3,2,1,0:T(8,128)(2,1)S(1)} %collective-permute-done.6.refs_0_, bf16[4,16,32,128]{3,2,1,0:T(8,128)(2,1)S(1)} %collective-permute-done.7.refs_1_, ...), custom_call_target="tpu_custom_call" | custom-call | flops 1811939328 | bytes 6291456 | tf_op jit(solution)/shard_map/pallas_call | solution.py:266
  (33 shorter events, 1.1 us)
Async XLA Ops:
  0.6 14.0 %collective-permute-start.2 = (bf16[16,4,32,128]{3,2,1,0:T(8,128)(2,1)}, bf16[16,4,32,128]{3,2,1,0:T(8,128)(2,1)S(1)}, u32[]{:S(2)}, u32[]{:S(2)}) collective-permute-start(bf16[16,4,32,128]{3,2,1,0:T(8,128)(2,1)} %refs_3_.1), channel_id=1, source_target_pairs={{0,1},{1,2},{2,3},{3,0},{4,5},{5,6},{6,7},{7,4},{8,9},{9,10},{10,1... | collective-permute-start | bytes 1572872 | tf_op jit(solution)/shard_map/ppermute | solution.py:17
  1.2 14.8 %collective-permute-start.3 = (bf16[16,4,32,128]{3,2,1,0:T(8,128)(2,1)}, bf16[16,4,32,128]{3,2,1,0:T(8,128)(2,1)S(1)}, u32[]{:S(2)}, u32[]{:S(2)}) collective-permute-start(bf16[16,4,32,128]{3,2,1,0:T(8,128)(2,1)} %refs_4_.1), channel_id=1, source_target_pairs={{0,3},{1,0},{2,1},{3,2},{4,7},{5,4},{6,5},{7,6},{8,11},{9,8},{10,9... | collective-permute-start | bytes 1572872 | tf_op jit(solution)/shard_map/ppermute | solution.py:17
  16.0 1.0 %copy-start = (bf16[16,4,32,128]{3,2,1,0:T(8,128)(2,1)S(1)}, bf16[16,4,32,128]{3,2,1,0:T(8,128)(2,1)}, u32[]{:S(2)}) copy-start(bf16[16,4,32,128]{3,2,1,0:T(8,128)(2,1)} %refs_3_.1) | copy-start | bytes 1572868
  17.0 1.0 %copy-start.2 = (bf16[16,4,32,128]{3,2,1,0:T(8,128)(2,1)S(1)}, bf16[16,4,32,128]{3,2,1,0:T(8,128)(2,1)}, u32[]{:S(2)}) copy-start(bf16[16,4,32,128]{3,2,1,0:T(8,128)(2,1)} %refs_4_.1) | copy-start | bytes 1572868
  18.1 2.5 %copy-start.1 = (bf16[16,4,32,128]{3,2,1,0:T(8,128)(2,1)S(1)}, bf16[16,4,32,128]{3,2,1,0:T(8,128)(2,1)}, u32[]{:S(2)}) copy-start(bf16[16,4,32,128]{3,2,1,0:T(8,128)(2,1)} %refs_3_.1) | copy-start | bytes 1572868
  18.1 2.5 %copy-start.3 = (bf16[16,4,32,128]{3,2,1,0:T(8,128)(2,1)S(1)}, bf16[16,4,32,128]{3,2,1,0:T(8,128)(2,1)}, u32[]{:S(2)}) copy-start(bf16[16,4,32,128]{3,2,1,0:T(8,128)(2,1)} %refs_4_.1) | copy-start | bytes 1572868
  19.1 0.8 %copy-start.6 = (bf16[4,16,32,128]{3,2,1,0:T(8,128)(2,1)}, bf16[4,16,32,128]{3,2,1,0:T(8,128)(2,1)S(1)}, u32[]{:S(2)}) copy-start(bf16[4,16,32,128]{3,2,1,0:T(8,128)(2,1)S(1)} %get-tuple-element.38) | copy-start | bytes 1572868
  19.9 0.7 %copy-start.8 = (bf16[2,16,32,128]{3,2,1,0:T(8,128)(2,1)}, bf16[2,16,32,128]{3,2,1,0:T(8,128)(2,1)S(1)}, u32[]{:S(2)}) copy-start(bf16[2,16,32,128]{3,2,1,0:T(8,128)(2,1)S(1)} %get-tuple-element.25) | copy-start | bytes 786436
  20.6 27.6 %collective-permute-start.13 = (bf16[4,16,32,128]{3,2,1,0:T(8,128)(2,1)}, bf16[4,16,32,128]{3,2,1,0:T(8,128)(2,1)}, u32[]{:S(2)}, u32[]{:S(2)}) collective-permute-start(bf16[4,16,32,128]{3,2,1,0:T(8,128)(2,1)} %get-tuple-element.37), channel_id=1, source_target_pairs={{0,4},{4,0},{8,12},{12,8},{16,20},{20,16},{24,28},{28,24},{32,36},... | collective-permute-start | bytes 1572872 | tf_op jit(solution)/shard_map/ppermute | solution.py:24
  20.6 3.4 %copy-start.9 = (bf16[2,16,32,128]{3,2,1,0:T(8,128)(2,1)S(1)}, bf16[2,16,32,128]{3,2,1,0:T(8,128)(2,1)}, u32[]{:S(2)}) copy-start(bf16[2,16,32,128]{3,2,1,0:T(8,128)(2,1)} %copy-done.8) | copy-start | bytes 786436
  20.6 10.5 %copy-start.7 = (bf16[4,16,32,128]{3,2,1,0:T(8,128)(2,1)S(1)}, bf16[4,16,32,128]{3,2,1,0:T(8,128)(2,1)}, u32[]{:S(2)}) copy-start(bf16[4,16,32,128]{3,2,1,0:T(8,128)(2,1)} %copy-done.6) | copy-start | bytes 1572868
  20.6 17.2 %copy-start.4 = (bf16[27,128,32]{1,2,0:T(8,128)(2,1)S(1)}, bf16[27,128,32]{1,2,0:T(8,128)(2,1)}, u32[]{:S(2)}) copy-start(bf16[27,128,32]{1,2,0:T(8,128)(2,1)} %param.5) | copy-start | bytes 663556
  20.7 10.5 %collective-permute-start = (bf16[2,16,32,128]{3,2,1,0:T(8,128)(2,1)S(1)}, bf16[2,16,32,128]{3,2,1,0:T(8,128)(2,1)S(1)}, u32[]{:S(2)}, u32[]{:S(2)}) collective-permute-start(bf16[2,16,32,128]{3,2,1,0:T(8,128)(2,1)S(1)} %get-tuple-element.23), channel_id=1, source_target_pairs={{0,3},{1,0},{2,1},{3,2},{4,7},{5,4},{6,5},{7,6},{8,11},{9,8},{10,9... | collective-permute-start | bytes 786440 | tf_op jit(solution)/shard_map/ppermute | solution.py:17
  21.1 17.4 %collective-permute-start.1 = (bf16[2,16,32,128]{3,2,1,0:T(8,128)(2,1)S(1)}, bf16[2,16,32,128]{3,2,1,0:T(8,128)(2,1)S(1)}, u32[]{:S(2)}, u32[]{:S(2)}) collective-permute-start(bf16[2,16,32,128]{3,2,1,0:T(8,128)(2,1)S(1)} %get-tuple-element.24), channel_id=1, source_target_pairs={{0,1},{1,2},{2,3},{3,0},{4,5},{5,6},{6,7},{7,4},{8,9},{9,10},{10,1... | collective-permute-start | bytes 786440 | tf_op jit(solution)/shard_map/ppermute | solution.py:17
  24.0 14.6 %collective-permute-start.4 = (bf16[2,16,32,128]{3,2,1,0:T(8,128)(2,1)S(1)}, bf16[2,16,32,128]{3,2,1,0:T(8,128)(2,1)S(1)}, u32[]{:S(2)}, u32[]{:S(2)}) collective-permute-start(bf16[2,16,32,128]{3,2,1,0:T(8,128)(2,1)S(1)} %copy-done.9), channel_id=1, source_target_pairs={{0,1},{1,2},{2,3},{3,0},{4,5},{5,6},{6,7},{7,4},{8,9},{9,10},{10,1... | collective-permute-start | bytes 786440 | tf_op jit(solution)/shard_map/ppermute | solution.py:17
  24.0 15.6 %collective-permute-start.5 = (bf16[2,16,32,128]{3,2,1,0:T(8,128)(2,1)S(1)}, bf16[2,16,32,128]{3,2,1,0:T(8,128)(2,1)S(1)}, u32[]{:S(2)}, u32[]{:S(2)}) collective-permute-start(bf16[2,16,32,128]{3,2,1,0:T(8,128)(2,1)S(1)} %get-tuple-element.26), channel_id=1, source_target_pairs={{0,3},{1,0},{2,1},{3,2},{4,7},{5,4},{6,5},{7,6},{8,11},{9,8},{10,9... | collective-permute-start | bytes 786440 | tf_op jit(solution)/shard_map/ppermute | solution.py:17
  31.1 23.0 %collective-permute-start.14 = (bf16[4,16,32,128]{3,2,1,0:T(8,128)(2,1)S(1)}, bf16[4,16,32,128]{3,2,1,0:T(8,128)(2,1)S(1)}, u32[]{:S(2)}, u32[]{:S(2)}) collective-permute-start(bf16[4,16,32,128]{3,2,1,0:T(8,128)(2,1)S(1)} %copy-done.7), channel_id=1, source_target_pairs={{4,8},{8,4},{12,16},{16,12},{20,24},{24,20},{28,32},{32,28},{36,40... | collective-permute-start | bytes 1572872 | tf_op jit(solution)/shard_map/ppermute | solution.py:24
  38.5 5.7 %collective-permute-start.10 = (bf16[7,32,128]{2,1,0:T(8,128)(2,1)S(1)}, bf16[7,32,128]{2,1,0:T(8,128)(2,1)S(1)}, u32[]{:S(2)}, u32[]{:S(2)}) collective-permute-start(bf16[7,32,128]{2,1,0:T(8,128)(2,1)S(1)} %get-tuple-element.32), channel_id=1, source_target_pairs={{0,3},{1,0},{2,1},{3,2},{4,7},{5,4},{6,5},{7,6},{8,11},{9,8},{10,9... | collective-permute-start | bytes 172040 | tf_op jit(solution)/shard_map/ppermute | solution.py:17
  38.6 6.4 %collective-permute-start.11 = (bf16[7,32,128]{2,1,0:T(8,128)(2,1)S(1)}, bf16[7,32,128]{2,1,0:T(8,128)(2,1)S(1)}, u32[]{:S(2)}, u32[]{:S(2)}) collective-permute-start(bf16[7,32,128]{2,1,0:T(8,128)(2,1)S(1)} %get-tuple-element.33), channel_id=1, source_target_pairs={{0,2},{1,3},{2,0},{3,1},{4,6},{5,7},{6,4},{7,5},{8,10},{9,11},{10,... | collective-permute-start | bytes 172040 | tf_op jit(solution)/shard_map/ppermute | solution.py:17
  39.6 8.5 %collective-permute-start.12 = (bf16[7,32,128]{2,1,0:T(8,128)(2,1)S(1)}, bf16[7,32,128]{2,1,0:T(8,128)(2,1)S(1)}, u32[]{:S(2)}, u32[]{:S(2)}) collective-permute-start(bf16[7,32,128]{2,1,0:T(8,128)(2,1)S(1)} %get-tuple-element.34), channel_id=1, source_target_pairs={{0,1},{1,2},{2,3},{3,0},{4,5},{5,6},{6,7},{7,4},{8,9},{9,10},{10,1... | collective-permute-start | bytes 172040 | tf_op jit(solution)/shard_map/ppermute | solution.py:17
  44.2 15.0 %collective-permute-start.8 = (bf16[4,16,32,128]{3,2,1,0:T(8,128)(2,1)S(1)}, bf16[4,16,32,128]{3,2,1,0:T(8,128)(2,1)S(1)}, u32[]{:S(2)}, u32[]{:S(2)}) collective-permute-start(bf16[4,16,32,128]{3,2,1,0:T(8,128)(2,1)S(1)} %get-tuple-element.29), channel_id=1, source_target_pairs={{0,3},{1,0},{2,1},{3,2},{4,7},{5,4},{6,5},{7,6},{8,11},{9,8},{10,9... | collective-permute-start | bytes 1572872 | tf_op jit(solution)/shard_map/ppermute | solution.py:17
  45.0 14.2 %collective-permute-start.9 = (bf16[4,16,32,128]{3,2,1,0:T(8,128)(2,1)S(1)}, bf16[4,16,32,128]{3,2,1,0:T(8,128)(2,1)S(1)}, u32[]{:S(2)}, u32[]{:S(2)}) collective-permute-start(bf16[4,16,32,128]{3,2,1,0:T(8,128)(2,1)S(1)} %get-tuple-element.30), channel_id=1, source_target_pairs={{0,1},{1,2},{2,3},{3,0},{4,5},{5,6},{6,7},{7,4},{8,9},{9,10},{10,1... | collective-permute-start | bytes 1572872 | tf_op jit(solution)/shard_map/ppermute | solution.py:17
  48.1 11.1 %collective-permute-start.6 = (bf16[4,16,32,128]{3,2,1,0:T(8,128)(2,1)S(1)}, bf16[4,16,32,128]{3,2,1,0:T(8,128)(2,1)S(1)}, u32[]{:S(2)}, u32[]{:S(2)}) collective-permute-start(bf16[4,16,32,128]{3,2,1,0:T(8,128)(2,1)S(1)} %get-tuple-element.27), channel_id=1, source_target_pairs={{0,4},{4,0},{8,12},{12,8},{16,20},{20,16},{24,28},{28,24},{32,36},... | collective-permute-start | bytes 1572872 | tf_op jit(solution)/shard_map/ppermute | solution.py:24
  48.1 12.6 %collective-permute-start.7 = (bf16[4,16,32,128]{3,2,1,0:T(8,128)(2,1)S(1)}, bf16[4,16,32,128]{3,2,1,0:T(8,128)(2,1)S(1)}, u32[]{:S(2)}, u32[]{:S(2)}) collective-permute-start(bf16[4,16,32,128]{3,2,1,0:T(8,128)(2,1)S(1)} %get-tuple-element.28), channel_id=1, source_target_pairs={{4,8},{8,4},{12,16},{16,12},{20,24},{24,20},{28,32},{32,28},{36,40... | collective-permute-start | bytes 1572872 | tf_op jit(solution)/shard_map/ppermute | solution.py:24
  (1 other events, 0.7 us)

commit v3 on v2

--- a/solution.py
+++ b/solution.py
@@ -21,35 +21,38 @@
     count = lax.axis_size("space")
     near = [(i, i ^ 1) for i in range(count)]
     far = [(i, i - 1 if i % 2 == 0 else i + 1) for i in range(1, count - 1)]
-    return lax.ppermute(on_chip, "space", near), lax.ppermute(off_chip, "space", far)
+    off_chip = lax.ppermute(off_chip, "space", far)
+    on_chip = lax.ppermute(on_chip, "space", near)
+    return on_chip, off_chip
 
 
 def pack_own(core, me, volume, cotangent):
     planes, rows, part, cells = volume.shape
 
-    def body(core_ref, me_ref, v, c, ev, ec):
-        for x, edge in ((v, ev), (c, ec)):
+    def body(core_ref, me_ref, v, c, ev, ec, on_chip, off_chip):
+        side = jnp.where(core_ref[0] == 0, 1, 0)
+        for n, (x, edge) in enumerate(((v, ev), (c, ec))):
             edge[0] = x[:, 0]
             edge[1] = x[:, rows - 1]
+            on_chip[n] = x[:, side * (rows - 1)]
+            off_chip[n] = x[:, (1 - side) * (rows - 1)]
 
     out = jax.ShapeDtypeStruct((2, planes, part, cells), BF16)
     return pl.pallas_call(
         body,
-        out_shape=(out, out),
+        out_shape=(out,) * 4,
         in_specs=[SMEM, SMEM, VMEM, VMEM],
-        out_specs=[VMEM] * 2,
+        out_specs=[VMEM] * 4,
         compiler_params=pltpu.CompilerParams(vmem_limit_bytes=4 * MIB),
         name="pack_own",
     )(core, me, volume, cotangent)
 
 
-def pack_near(core, volume, cotangent, vol_near, cot_near):
+def pack_forward(volume, cotangent, vol_near, cot_near):
     planes, rows, part, cells = volume.shape
     inside = rows - 2
 
-    def body(core_ref, v, c, vn, cn, ev, ec, m_up, m_down, on_chip, off_chip):
-        inner = jnp.where(core_ref[0] == 0, rows - 1, 0)
-        outer = rows - 1 - inner
+    def body(v, c, vn, cn, ev, ec, m_up, m_down):
         for x, edge in ((vn, ev), (cn, ec)):
             edge[0] = x[:, 0]
             edge[1] = x[:, rows - 1]
@@ -58,33 +61,35 @@
                 m_up[n * inside + r] = x[:, 1 + r]
             for n, x in enumerate((v, cn)):
                 m_down[n * inside + r] = x[:, 1 + r]
-        for n, x in enumerate((v, c, vn, cn)):
-            on_chip[n] = x[:, inner]
-            off_chip[n] = x[:, outer]
 
     def out(n):
         return jax.ShapeDtypeStruct((n, planes, part, cells), BF16)
 
     return pl.pallas_call(
         body,
-        out_shape=(out(2), out(2), out(2 * inside), out(2 * inside), out(4), out(4)),
-        in_specs=[SMEM, *[VMEM] * 4],
-        out_specs=[VMEM] * 6,
+        out_shape=(out(2), out(2), out(2 * inside), out(2 * inside)),
+        in_specs=[VMEM] * 4,
+        out_specs=[VMEM] * 4,
         compiler_params=pltpu.CompilerParams(vmem_limit_bytes=8 * MIB),
-        name="pack_near",
-    )(core, volume, cotangent, vol_near, cot_near)
-
-
-def pack_far(core, blocks):
-    _, planes, part, cells = blocks[0].shape
-    count = len(blocks)
+        name="pack_forward",
+    )(volume, cotangent, vol_near, cot_near)
+
+
+def pack_rows(core, wholes, edges):
+    planes, part, cells = edges[0].shape[1:]
+    count = len(wholes) + len(edges)
 
     def body(core_ref, *refs):
         *held, on_chip, off_chip = refs
         side = jnp.where(core_ref[0] == 0, 1, 0)
         for n, x in enumerate(held):
-            on_chip[n] = x[side]
-            off_chip[n] = x[1 - side]
+            if n < len(wholes):
+                rows = x.shape[1]
+                on_chip[n] = x[:, side * (rows - 1)]
+                off_chip[n] = x[:, (1 - side) * (rows - 1)]
+            else:
+                on_chip[n] = x[side]
+                off_chip[n] = x[1 - side]
 
     out = jax.ShapeDtypeStruct((count, planes, part, cells), BF16)
     return pl.pallas_call(
@@ -92,17 +97,20 @@
         out_shape=(out, out),
         in_specs=[SMEM, *[VMEM] * count],
         out_specs=[VMEM] * 2,
-        compiler_params=pltpu.CompilerParams(vmem_limit_bytes=6 * MIB),
-        name="pack_far",
-    )(core, *blocks)
-
-
-def pack_taps(place, own, size):
+        compiler_params=pltpu.CompilerParams(vmem_limit_bytes=8 * MIB),
+    )(core, *wholes, *edges)
+
+
+def pack_taps(place, own, bias, size, cells):
     taps, outs, chans = own.shape
     part = chans // size
     groups = -(-taps // size)
 
-    def body(place_ref, own_ref, *send_refs):
+    def body(place_ref, own_ref, bias_ref, wide_ref, *send_refs):
+        shape = (outs, outs)
+        same = lax.broadcasted_iota(jnp.int32, shape, 0) == lax.broadcasted_iota(jnp.int32, shape, 1)
+        column = jnp.sum(jnp.where(same, bias_ref[...], 0.0), axis=1, keepdims=True)
+        wide_ref[...] = jnp.broadcast_to(column, wide_ref.shape)
         turn = lax.rem(size - place_ref[0], size) * part
         empty = jnp.zeros((outs, chans), jnp.float32)
         for g in range(groups):
@@ -116,15 +124,18 @@
 
     return pl.pallas_call(
         body,
-        out_shape=(jax.ShapeDtypeStruct((groups, outs, chans), BF16),) * size,
-        in_specs=[SMEM, VMEM],
-        out_specs=[VMEM] * size,
+        out_shape=(
+            jax.ShapeDtypeStruct((outs, cells), jnp.float32),
+            *[jax.ShapeDtypeStruct((groups, outs, chans), BF16)] * size,
+        ),
+        in_specs=[SMEM, VMEM, VMEM],
+        out_specs=[VMEM] * (size + 1),
         compiler_params=pltpu.CompilerParams(vmem_limit_bytes=4 * MIB),
         name="pack_taps",
-    )(place, own)
-
-
-def weights(place, own, received, bias, cells):
+    )(place, own, bias.reshape(1, outs))
+
+
+def weights(place, own, received):
     taps, outs, chans = own.shape
     size, groups = len(received), received[0].shape[0]
     part = chans // size
@@ -132,12 +143,8 @@
 
     def body(place_ref, own_ref, *refs):
         got_refs = refs[:size]
-        bias_ref, ahead_a, ahead_b, back_a, back_b, wide_ref = refs[size:]
+        ahead_a, ahead_b, back_a, back_b = refs[size:]
         turn = lax.rem(size - place_ref[0] + 1, size) * part
-        shape = (outs, outs)
-        same = lax.broadcasted_iota(jnp.int32, shape, 0) == lax.broadcasted_iota(jnp.int32, shape, 1)
-        column = jnp.sum(jnp.where(same, bias_ref[...], 0.0), axis=1, keepdims=True)
-        wide_ref[...] = jnp.broadcast_to(column, wide_ref.shape)
         low = lax.broadcasted_iota(jnp.int32, (outs, chans), 1) < half
 
         def put(refs, tiles):
@@ -168,12 +175,12 @@
     out = jax.ShapeDtypeStruct((3 * outs, 9 * half), BF16)
     return pl.pallas_call(
         body,
-        out_shape=(*[out] * 4, jax.ShapeDtypeStruct((outs, cells), jnp.float32)),
-        in_specs=[SMEM, *[VMEM] * (size + 2)],
-        out_specs=[VMEM] * 5,
+        out_shape=(out,) * 4,
+        in_specs=[SMEM, *[VMEM] * (size + 1)],
+        out_specs=[VMEM] * 4,
         compiler_params=pltpu.CompilerParams(vmem_limit_bytes=6 * MIB),
         name="weights",
-    )(place, own, *received, bias.reshape(1, outs))
+    )(place, own, *received)
 
 
 def convolve(source, w_ref, start, o_ref):
@@ -286,22 +293,24 @@
 
     vol_left = shifted(volume, 1)
     cot_right = shifted(cotangent, -1)
-    vol_edge, cot_edge = pack_own(core, me, volume, cotangent)
+    vol_edge, cot_edge, on_chip, off_chip = pack_own(core, me, volume, cotangent)
+    mine = swapped_rows(on_chip, off_chip)
     cot_left_edge = shifted(cot_edge, 1)
     vol_right_edge = shifted(vol_edge, -1)
     own = jnp.swapaxes(kernel, 1, 2)
-    sent = pack_taps(me, own, size)
+    wide, *sent = pack_taps(me, own, bias, size, cells)
     received = [sent[0], *[shifted(sent[size - d], -d) for d in range(1, size)]]
 
-    vol_edge, cot_edge, mid_up, mid_down, on_chip, off_chip = pack_near(core, volume, cotangent, vol_left, cot_right)
+    vol_edge, cot_edge, mid_up, mid_down = pack_forward(volume, cotangent, vol_left, cot_right)
     vol_edge, cot_edge = shifted(vol_edge, 1), shifted(cot_edge, -1)
     mid_up, mid_down = shifted(mid_up, 1), shifted(mid_down, -1)
-    near = swapped_rows(on_chip, off_chip)
-
-    ahead_a, ahead_b, back_a, back_b, wide = weights(me, own, received, bias, cells)
-
-    on_chip, off_chip = pack_far(core, (vol_right_edge, cot_left_edge, vol_edge, cot_edge))
-    far = swapped_rows(on_chip, off_chip)
+    near = pack_rows(core, (vol_left, cot_right), (vol_right_edge, cot_left_edge))
+    near = swapped_rows(*near)
+
+    ahead_a, ahead_b, back_a, back_b = weights(me, own, received)
+
+    far = pack_rows(core, (), (vol_edge, cot_edge))
+    far = swapped_rows(*far)
 
     def whole(x, pair, n):
         return (*pair, n, [(x, False, r) for r in range(rows)])
@@ -312,7 +321,7 @@
 
     sums = stage(
         core,
-        [[whole(vol_left, near, 2), whole(volume, near, 0)], [whole(cotangent, near, 1), whole(cot_right, near, 3)]],
+        [[whole(vol_left, near, 0), whole(volume, mine, 0)], [whole(cotangent, mine, 1), whole(cot_right, near, 1)]],
         (ahead_a, back_a),
         (wide,),
         jnp.float32,
@@ -321,8 +330,8 @@
     return stage(
         core,
         [
-            [split(vol_right_edge, mid_down, 0, far, 0), split(vol_edge, mid_up, 1, far, 2)],
-            [split(cot_edge, mid_down, 1, far, 3), split(cot_left_edge, mid_up, 0, far, 1)],
+            [split(vol_right_edge, mid_down, 0, near, 2), split(vol_edge, mid_up, 1, far, 0)],
+            [split(cot_edge, mid_down, 1, far, 1), split(cot_left_edge, mid_up, 0, near, 3)],
         ],
         (ahead_b, back_b),
         sums,

time: 65.6 us -> 67.3 us (1.026)
  the two profiles are of different devices: /device:TPU:30 before, /device:TPU:24 now
where the time goes in v3:
time: 67.3 us; the launch traced here: 67 us
  starting transfers between devices  30.7 us (46%)
  waiting for transfers between devices  22.3 us (33%)
  Pallas kernels  9.93 us (15%)
  local copies, waits for them, and re-layouts  3.26 us (5%)
  between operations  0.8 us (1%)
    ppermute x11, waiting for transfers between devices, shifted(): lax.ppermute(x, 'chan', [(i, (i + steps) % count) for i in range(count)])  16.6 us
    ppermute x11, starting transfers between devices, shifted(): lax.ppermute(x, 'chan', [(i, (i + steps) % count) for i in range(count)])  16.4 us
    ppermute x3, starting transfers between devices, swapped_rows(): off_chip = lax.ppermute(off_chip, 'space', far)  13.7 us
    pallas_call x2, Pallas kernels, stage(): pl.pallas_call(body, out_shape=(out, out), in_specs=[SMEM, *[VMEM] * (len...  8.59 us
    ppermute x3, waiting for transfers between devices, swapped_rows(): off_chip = lax.ppermute(off_chip, 'space', far)  5.72 us
    unnamed x12, local copies, waits for them, and re-layouts  3.26 us
  transfers between devices with their start and end apart: 17, of which 3 were waited for; matrix products, arithmetic and copies ran while one was open for 0% of the time, Pallas kernels for 8%

profile of v3, /device:TPU:24, one launch (start us, length us, event | category | flops | bytes accessed | tf_op | source)
XLA Modules:
  0.0 67.0 jit_solution(8264623875286457790)
XLA Ops:
  0.6 1.6 %collective-permute-start = (bf16[16,4,32,128]{3,2,1,0:T(8,128)(2,1)}, bf16[16,4,32,128]{3,2,1,0:T(8,128)(2,1)S(1)}, u32[]{:S(2)}, u32[]{:S(2)}) collective-permute-start(bf16[16,4,32,128]{3,2,1,0:T(8,128)(2,1)} %refs_5_.1), channel_id=1, source_target_pairs={{0,1},{1,2},{2,3},{3,0},{4,5},{5,6},{6,7},{7,4},{8,9},{9,10},{10,1... | collective-permute-start | bytes 1572872 | tf_op jit(solution)/shard_map/ppermute | solution.py:17
  2.2 1.7 %collective-permute-start.1 = (bf16[16,4,32,128]{3,2,1,0:T(8,128)(2,1)}, bf16[16,4,32,128]{3,2,1,0:T(8,128)(2,1)S(1)}, u32[]{:S(2)}, u32[]{:S(2)}) collective-permute-start(bf16[16,4,32,128]{3,2,1,0:T(8,128)(2,1)} %refs_6_.1), channel_id=1, source_target_pairs={{0,3},{1,0},{2,1},{3,2},{4,7},{5,4},{6,5},{7,6},{8,11},{9,8},{10,9... | collective-permute-start | bytes 1572872 | tf_op jit(solution)/shard_map/ppermute | solution.py:17
  3.9 1.0 %copy-done = bf16[16,4,32,128]{3,2,1,0:T(8,128)(2,1)S(1)} copy-done((bf16[16,4,32,128]{3,2,1,0:T(8,128)(2,1)S(1)}, bf16[16,4,32,128]{3,2,1,0:T(8,128)(2,1)}, u32[]{:S(2)}) %copy-start) | copy-done | bytes 524312
  5.0 1.0 %copy-done.2 = bf16[16,4,32,128]{3,2,1,0:T(8,128)(2,1)S(1)} copy-done((bf16[16,4,32,128]{3,2,1,0:T(8,128)(2,1)S(1)}, bf16[16,4,32,128]{3,2,1,0:T(8,128)(2,1)}, u32[]{:S(2)}) %copy-start.2) | copy-done | bytes 524312
  6.1 1.6 %collective-permute-start.2 = (bf16[2,16,32,128]{3,2,1,0:T(8,128)(2,1)S(1)}, bf16[2,16,32,128]{3,2,1,0:T(8,128)(2,1)S(1)}, u32[]{:S(2)}, u32[]{:S(2)}) collective-permute-start(bf16[2,16,32,128]{3,2,1,0:T(8,128)(2,1)S(1)} %get-tuple-element.25), channel_id=1, source_target_pairs={{0,3},{1,0},{2,1},{3,2},{4,7},{5,4},{6,5},{7,6},{8,11},{9,8},{10,9... | collective-permute-start | bytes 786440 | tf_op jit(solution)/shard_map/ppermute | solution.py:17
  7.7 0.5 collective-permute-start.3
  8.2 0.7 copy-done.5
  8.9 0.7 pack_taps.1
  9.5 2.8 %collective-permute-start.12 = (bf16[7,32,128]{2,1,0:T(8,128)(2,1)S(1)}, bf16[7,32,128]{2,1,0:T(8,128)(2,1)S(1)}, u32[]{:S(2)}, u32[]{:S(2)}) collective-permute-start(bf16[7,32,128]{2,1,0:T(8,128)(2,1)S(1)} %get-tuple-element.36), channel_id=1, source_target_pairs={{0,3},{1,0},{2,1},{3,2},{4,7},{5,4},{6,5},{7,6},{8,11},{9,8},{10,9... | collective-permute-start | bytes 172040 | tf_op jit(solution)/shard_map/ppermute | solution.py:17
  12.4 9.7 %collective-permute-done.2.refs_2_ = bf16[2,16,32,128]{3,2,1,0:T(8,128)(2,1)S(1)} collective-permute-done((bf16[2,16,32,128]{3,2,1,0:T(8,128)(2,1)S(1)}, bf16[2,16,32,128]{3,2,1,0:T(8,128)(2,1)S(1)}, u32[]{:S(2)}, u32[]{:S(2)}) %collective-permute-start.2) | collective-permute-done | bytes 262176 | tf_op jit(solution)/shard_map/ppermute | solution.py:17
  22.0 2.7 %collective-permute-start.13 = (bf16[7,32,128]{2,1,0:T(8,128)(2,1)S(1)}, bf16[7,32,128]{2,1,0:T(8,128)(2,1)S(1)}, u32[]{:S(2)}, u32[]{:S(2)}) collective-permute-start(bf16[7,32,128]{2,1,0:T(8,128)(2,1)S(1)} %get-tuple-element.37), channel_id=1, source_target_pairs={{0,2},{1,3},{2,0},{3,1},{4,6},{5,7},{6,4},{7,5},{8,10},{9,11},{10,... | collective-permute-start | bytes 172040 | tf_op jit(solution)/shard_map/ppermute | solution.py:17
  24.9 0.6 collective-permute-start.4
  25.4 0.4 copy-done.1
  26.1 1.2 %collective-permute-start.7 = (bf16[2,16,32,128]{3,2,1,0:T(8,128)(2,1)S(1)}, bf16[2,16,32,128]{3,2,1,0:T(8,128)(2,1)S(1)}, u32[]{:S(2)}, u32[]{:S(2)}) collective-permute-start(bf16[2,16,32,128]{3,2,1,0:T(8,128)(2,1)S(1)} %get-tuple-element.30), channel_id=1, source_target_pairs={{0,1},{1,2},{2,3},{3,0},{4,5},{5,6},{6,7},{7,4},{8,9},{9,10},{10,1... | collective-permute-start | bytes 786440 | tf_op jit(solution)/shard_map/ppermute | solution.py:17
  27.2 2.2 %collective-permute-start.8 = (bf16[2,16,32,128]{3,2,1,0:T(8,128)(2,1)S(1)}, bf16[2,16,32,128]{3,2,1,0:T(8,128)(2,1)S(1)}, u32[]{:S(2)}, u32[]{:S(2)}) collective-permute-start(bf16[2,16,32,128]{3,2,1,0:T(8,128)(2,1)S(1)} %get-tuple-element.31), channel_id=1, source_target_pairs={{0,3},{1,0},{2,1},{3,2},{4,7},{5,4},{6,5},{7,6},{8,11},{9,8},{10,9... | collective-permute-start | bytes 786440 | tf_op jit(solution)/shard_map/ppermute | solution.py:17
  29.4 6.9 %collective-permute-done.14.refs_3_ = bf16[7,32,128]{2,1,0:T(8,128)(2,1)S(1)} collective-permute-done((bf16[7,32,128]{2,1,0:T(8,128)(2,1)S(1)}, bf16[7,32,128]{2,1,0:T(8,128)(2,1)S(1)}, u32[]{:S(2)}, u32[]{:S(2)}) %collective-permute-start.14) | collective-permute-done | bytes 57376 | tf_op jit(solution)/shard_map/ppermute | solution.py:17
  36.3 6.2 %collective-permute-start.5 = (bf16[4,16,32,128]{3,2,1,0:T(8,128)(2,1)S(1)}, bf16[4,16,32,128]{3,2,1,0:T(8,128)(2,1)S(1)}, u32[]{:S(2)}, u32[]{:S(2)}) collective-permute-start(bf16[4,16,32,128]{3,2,1,0:T(8,128)(2,1)S(1)} %get-tuple-element.28), channel_id=1, source_target_pairs={{4,8},{8,4},{12,16},{16,12},{20,24},{24,20},{28,32},{32,28},{36,40... | collective-permute-start | bytes 1572872 | tf_op jit(solution)/shard_map/ppermute | solution.py:24
  42.5 1.9 %collective-permute-start.16 = (bf16[2,16,32,128]{3,2,1,0:T(8,128)(2,1)S(1)}, bf16[2,16,32,128]{3,2,1,0:T(8,128)(2,1)S(1)}, u32[]{:S(2)}, u32[]{:S(2)}) collective-permute-start(bf16[2,16,32,128]{3,2,1,0:T(8,128)(2,1)S(1)} %get-tuple-element.42), channel_id=1, source_target_pairs={{4,8},{8,4},{12,16},{16,12},{20,24},{24,20},{28,32},{32,28},{36,40... | collective-permute-start | bytes 786440 | tf_op jit(solution)/shard_map/ppermute | solution.py:24
  44.8 1.8 %collective-permute-start.11 = (bf16[4,16,32,128]{3,2,1,0:T(8,128)(2,1)S(1)}, bf16[4,16,32,128]{3,2,1,0:T(8,128)(2,1)S(1)}, u32[]{:S(2)}, u32[]{:S(2)}) collective-permute-start(bf16[4,16,32,128]{3,2,1,0:T(8,128)(2,1)S(1)} %get-tuple-element.34), channel_id=1, source_target_pairs={{0,1},{1,2},{2,3},{3,0},{4,5},{5,6},{6,7},{7,4},{8,9},{9,10},{10,1... | collective-permute-start | bytes 1572872 | tf_op jit(solution)/shard_map/ppermute | solution.py:17
  46.6 5.7 %collective-permute-done.16.refs_4_ = bf16[2,16,32,128]{3,2,1,0:T(8,128)(2,1)S(1)} collective-permute-done((bf16[2,16,32,128]{3,2,1,0:T(8,128)(2,1)S(1)}, bf16[2,16,32,128]{3,2,1,0:T(8,128)(2,1)S(1)}, u32[]{:S(2)}, u32[]{:S(2)}) %collective-permute-start.16) | collective-permute-done | bytes 262176 | tf_op jit(solution)/shard_map/ppermute | solution.py:24
  52.4 5.6 %collective-permute-start.10 = (bf16[2,16,32,128]{3,2,1,0:T(8,128)(2,1)S(1)}, bf16[2,16,32,128]{3,2,1,0:T(8,128)(2,1)S(1)}, u32[]{:S(2)}, u32[]{:S(2)}) collective-permute-start(bf16[2,16,32,128]{3,2,1,0:T(8,128)(2,1)S(1)} %get-tuple-element.33), channel_id=1, source_target_pairs={{4,8},{8,4},{12,16},{16,12},{20,24},{24,20},{28,32},{32,28},{36,40... | collective-permute-start | bytes 786440 | tf_op jit(solution)/shard_map/ppermute | solution.py:24
  58.0 0.4 weights.1
  58.3 4.0 %shard_map.61 = (f32[16,4,32,128]{3,2,1,0:T(8,128)S(1)}, f32[16,4,32,128]{3,2,1,0:T(8,128)S(1)}) custom-call(s32[1]{0:T(128)} %bitcast.core_ref, bf16[4,16,32,128]{3,2,1,0:T(8,128)(2,1)S(1)} %collective-permute-done.4.refs_0_, bf16[4,16,32,128]{3,2,1,0:T(8,128)(2,1)S(1)} %collective-permute-done.5.refs_1_, ...), custom_call_target="tpu_custom_call" | custom-call | flops 1811939328 | bytes 6291456 | tf_op jit(solution)/shard_map/pallas_call | solution.py:273
  62.4 4.6 %shard_map.62 = (bf16[16,4,32,128]{3,2,1,0:T(8,128)(2,1)}, bf16[16,4,32,128]{3,2,1,0:T(8,128)(2,1)}) custom-call(s32[1]{0:T(128)} %bitcast.core_ref, bf16[4,16,32,128]{3,2,1,0:T(8,128)(2,1)S(1)} %collective-permute-done.4.refs_0_, bf16[4,16,32,128]{3,2,1,0:T(8,128)(2,1)S(1)} %collective-permute-done.5.refs_1_, ...), custom_call_target="tpu_custom_call" | custom-call | flops 1811939328 | bytes 6291456 | tf_op jit(solution)/shard_map/pallas_call | solution.py:273
  (30 shorter events, 0.8 us)
Async XLA Ops:
  0.6 24.1 %collective-permute-start = (bf16[16,4,32,128]{3,2,1,0:T(8,128)(2,1)}, bf16[16,4,32,128]{3,2,1,0:T(8,128)(2,1)S(1)}, u32[]{:S(2)}, u32[]{:S(2)}) collective-permute-start(bf16[16,4,32,128]{3,2,1,0:T(8,128)(2,1)} %refs_5_.1), channel_id=1, source_target_pairs={{0,1},{1,2},{2,3},{3,0},{4,5},{5,6},{6,7},{7,4},{8,9},{9,10},{10,1... | collective-permute-start | bytes 1572872 | tf_op jit(solution)/shard_map/ppermute | solution.py:17
  2.2 22.6 %collective-permute-start.1 = (bf16[16,4,32,128]{3,2,1,0:T(8,128)(2,1)}, bf16[16,4,32,128]{3,2,1,0:T(8,128)(2,1)S(1)}, u32[]{:S(2)}, u32[]{:S(2)}) collective-permute-start(bf16[16,4,32,128]{3,2,1,0:T(8,128)(2,1)} %refs_6_.1), channel_id=1, source_target_pairs={{0,3},{1,0},{2,1},{3,2},{4,7},{5,4},{6,5},{7,6},{8,11},{9,8},{10,9... | collective-permute-start | bytes 1572872 | tf_op jit(solution)/shard_map/ppermute | solution.py:17
  3.9 1.0 %copy-start = (bf16[16,4,32,128]{3,2,1,0:T(8,128)(2,1)S(1)}, bf16[16,4,32,128]{3,2,1,0:T(8,128)(2,1)}, u32[]{:S(2)}) copy-start(bf16[16,4,32,128]{3,2,1,0:T(8,128)(2,1)} %refs_5_.1) | copy-start | bytes 1572868
  5.0 1.0 %copy-start.2 = (bf16[16,4,32,128]{3,2,1,0:T(8,128)(2,1)S(1)}, bf16[16,4,32,128]{3,2,1,0:T(8,128)(2,1)}, u32[]{:S(2)}) copy-start(bf16[16,4,32,128]{3,2,1,0:T(8,128)(2,1)} %refs_6_.1) | copy-start | bytes 1572868
  6.0 2.2 %copy-start.4 = (bf16[27,128,32]{1,2,0:T(8,128)(2,1)S(1)}, bf16[27,128,32]{1,2,0:T(8,128)(2,1)}, u32[]{:S(2)}) copy-start(bf16[27,128,32]{1,2,0:T(8,128)(2,1)} %param.5) | copy-start | bytes 663556
  6.1 15.9 %collective-permute-start.2 = (bf16[2,16,32,128]{3,2,1,0:T(8,128)(2,1)S(1)}, bf16[2,16,32,128]{3,2,1,0:T(8,128)(2,1)S(1)}, u32[]{:S(2)}, u32[]{:S(2)}) collective-permute-start(bf16[2,16,32,128]{3,2,1,0:T(8,128)(2,1)S(1)} %get-tuple-element.25), channel_id=1, source_target_pairs={{0,3},{1,0},{2,1},{3,2},{4,7},{5,4},{6,5},{7,6},{8,11},{9,8},{10,9... | collective-permute-start | bytes 786440 | tf_op jit(solution)/shard_map/ppermute | solution.py:17
  7.7 17.0 %collective-permute-start.3 = (bf16[2,16,32,128]{3,2,1,0:T(8,128)(2,1)S(1)}, bf16[2,16,32,128]{3,2,1,0:T(8,128)(2,1)S(1)}, u32[]{:S(2)}, u32[]{:S(2)}) collective-permute-start(bf16[2,16,32,128]{3,2,1,0:T(8,128)(2,1)S(1)} %get-tuple-element.26), channel_id=1, source_target_pairs={{0,1},{1,2},{2,3},{3,0},{4,5},{5,6},{6,7},{7,4},{8,9},{9,10},{10,1... | collective-permute-start | bytes 786440 | tf_op jit(solution)/shard_map/ppermute | solution.py:17
  8.2 0.7 copy-start.5
  9.5 17.7 %collective-permute-start.12 = (bf16[7,32,128]{2,1,0:T(8,128)(2,1)S(1)}, bf16[7,32,128]{2,1,0:T(8,128)(2,1)S(1)}, u32[]{:S(2)}, u32[]{:S(2)}) collective-permute-start(bf16[7,32,128]{2,1,0:T(8,128)(2,1)S(1)} %get-tuple-element.36), channel_id=1, source_target_pairs={{0,3},{1,0},{2,1},{3,2},{4,7},{5,4},{6,5},{7,6},{8,11},{9,8},{10,9... | collective-permute-start | bytes 172040 | tf_op jit(solution)/shard_map/ppermute | solution.py:17
  22.0 7.4 %collective-permute-start.13 = (bf16[7,32,128]{2,1,0:T(8,128)(2,1)S(1)}, bf16[7,32,128]{2,1,0:T(8,128)(2,1)S(1)}, u32[]{:S(2)}, u32[]{:S(2)}) collective-permute-start(bf16[7,32,128]{2,1,0:T(8,128)(2,1)S(1)} %get-tuple-element.37), channel_id=1, source_target_pairs={{0,2},{1,3},{2,0},{3,1},{4,6},{5,7},{6,4},{7,5},{8,10},{9,11},{10,... | collective-permute-start | bytes 172040 | tf_op jit(solution)/shard_map/ppermute | solution.py:17
  24.8 1.0 %copy-start.1 = (bf16[16,4,32,128]{3,2,1,0:T(8,128)(2,1)S(1)}, bf16[16,4,32,128]{3,2,1,0:T(8,128)(2,1)}, u32[]{:S(2)}) copy-start(bf16[16,4,32,128]{3,2,1,0:T(8,128)(2,1)} %refs_5_.1) | copy-start | bytes 1572868
  24.8 1.2 %copy-start.3 = (bf16[16,4,32,128]{3,2,1,0:T(8,128)(2,1)S(1)}, bf16[16,4,32,128]{3,2,1,0:T(8,128)(2,1)}, u32[]{:S(2)}) copy-start(bf16[16,4,32,128]{3,2,1,0:T(8,128)(2,1)} %refs_6_.1) | copy-start | bytes 1572868
  24.8 17.8 %collective-permute-start.15 = (bf16[2,16,32,128]{3,2,1,0:T(8,128)(2,1)S(1)}, bf16[2,16,32,128]{3,2,1,0:T(8,128)(2,1)S(1)}, u32[]{:S(2)}, u32[]{:S(2)}) collective-permute-start(bf16[2,16,32,128]{3,2,1,0:T(8,128)(2,1)S(1)} %get-tuple-element.41), channel_id=1, source_target_pairs={{0,4},{4,0},{8,12},{12,8},{16,20},{20,16},{24,28},{28,24},{32,36},... | collective-permute-start | bytes 786440 | tf_op jit(solution)/shard_map/ppermute | solution.py:25
  24.9 27.5 %collective-permute-start.4 = (bf16[4,16,32,128]{3,2,1,0:T(8,128)(2,1)S(1)}, bf16[4,16,32,128]{3,2,1,0:T(8,128)(2,1)S(1)}, u32[]{:S(2)}, u32[]{:S(2)}) collective-permute-start(bf16[4,16,32,128]{3,2,1,0:T(8,128)(2,1)S(1)} %get-tuple-element.27), channel_id=1, source_target_pairs={{0,4},{4,0},{8,12},{12,8},{16,20},{20,16},{24,28},{28,24},{32,36},... | collective-permute-start | bytes 1572872 | tf_op jit(solution)/shard_map/ppermute | solution.py:25
  26.1 18.4 %collective-permute-start.7 = (bf16[2,16,32,128]{3,2,1,0:T(8,128)(2,1)S(1)}, bf16[2,16,32,128]{3,2,1,0:T(8,128)(2,1)S(1)}, u32[]{:S(2)}, u32[]{:S(2)}) collective-permute-start(bf16[2,16,32,128]{3,2,1,0:T(8,128)(2,1)S(1)} %get-tuple-element.30), channel_id=1, source_target_pairs={{0,1},{1,2},{2,3},{3,0},{4,5},{5,6},{6,7},{7,4},{8,9},{9,10},{10,1... | collective-permute-start | bytes 786440 | tf_op jit(solution)/shard_map/ppermute | solution.py:17
  27.2 17.5 %collective-permute-start.8 = (bf16[2,16,32,128]{3,2,1,0:T(8,128)(2,1)S(1)}, bf16[2,16,32,128]{3,2,1,0:T(8,128)(2,1)S(1)}, u32[]{:S(2)}, u32[]{:S(2)}) collective-permute-start(bf16[2,16,32,128]{3,2,1,0:T(8,128)(2,1)S(1)} %get-tuple-element.31), channel_id=1, source_target_pairs={{0,3},{1,0},{2,1},{3,2},{4,7},{5,4},{6,5},{7,6},{8,11},{9,8},{10,9... | collective-permute-start | bytes 786440 | tf_op jit(solution)/shard_map/ppermute | solution.py:17
  29.4 6.9 %collective-permute-start.14 = (bf16[7,32,128]{2,1,0:T(8,128)(2,1)S(1)}, bf16[7,32,128]{2,1,0:T(8,128)(2,1)S(1)}, u32[]{:S(2)}, u32[]{:S(2)}) collective-permute-start(bf16[7,32,128]{2,1,0:T(8,128)(2,1)S(1)} %get-tuple-element.38), channel_id=1, source_target_pairs={{0,1},{1,2},{2,3},{3,0},{4,5},{5,6},{6,7},{7,4},{8,9},{9,10},{10,1... | collective-permute-start | bytes 172040 | tf_op jit(solution)/shard_map/ppermute | solution.py:17
  36.3 22.0 %collective-permute-start.5 = (bf16[4,16,32,128]{3,2,1,0:T(8,128)(2,1)S(1)}, bf16[4,16,32,128]{3,2,1,0:T(8,128)(2,1)S(1)}, u32[]{:S(2)}, u32[]{:S(2)}) collective-permute-start(bf16[4,16,32,128]{3,2,1,0:T(8,128)(2,1)S(1)} %get-tuple-element.28), channel_id=1, source_target_pairs={{4,8},{8,4},{12,16},{16,12},{20,24},{24,20},{28,32},{32,28},{36,40... | collective-permute-start | bytes 1572872 | tf_op jit(solution)/shard_map/ppermute | solution.py:24
  42.5 9.8 %collective-permute-start.16 = (bf16[2,16,32,128]{3,2,1,0:T(8,128)(2,1)S(1)}, bf16[2,16,32,128]{3,2,1,0:T(8,128)(2,1)S(1)}, u32[]{:S(2)}, u32[]{:S(2)}) collective-permute-start(bf16[2,16,32,128]{3,2,1,0:T(8,128)(2,1)S(1)} %get-tuple-element.42), channel_id=1, source_target_pairs={{4,8},{8,4},{12,16},{16,12},{20,24},{24,20},{28,32},{32,28},{36,40... | collective-permute-start | bytes 786440 | tf_op jit(solution)/shard_map/ppermute | solution.py:24
  44.5 17.9 %collective-permute-start.6 = (bf16[4,16,32,128]{3,2,1,0:T(8,128)(2,1)S(1)}, bf16[4,16,32,128]{3,2,1,0:T(8,128)(2,1)S(1)}, u32[]{:S(2)}, u32[]{:S(2)}) collective-permute-start(bf16[4,16,32,128]{3,2,1,0:T(8,128)(2,1)S(1)} %get-tuple-element.29), channel_id=1, source_target_pairs={{0,3},{1,0},{2,1},{3,2},{4,7},{5,4},{6,5},{7,6},{8,11},{9,8},{10,9... | collective-permute-start | bytes 1572872 | tf_op jit(solution)/shard_map/ppermute | solution.py:17
  44.8 17.6 %collective-permute-start.11 = (bf16[4,16,32,128]{3,2,1,0:T(8,128)(2,1)S(1)}, bf16[4,16,32,128]{3,2,1,0:T(8,128)(2,1)S(1)}, u32[]{:S(2)}, u32[]{:S(2)}) collective-permute-start(bf16[4,16,32,128]{3,2,1,0:T(8,128)(2,1)S(1)} %get-tuple-element.34), channel_id=1, source_target_pairs={{0,1},{1,2},{2,3},{3,0},{4,5},{5,6},{6,7},{7,4},{8,9},{9,10},{10,1... | collective-permute-start | bytes 1572872 | tf_op jit(solution)/shard_map/ppermute | solution.py:17
  52.3 10.0 %collective-permute-start.9 = (bf16[2,16,32,128]{3,2,1,0:T(8,128)(2,1)S(1)}, bf16[2,16,32,128]{3,2,1,0:T(8,128)(2,1)S(1)}, u32[]{:S(2)}, u32[]{:S(2)}) collective-permute-start(bf16[2,16,32,128]{3,2,1,0:T(8,128)(2,1)S(1)} %get-tuple-element.32), channel_id=1, source_target_pairs={{0,4},{4,0},{8,12},{12,8},{16,20},{20,16},{24,28},{28,24},{32,36},... | collective-permute-start | bytes 786440 | tf_op jit(solution)/shard_map/ppermute | solution.py:25
  52.4 10.0 %collective-permute-start.10 = (bf16[2,16,32,128]{3,2,1,0:T(8,128)(2,1)S(1)}, bf16[2,16,32,128]{3,2,1,0:T(8,128)(2,1)S(1)}, u32[]{:S(2)}, u32[]{:S(2)}) collective-permute-start(bf16[2,16,32,128]{3,2,1,0:T(8,128)(2,1)S(1)} %get-tuple-element.33), channel_id=1, source_target_pairs={{4,8},{8,4},{12,16},{16,12},{20,24},{24,20},{28,32},{32,28},{36,40... | collective-permute-start | bytes 786440 | tf_op jit(solution)/shard_map/ppermute | solution.py:24

commit v4 on v3

v4 whole, which is shorter than its diff:
```python
import jax
import jax.numpy as jnp
from jax import lax
from jax.experimental import pallas as pl
from jax.experimental.pallas import tpu as pltpu
from jax.sharding import PartitionSpec as P


MIB = 1024 * 1024
BF16 = jnp.bfloat16
VMEM = pl.BlockSpec(memory_space=pltpu.VMEM)
SMEM = pl.BlockSpec(memory_space=pltpu.SMEM)


INNER_ONE = tuple((0, at) for at in range(8))
INNER_TWO = (*[(1, at) for at in range(9)], (0, 8))
OUTER_ONE = (*[(0, at) for at in range(9)], (1, 1), (1, 4), (1, 7))
OUTER_TWO = tuple((1, at) for at in (0, 2, 3, 5, 6, 8))


def shifted(x, steps):
    count = lax.axis_size("chan")
    return lax.ppermute(x, "chan", [(i, (i + steps) % count) for i in range(count)])


def swapped_rows(on_chip, off_chip):
    count = lax.axis_size("space")
    near = [(i, i ^ 1) for i in range(count)]
    far = [(i, i - 1 if i % 2 == 0 else i + 1) for i in range(1, count - 1)]
    off_chip = lax.ppermute(off_chip, "space", far)
    on_chip = lax.ppermute(on_chip, "space", near)
    return on_chip, off_chip


def pack_forward(volume, cotangent, vol_near, cot_near):
    planes, rows, part, cells = volume.shape
    inside = rows - 2

    def body(v, c, vn, cn, ev, ec, m_up, m_down):
        for x, edge in ((vn, ev), (cn, ec)):
            edge[0] = x[:, 0]
            edge[1] = x[:, rows - 1]
        for r in range(inside):
            for n, x in enumerate((c, vn)):
                m_up[n * inside + r] = x[:, 1 + r]
            for n, x in enumerate((v, cn)):
                m_down[n * inside + r] = x[:, 1 + r]

    def out(n):
        return jax.ShapeDtypeStruct((n, planes, part, cells), BF16)

    return pl.pallas_call(
        body,
        out_shape=(out(2), out(2), out(2 * inside), out(2 * inside)),
        in_specs=[VMEM] * 4,
        out_specs=[VMEM] * 4,
        compiler_params=pltpu.CompilerParams(vmem_limit_bytes=8 * MIB),
        name="pack_forward",
    )(volume, cotangent, vol_near, cot_near)


def pack_rows(core, wholes, edges):
    planes, part, cells = edges[0].shape[1:]
    count = len(wholes) + len(edges)

    def body(core_ref, *refs):
        *held, on_chip, off_chip = refs
        side = jnp.where(core_ref[0] == 0, 1, 0)
        for n, x in enumerate(held):
            if n < len(wholes):
                rows = x.shape[1]
                on_chip[n] = x[:, side * (rows - 1)]
                off_chip[n] = x[:, (1 - side) * (rows - 1)]
            else:
                on_chip[n] = x[side]
                off_chip[n] = x[1 - side]

    out = jax.ShapeDtypeStruct((count, planes, part, cells), BF16)
    return pl.pallas_call(
        body,
        out_shape=(out, out),
        in_specs=[SMEM, *[VMEM] * count],
        out_specs=[VMEM] * 2,
        compiler_params=pltpu.CompilerParams(vmem_limit_bytes=8 * MIB),
    )(core, *wholes, *edges)


def prologue(core, place, volume, cotangent, own, bias, size):
    planes, rows, part, cells = volume.shape
    taps, outs, chans = own.shape
    groups = -(-taps // size)

    def body(core_ref, place_ref, v, c, own_ref, bias_ref, *out_refs):
        ev, ec, on_chip, off_chip, wide_ref, *send_refs = out_refs
        side = jnp.where(core_ref[0] == 0, 1, 0)
        for n, (x, edge) in enumerate(((v, ev), (c, ec))):
            edge[0] = x[:, 0]
            edge[1] = x[:, rows - 1]
            on_chip[n] = x[:, side * (rows - 1)]
            off_chip[n] = x[:, (1 - side) * (rows - 1)]
        shape = (outs, outs)
        same = lax.broadcasted_iota(jnp.int32, shape, 0) == lax.broadcasted_iota(jnp.int32, shape, 1)
        column = jnp.sum(jnp.where(same, bias_ref[...], 0.0), axis=1, keepdims=True)
        wide_ref[...] = jnp.broadcast_to(column, wide_ref.shape)
        turn = lax.rem(size - place_ref[0], size) * part
        empty = jnp.zeros((outs, chans), jnp.float32)
        for g in range(groups):
            quad = [
                pltpu.roll(own_ref[taps - 1 - t].astype(jnp.float32), turn, 1) if t < taps else empty
                for t in range(g * size, (g + 1) * size)
            ]
            for j in range(size):
                pieces = [q[:, j * part : (j + 1) * part] for q in quad]
                send_refs[j][g] = jnp.concatenate(pieces, axis=1).astype(BF16)

    two = jax.ShapeDtypeStruct((2, planes, part, cells), BF16)
    return pl.pallas_call(
        body,
        out_shape=(
            *[two] * 4,
            jax.ShapeDtypeStruct((outs, cells), jnp.float32),
            *[jax.ShapeDtypeStruct((groups, outs, chans), BF16)] * size,
        ),
        in_specs=[SMEM, SMEM, *[VMEM] * 4],
        out_specs=[VMEM] * (size + 5),
        compiler_params=pltpu.CompilerParams(vmem_limit_bytes=61 * MIB + MIB // 2),
        name="prologue",
    )(core, place, volume, cotangent, own, bias.reshape(1, outs))


def weights(place, own, received, layouts):
    taps, outs, chans = own.shape
    size, groups = len(received), received[0].shape[0]
    part = chans // size
    half = chans // 2

    def body(place_ref, own_ref, *refs):
        got_refs = refs[:size]
        table_refs = refs[size:]
        turn = lax.rem(size - place_ref[0] + 1, size) * part
        low = lax.broadcasted_iota(jnp.int32, (outs, chans), 1) < half

        def put(ref, chunks, tiles):
            for c in range(3):
                here = slice(c * outs, (c + 1) * outs)
                for k in range(0, len(chunks), 2):
                    found = []
                    for side, (n, at) in enumerate(chunks[k : k + 2]):
                        tile = tiles[3 * at + c]
                        found.append(tile if n == side else pltpu.roll(tile, half, 1))
                    if len(found) == 2:
                        both = jnp.where(low, *found)
                        ref[here, k * half : (k + 2) * half] = both.astype(BF16)
                    else:
                        ref[here, k * half :] = found[0][:, :half].astype(BF16)

        tiles = [pltpu.roll(own_ref[t].astype(jnp.float32), turn, 1) for t in range(taps)]
        for n, chunks in enumerate(layouts):
            put(table_refs[2 * n], chunks, tiles)
        tiles = []
        for g in range(groups):
            tile = jnp.concatenate([got[g] for got in got_refs], axis=0)
            tile = tile.astype(jnp.float32).T
            tiles += [tile[t * part : (t + 1) * part] for t in range(size)]
        for n, chunks in enumerate(layouts):
            put(table_refs[2 * n + 1], chunks, tiles)

    shapes = [jax.ShapeDtypeStruct((3 * outs, len(chunks) * half), BF16) for chunks in layouts]
    return pl.pallas_call(
        body,
        out_shape=tuple(shape for shape in shapes for _ in range(2)),
        in_specs=[SMEM, *[VMEM] * (size + 1)],
        out_specs=[VMEM] * (2 * len(layouts)),
        compiler_params=pltpu.CompilerParams(vmem_limit_bytes=8 * MIB),
        name="weights",
    )(place, own, *received)


def stage(core, halves, jobs, starts, shape, final):
    planes, rows, part, cells = shape
    outs = part
    wide = 2 * cells
    needed = set()
    for pair, chunks, _ in jobs:
        needed |= {(n, r + at % 3) for n, at in chunks for r in pair}
    operands = []

    def place(x):
        for i, y in enumerate(operands):
            if y is x:
                return i
        operands.append(x)
        return len(operands) - 1

    blocks = []
    edges = []
    for n in range(2):
        for conv in range(2):
            for s, (on_chip, off_chip, index, inner) in enumerate(halves[n][conv]):
                for r in range(1, rows + 1):
                    if (n, r) in needed:
                        x, before, at = inner[r - 1]
                        blocks.append(((n, conv, s, r), place(x), before, at))
                if (n, 0) in needed or (n, rows + 1) in needed:
                    edges.append(((n, conv, s), place(on_chip), place(off_chip), index))
    where = {key: rest for key, *rest in blocks}
    edge_at = {key: i for i, (key, *_) in enumerate(edges)}
    tables = [table for _, _, pair in jobs for table in pair]
    extra = [x for found in starts for _, x in found]
    offsets = [sum(len(found) for found in starts[:n]) for n in range(2)]
    count = len(halves[0][0])

    def body(core_ref, *refs):
        refs = list(refs)
        held = [refs.pop(0) for _ in operands]
        w_refs = [refs.pop(0) for _ in tables]
        s_refs = [refs.pop(0) for _ in extra]
        o_refs = [refs.pop(0) for _ in range(2)]
        if edges:
            low_ref, high_ref = refs.pop(0), refs.pop(0)

            @pl.when(core_ref[0] == 0)
            def _():
                for i, (_, on_chip, off_chip, index) in enumerate(edges):
                    high_ref[i] = held[on_chip][index]
                    low_ref[i] = held[off_chip][index]

            @pl.when(core_ref[0] != 0)
            def _():
                for i, (_, on_chip, off_chip, index) in enumerate(edges):
                    low_ref[i] = held[on_chip][index]
                    high_ref[i] = held[off_chip][index]

        if final:
            done_refs, sems = [refs.pop(0), refs.pop(0)], refs.pop(0)
        lane = lax.broadcasted_iota(jnp.int32, (outs, wide), 1) % cells
        first = lane == 0
        last = lane == cells - 1
        zero = jnp.zeros((count * part, cells), BF16)

        def source(n, conv, p, r):
            if p < 0 or p >= planes:
                return [zero]
            if r == 0:
                return [low_ref[edge_at[n, conv, s], p] for s in range(count)]
            if r == rows + 1:
                return [high_ref[edge_at[n, conv, s], p] for s in range(count)]
            found = []
            for s in range(count):
                operand, before, at = where[n, conv, s, r]
                found.append(held[operand][at, p] if before else held[operand][p, at])
            return found

        pending = []
        half = planes // 2
        for conv in range(2):
            for p in range(planes):
                for j, (pair, chunks, _) in enumerate(jobs):
                    columns = []
                    for r in pair:
                        stack = []
                        for n, at in chunks:
                            stack += source(n, conv, p + at // 3 - 1, r + at % 3)
                        columns.append(jnp.concatenate(stack, axis=0))
                    data = jnp.concatenate(columns, axis=1)
                    sums = jnp.dot(w_refs[2 * j + conv][...], data, preferred_element_type=jnp.float32)
                    total = sums[outs : 2 * outs]
                    total = total + jnp.where(first, 0.0, pltpu.roll(sums[:outs], 1, 1))
                    total = total + jnp.where(last, 0.0, pltpu.roll(sums[2 * outs :], wide - 1, 1))
                    for i, r in enumerate(pair):
                        piece = total[:, i * cells : (i + 1) * cells]
                        for m, (which, _) in enumerate(starts[conv]):
                            ref = s_refs[offsets[conv] + m]
                            if which is None:
                                piece = piece + ref[...]
                            elif r in which:
                                piece = piece + ref[p, which.index(r)]
                        if final:
                            done_refs[conv][p, r] = piece.astype(BF16)
                        else:
                            o_refs[conv][p, i] = piece
                if final and (p + 1) % half == 0:
                    span = pl.ds(p + 1 - half, half)
                    copy = pltpu.make_async_copy(
                        done_refs[conv].at[span], o_refs[conv].at[span], sems.at[len(pending)]
                    )
                    copy.start()
                    pending.append(copy)
        for copy in pending:
            copy.wait()

    kept = rows if final else 2
    out = jax.ShapeDtypeStruct((planes, kept, part, cells), BF16 if final else jnp.float32)
    scratch = []
    if edges:
        scratch += [pltpu.VMEM((len(edges), planes, part, cells), BF16)] * 2
    if final:
        scratch += [pltpu.VMEM(shape, BF16)] * 2 + [pltpu.SemaphoreType.DMA((4,))]
    depth = sum(len(chunks) for _, chunks, _ in jobs)
    return pl.pallas_call(
        body,
        out_shape=(out, out),
        in_specs=[SMEM, *[VMEM] * (len(operands) + len(tables) + len(extra))],
        out_specs=[pl.BlockSpec(memory_space=pl.ANY)] * 2 if final else [VMEM, VMEM],
        scratch_shapes=scratch,
        compiler_params=pltpu.CompilerParams(vmem_limit_bytes=14 * MIB),
        cost_estimate=pl.CostEstimate(
            flops=8 * 3 * outs * depth * count * part * planes * cells,
            bytes_accessed=6 * MIB,
            transcendentals=0,
        ),
    )(core, *operands, *tables, *extra)


def per_device(volume, kernel, bias, cotangent):
    size = lax.axis_size("chan")
    me = lax.axis_index("chan").astype(jnp.int32).reshape(1)
    core = (lax.axis_index("space") % 2).astype(jnp.int32).reshape(1)
    _, rows, _, _ = volume.shape

    vol_left = shifted(volume, 1)
    cot_right = shifted(cotangent, -1)
    own = jnp.swapaxes(kernel, 1, 2)
    vol_edge, cot_edge, on_chip, off_chip, wide, *sent = prologue(
        core, me, volume, cotangent, own, bias, size
    )
    received = [sent[0], *[shifted(sent[size - d], -d) for d in range(1, size)]]
    cot_left_edge = shifted(cot_edge, 1)
    vol_right_edge = shifted(vol_edge, -1)
    mine = swapped_rows(on_chip, off_chip)

    vol_edge, cot_edge, mid_up, mid_down = pack_forward(volume, cotangent, vol_left, cot_right)
    vol_edge, cot_edge = shifted(vol_edge, 1), shifted(cot_edge, -1)
    mid_up, mid_down = shifted(mid_up, 1), shifted(mid_down, -1)
    near = pack_rows(core, (vol_left, cot_right), (vol_right_edge, cot_left_edge))
    near = swapped_rows(*near)

    tables = weights(me, own, received, (INNER_ONE, OUTER_ONE, INNER_TWO, OUTER_TWO))
    inner_one, outer_one, inner_two, outer_two = (tables[n : n + 2] for n in range(0, 8, 2))

    far = pack_rows(core, (), (vol_edge, cot_edge))
    far = swapped_rows(*far)

    def whole(x, pair, n):
        return (*pair, n, [(x, False, r) for r in range(rows)])

    def split(edge, middle, half, pair, n):
        inner = [(middle, True, half * (rows - 2) + r) for r in range(rows - 2)]
        return (*pair, n, [(edge, True, 0), *inner, (edge, True, 1)])

    halves = (
        (
            [whole(vol_left, near, 0), whole(volume, mine, 0)],
            [whole(cotangent, mine, 1), whole(cot_right, near, 1)],
        ),
        (
            [split(vol_right_edge, mid_down, 0, near, 2), split(vol_edge, mid_up, 1, far, 0)],
            [split(cot_edge, mid_down, 1, far, 1), split(cot_left_edge, mid_up, 0, near, 3)],
        ),
    )
    inner, outer = tuple(range(1, rows - 1)), (0, rows - 1)
    starts = (((None, wide),), ())
    shape = volume.shape
    jobs = ((inner, INNER_ONE, inner_one),)
    insides = stage(core, halves, jobs, starts, shape, False)
    jobs = ((outer, OUTER_ONE, outer_one),)
    outsides = stage(core, halves, jobs, starts, shape, False)
    jobs = ((inner, INNER_TWO, inner_two), (outer, OUTER_TWO, outer_two))
    starts = tuple(((inner, insides[n]), (outer, outsides[n])) for n in range(2))
    return stage(core, halves, jobs, starts, shape, True)


def solution(mesh):
    spec = P(None, "space", "chan", None)

    return jax.shard_map(
        per_device,
        mesh=mesh,
        in_specs=(spec, P(None, None, "chan"), P("chan"), spec),
        out_specs=(spec, spec),
        check_vma=False,
    )
```

time: 67.3 us -> 67.5 us (level)
  local copies, waits for them, and re-layouts: 3.26 us -> 0.31 us
  starting transfers between devices: 30.7 us -> 32.7 us
  Pallas kernels: 9.93 us -> 11.1 us
    unnamed x12 -> x16, local copies, waits for them, and re-layouts: 3.26 us -> 0.31 us
    ppermute x11, starting transfers between devices: 16.4 us -> 18.7 us  [shifted(): lax.ppermute(x, 'chan', [(i, (i + steps) % count) for i in range(count)])]
    pallas_call x3 -> x2, Pallas kernels: 1.11 us -> 3.39 us  [the longest x1 2.96 us: prologue(): pl.pallas_call(body, out_shape=(*[two] * 4, jax.ShapeDtypeStruct((outs, c...]
    pallas_call x2 -> x3, Pallas kernels: 8.59 us -> 7.48 us  [stage(): pl.pallas_call(body, out_shape=(out, out), in_specs=[SMEM, *[VMEM] * (len...]
  transfers between devices with their start and end apart: 17 -> 17, of which waited for: 3 -> 6; matrix products, arithmetic and copies ran while one was open for 0% -> 0% of each run, Pallas kernels for 8% -> 11%
where the time goes in v4:
time: 67.5 us; the launch traced here: 67.2 us
  starting transfers between devices  32.7 us (48%)
  waiting for transfers between devices  22.2 us (33%)
  Pallas kernels  11.1 us (16%)
  between operations  0.99 us (1%)
    ppermute x11, starting transfers between devices, shifted(): lax.ppermute(x, 'chan', [(i, (i + steps) % count) for i in range(count)])  18.7 us
    ppermute x11, waiting for transfers between devices, shifted(): lax.ppermute(x, 'chan', [(i, (i + steps) % count) for i in range(count)])  16.5 us
    ppermute x3, starting transfers between devices, swapped_rows(): off_chip = lax.ppermute(off_chip, 'space', far)  13.8 us
    pallas_call x3, Pallas kernels, stage(): pl.pallas_call(body, out_shape=(out, out), in_specs=[SMEM, *[VMEM] * (len...  7.48 us
    ppermute x3, waiting for transfers between devices, swapped_rows(): off_chip = lax.ppermute(off_chip, 'space', far)  5.72 us
    pallas_call x1, Pallas kernels, prologue(): pl.pallas_call(body, out_shape=(*[two] * 4, jax.ShapeDtypeStruct((outs, c...  2.96 us
  transfers between devices with their start and end apart: 17, of which 6 were waited for; matrix products, arithmetic and copies ran while one was open for 0% of the time, Pallas kernels for 11%

profile of v4, /device:TPU:24, one launch (start us, length us, event | category | flops | bytes accessed | tf_op | source)
XLA Modules:
  0.0 67.2 jit_solution(14281759889832447196)
XLA Ops:
  0.6 1.6 %collective-permute-start = (bf16[16,4,32,128]{3,2,1,0:T(8,128)(2,1)}, bf16[16,4,32,128]{3,2,1,0:T(8,128)(2,1)S(1)}, u32[]{:S(2)}, u32[]{:S(2)}) collective-permute-start(bf16[16,4,32,128]{3,2,1,0:T(8,128)(2,1)} %refs_1_.3), channel_id=1, source_target_pairs={{0,1},{1,2},{2,3},{3,0},{4,5},{5,6},{6,7},{7,4},{8,9},{9,10},{10,1... | collective-permute-start | bytes 1572872 | tf_op jit(solution)/shard_map/ppermute | solution.py:23
  2.2 1.7 %collective-permute-start.1 = (bf16[16,4,32,128]{3,2,1,0:T(8,128)(2,1)}, bf16[16,4,32,128]{3,2,1,0:T(8,128)(2,1)S(1)}, u32[]{:S(2)}, u32[]{:S(2)}) collective-permute-start(bf16[16,4,32,128]{3,2,1,0:T(8,128)(2,1)} %refs_2_.3), channel_id=1, source_target_pairs={{0,3},{1,0},{2,1},{3,2},{4,7},{5,4},{6,5},{7,6},{8,11},{9,8},{10,9... | collective-permute-start | bytes 1572872 | tf_op jit(solution)/shard_map/ppermute | solution.py:23
  3.9 3.0 %prologue.1 = (bf16[2,16,32,128]{3,2,1,0:T(8,128)(2,1)}, bf16[2,16,32,128]{3,2,1,0:T(8,128)(2,1)}, bf16[2,16,32,128]{3,2,1,0:T(8,128)(2,1)}, bf16[2,16,32,128]{3...) custom-call(s32[1]{0:T(128)} %bitcast.core_ref, ...), custom_call_target="tpu_custom_call" | custom-call | tf_op jit(solution)/shard_map/prologue/pallas_call | solution.py:117
  6.9 1.5 %collective-permute-start.2 = (bf16[2,16,32,128]{3,2,1,0:T(8,128)(2,1)}, bf16[2,16,32,128]{3,2,1,0:T(8,128)(2,1)S(1)}, u32[]{:S(2)}, u32[]{:S(2)}) collective-permute-start(bf16[2,16,32,128]{3,2,1,0:T(8,128)(2,1)} %get-tuple-element.31), channel_id=1, source_target_pairs={{0,3},{1,0},{2,1},{3,2},{4,7},{5,4},{6,5},{7,6},{8,11},{9,8},{10,9... | collective-permute-start | bytes 786440 | tf_op jit(solution)/shard_map/ppermute | solution.py:23
  8.5 0.5 collective-permute-start.4
  8.9 2.8 %collective-permute-start.12 = (bf16[7,32,128]{2,1,0:T(8,128)(2,1)}, bf16[7,32,128]{2,1,0:T(8,128)(2,1)S(1)}, u32[]{:S(2)}, u32[]{:S(2)}) collective-permute-start(bf16[7,32,128]{2,1,0:T(8,128)(2,1)} %get-tuple-element.42), channel_id=1, source_target_pairs={{0,3},{1,0},{2,1},{3,2},{4,7},{5,4},{6,5},{7,6},{8,11},{9,8},{10,9... | collective-permute-start | bytes 172040 | tf_op jit(solution)/shard_map/ppermute | solution.py:23
  11.7 5.2 %collective-permute-done.vn.refs_0_ = bf16[16,4,32,128]{3,2,1,0:T(8,128)(2,1)S(1)} collective-permute-done((bf16[16,4,32,128]{3,2,1,0:T(8,128)(2,1)}, bf16[16,4,32,128]{3,2,1,0:T(8,128)(2,1)S(1)}, u32[]{:S(2)}, u32[]{:S(2)}) %collective-permute-start) | collective-permute-done | bytes 524320 | tf_op jit(solution)/shard_map/ppermute | solution.py:23
  17.4 1.6 %collective-permute-start.7 = (bf16[2,16,32,128]{3,2,1,0:T(8,128)(2,1)S(1)}, bf16[2,16,32,128]{3,2,1,0:T(8,128)(2,1)S(1)}, u32[]{:S(2)}, u32[]{:S(2)}) collective-permute-start(bf16[2,16,32,128]{3,2,1,0:T(8,128)(2,1)S(1)} %get-tuple-element.36), channel_id=1, source_target_pairs={{0,1},{1,2},{2,3},{3,0},{4,5},{5,6},{6,7},{7,4},{8,9},{9,10},{10,1... | collective-permute-start | bytes 786440 | tf_op jit(solution)/shard_map/ppermute | solution.py:23
  18.9 3.1 %collective-permute-done.2.refs_2_.refs_8_.refs_4_ = bf16[2,16,32,128]{3,2,1,0:T(8,128)(2,1)S(1)} collective-permute-done((bf16[2,16,32,128]{3,2,1,0:T(8,128)(2,1)}, bf16[2,16,32,128]{3,2,1,0:T(8,128)(2,1)S(1)}, u32[]{:S(2)}, u32[]{:S(2)}) %collective-permute-start.2) | collective-permute-done | bytes 262176 | tf_op jit(solution)/shard_map/ppermute | solution.py:23
  22.2 3.0 %collective-permute-start.9 = (bf16[2,16,32,128]{3,2,1,0:T(8,128)(2,1)S(1)}, bf16[2,16,32,128]{3,2,1,0:T(8,128)(2,1)S(1)}, u32[]{:S(2)}, u32[]{:S(2)}) collective-permute-start(bf16[2,16,32,128]{3,2,1,0:T(8,128)(2,1)S(1)} %get-tuple-element.38), channel_id=1, source_target_pairs={{0,3},{1,0},{2,1},{3,2},{4,7},{5,4},{6,5},{7,6},{8,11},{9,8},{10,9... | collective-permute-start | bytes 786440 | tf_op jit(solution)/shard_map/ppermute | solution.py:23
  25.2 0.6 collective-permute-start.13
  25.8 5.1 %collective-permute-done.13.refs_2_ = bf16[7,32,128]{2,1,0:T(8,128)(2,1)S(1)} collective-permute-done((bf16[7,32,128]{2,1,0:T(8,128)(2,1)S(1)}, bf16[7,32,128]{2,1,0:T(8,128)(2,1)S(1)}, u32[]{:S(2)}, u32[]{:S(2)}) %collective-permute-start.13) | collective-permute-done | bytes 57376 | tf_op jit(solution)/shard_map/ppermute | solution.py:23
  30.9 3.3 %collective-permute-start.14 = (bf16[7,32,128]{2,1,0:T(8,128)(2,1)S(1)}, bf16[7,32,128]{2,1,0:T(8,128)(2,1)S(1)}, u32[]{:S(2)}, u32[]{:S(2)}) collective-permute-start(bf16[7,32,128]{2,1,0:T(8,128)(2,1)S(1)} %copy-done.6), channel_id=1, source_target_pairs={{0,1},{1,2},{2,3},{3,0},{4,5},{5,6},{6,7},{7,4},{8,9},{9,10},{10,1... | collective-permute-start | bytes 172040 | tf_op jit(solution)/shard_map/ppermute | solution.py:23
  34.3 2.8 %collective-permute-done.14.refs_3_ = bf16[7,32,128]{2,1,0:T(8,128)(2,1)S(1)} collective-permute-done((bf16[7,32,128]{2,1,0:T(8,128)(2,1)S(1)}, bf16[7,32,128]{2,1,0:T(8,128)(2,1)S(1)}, u32[]{:S(2)}, u32[]{:S(2)}) %collective-permute-start.14) | collective-permute-done | bytes 57376 | tf_op jit(solution)/shard_map/ppermute | solution.py:23
  37.1 6.1 %collective-permute-start.6 = (bf16[4,16,32,128]{3,2,1,0:T(8,128)(2,1)S(1)}, bf16[4,16,32,128]{3,2,1,0:T(8,128)(2,1)S(1)}, u32[]{:S(2)}, u32[]{:S(2)}) collective-permute-start(bf16[4,16,32,128]{3,2,1,0:T(8,128)(2,1)S(1)} %get-tuple-element.35), channel_id=1, source_target_pairs={{4,8},{8,4},{12,16},{16,12},{20,24},{24,20},{28,32},{32,28},{36,40... | collective-permute-start | bytes 1572872 | tf_op jit(solution)/shard_map/ppermute | solution.py:30
  43.2 1.9 %collective-permute-start.16 = (bf16[2,16,32,128]{3,2,1,0:T(8,128)(2,1)S(1)}, bf16[2,16,32,128]{3,2,1,0:T(8,128)(2,1)S(1)}, u32[]{:S(2)}, u32[]{:S(2)}) collective-permute-start(bf16[2,16,32,128]{3,2,1,0:T(8,128)(2,1)S(1)} %copy-done.5), channel_id=1, source_target_pairs={{4,8},{8,4},{12,16},{16,12},{20,24},{24,20},{28,32},{32,28},{36,40... | collective-permute-start | bytes 786440 | tf_op jit(solution)/shard_map/ppermute | solution.py:30
  45.2 1.8 %collective-permute-start.3 = (bf16[4,16,32,128]{3,2,1,0:T(8,128)(2,1)S(1)}, bf16[4,16,32,128]{3,2,1,0:T(8,128)(2,1)S(1)}, u32[]{:S(2)}, u32[]{:S(2)}) collective-permute-start(bf16[4,16,32,128]{3,2,1,0:T(8,128)(2,1)S(1)} %get-tuple-element.32), channel_id=1, source_target_pairs={{0,3},{1,0},{2,1},{3,2},{4,7},{5,4},{6,5},{7,6},{8,11},{9,8},{10,9... | collective-permute-start | bytes 1572872 | tf_op jit(solution)/shard_map/ppermute | solution.py:23
  47.0 0.3 collective-permute-start.8
  47.3 5.7 %collective-permute-done.16.refs_5_ = bf16[2,16,32,128]{3,2,1,0:T(8,128)(2,1)S(1)} collective-permute-done((bf16[2,16,32,128]{3,2,1,0:T(8,128)(2,1)S(1)}, bf16[2,16,32,128]{3,2,1,0:T(8,128)(2,1)S(1)}, u32[]{:S(2)}, u32[]{:S(2)}) %collective-permute-start.16) | collective-permute-done | bytes 262176 | tf_op jit(solution)/shard_map/ppermute | solution.py:30
  53.0 5.8 %collective-permute-start.11 = (bf16[2,16,32,128]{3,2,1,0:T(8,128)(2,1)S(1)}, bf16[2,16,32,128]{3,2,1,0:T(8,128)(2,1)S(1)}, u32[]{:S(2)}, u32[]{:S(2)}) collective-permute-start(bf16[2,16,32,128]{3,2,1,0:T(8,128)(2,1)S(1)} %get-tuple-element.40), channel_id=1, source_target_pairs={{4,8},{8,4},{12,16},{16,12},{20,24},{24,20},{28,32},{32,28},{36,40... | collective-permute-start | bytes 786440 | tf_op jit(solution)/shard_map/ppermute | solution.py:30
  58.8 0.4 weights.1
  59.5 1.5 %shard_map.61 = (f32[16,2,32,128]{3,2,1,0:T(8,128)S(1)}, f32[16,2,32,128]{3,2,1,0:T(8,128)S(1)}) custom-call(s32[1]{0:T(128)} %bitcast.core_ref, bf16[16,4,32,128]{3,2,1,0:T(8,128)(2,1)S(1)} %collective-permute-done.vn.refs_0_, bf16[16,4,32,128]{3,2,1,0:T(8,128)(2,1)S(1)} %copy-done, bf16[16,4,32,128]{3,2,1,0:T(8,128)(2,1)S(1)} %copy-done.1, ...), custom_call_target="tpu_custom_call" | custom-call | flops 805306368 | bytes 6291456 | tf_op jit(solution)/shard_map/pallas_call | solution.py:300
  61.0 2.1 %shard_map.62 = (f32[16,2,32,128]{3,2,1,0:T(8,128)S(1)}, f32[16,2,32,128]{3,2,1,0:T(8,128)S(1)}) custom-call(s32[1]{0:T(128)} %bitcast.core_ref, bf16[16,4,32,128]{3,2,1,0:T(8,128)(2,1)S(1)} %collective-permute-done.vn.refs_0_, bf16[4,16,32,128]{3,2,1,0:T(8,128)(2,1)S(1)} %collective-permute-done.5.refs_1_.refs_6_, ...), custom_call_target="tpu_custom_call" | custom-call | flops 1207959552 | bytes 6291456 | tf_op jit(solution)/shard_map/pallas_call | solution.py:300
  63.2 3.9 %shard_map.63 = (bf16[16,4,32,128]{3,2,1,0:T(8,128)(2,1)}, bf16[16,4,32,128]{3,2,1,0:T(8,128)(2,1)}) custom-call(s32[1]{0:T(128)} %bitcast.core_ref, bf16[16,4,32,128]{3,2,1,0:T(8,128)(2,1)S(1)} %collective-permute-done.vn.refs_0_, bf16[16,4,32,128]{3,2,1,0:T(8,128)(2,1)S(1)} %copy-done, bf16[16,4,32,128]{3,2,1,0:T(8,128)(2,1)S(1)} %copy-done.1, ...), custom_call_target="tpu_custom_call" | custom-call | flops 1610612736 | bytes 6291456 | tf_op jit(solution)/shard_map/pallas_call | solution.py:300
  (34 shorter events, 0.9 us)
Async XLA Ops:
  0.6 16.3 %collective-permute-start = (bf16[16,4,32,128]{3,2,1,0:T(8,128)(2,1)}, bf16[16,4,32,128]{3,2,1,0:T(8,128)(2,1)S(1)}, u32[]{:S(2)}, u32[]{:S(2)}) collective-permute-start(bf16[16,4,32,128]{3,2,1,0:T(8,128)(2,1)} %refs_1_.3), channel_id=1, source_target_pairs={{0,1},{1,2},{2,3},{3,0},{4,5},{5,6},{6,7},{7,4},{8,9},{9,10},{10,1... | collective-permute-start | bytes 1572872 | tf_op jit(solution)/shard_map/ppermute | solution.py:23
  2.2 15.0 %collective-permute-start.1 = (bf16[16,4,32,128]{3,2,1,0:T(8,128)(2,1)}, bf16[16,4,32,128]{3,2,1,0:T(8,128)(2,1)S(1)}, u32[]{:S(2)}, u32[]{:S(2)}) collective-permute-start(bf16[16,4,32,128]{3,2,1,0:T(8,128)(2,1)} %refs_2_.3), channel_id=1, source_target_pairs={{0,3},{1,0},{2,1},{3,2},{4,7},{5,4},{6,5},{7,6},{8,11},{9,8},{10,9... | collective-permute-start | bytes 1572872 | tf_op jit(solution)/shard_map/ppermute | solution.py:23
  3.9 13.3 %copy-start = (bf16[16,4,32,128]{3,2,1,0:T(8,128)(2,1)S(1)}, bf16[16,4,32,128]{3,2,1,0:T(8,128)(2,1)}, u32[]{:S(2)}) copy-start(bf16[16,4,32,128]{3,2,1,0:T(8,128)(2,1)} %refs_1_.3) | copy-start | bytes 1572868
  3.9 13.3 %copy-start.1 = (bf16[16,4,32,128]{3,2,1,0:T(8,128)(2,1)S(1)}, bf16[16,4,32,128]{3,2,1,0:T(8,128)(2,1)}, u32[]{:S(2)}) copy-start(bf16[16,4,32,128]{3,2,1,0:T(8,128)(2,1)} %refs_2_.3) | copy-start | bytes 1572868
  6.9 15.1 %collective-permute-start.2 = (bf16[2,16,32,128]{3,2,1,0:T(8,128)(2,1)}, bf16[2,16,32,128]{3,2,1,0:T(8,128)(2,1)S(1)}, u32[]{:S(2)}, u32[]{:S(2)}) collective-permute-start(bf16[2,16,32,128]{3,2,1,0:T(8,128)(2,1)} %get-tuple-element.31), channel_id=1, source_target_pairs={{0,3},{1,0},{2,1},{3,2},{4,7},{5,4},{6,5},{7,6},{8,11},{9,8},{10,9... | collective-permute-start | bytes 786440 | tf_op jit(solution)/shard_map/ppermute | solution.py:23
  8.5 13.6 %collective-permute-start.4 = (bf16[2,16,32,128]{3,2,1,0:T(8,128)(2,1)}, bf16[2,16,32,128]{3,2,1,0:T(8,128)(2,1)S(1)}, u32[]{:S(2)}, u32[]{:S(2)}) collective-permute-start(bf16[2,16,32,128]{3,2,1,0:T(8,128)(2,1)} %get-tuple-element.33), channel_id=1, source_target_pairs={{0,1},{1,2},{2,3},{3,0},{4,5},{5,6},{6,7},{7,4},{8,9},{9,10},{10,1... | collective-permute-start | bytes 786440 | tf_op jit(solution)/shard_map/ppermute | solution.py:23
  8.9 16.3 %collective-permute-start.12 = (bf16[7,32,128]{2,1,0:T(8,128)(2,1)}, bf16[7,32,128]{2,1,0:T(8,128)(2,1)S(1)}, u32[]{:S(2)}, u32[]{:S(2)}) collective-permute-start(bf16[7,32,128]{2,1,0:T(8,128)(2,1)} %get-tuple-element.42), channel_id=1, source_target_pairs={{0,3},{1,0},{2,1},{3,2},{4,7},{5,4},{6,5},{7,6},{8,11},{9,8},{10,9... | collective-permute-start | bytes 172040 | tf_op jit(solution)/shard_map/ppermute | solution.py:23
  16.9 26.3 %collective-permute-start.15 = (bf16[2,16,32,128]{3,2,1,0:T(8,128)(2,1)}, bf16[2,16,32,128]{3,2,1,0:T(8,128)(2,1)S(1)}, u32[]{:S(2)}, u32[]{:S(2)}) collective-permute-start(bf16[2,16,32,128]{3,2,1,0:T(8,128)(2,1)} %get-tuple-element.53), channel_id=1, source_target_pairs={{0,4},{4,0},{8,12},{12,8},{16,20},{20,16},{24,28},{28,24},{32,36},... | collective-permute-start | bytes 786440 | tf_op jit(solution)/shard_map/ppermute | solution.py:31
  17.3 7.9 %copy-start.7 = (bf16[7,32,128]{2,1,0:T(8,128)(2,1)S(1)}, bf16[7,32,128]{2,1,0:T(8,128)(2,1)}, u32[]{:S(2)}) copy-start(bf16[7,32,128]{2,1,0:T(8,128)(2,1)} %get-tuple-element.43) | copy-start | bytes 172036
  17.3 13.6 %copy-start.6 = (bf16[7,32,128]{2,1,0:T(8,128)(2,1)S(1)}, bf16[7,32,128]{2,1,0:T(8,128)(2,1)}, u32[]{:S(2)}) copy-start(bf16[7,32,128]{2,1,0:T(8,128)(2,1)} %get-tuple-element.44) | copy-start | bytes 172036
  17.3 25.9 %copy-start.5 = (bf16[2,16,32,128]{3,2,1,0:T(8,128)(2,1)S(1)}, bf16[2,16,32,128]{3,2,1,0:T(8,128)(2,1)}, u32[]{:S(2)}) copy-start(bf16[2,16,32,128]{3,2,1,0:T(8,128)(2,1)} %get-tuple-element.54) | copy-start | bytes 786436
  17.4 27.8 %collective-permute-start.7 = (bf16[2,16,32,128]{3,2,1,0:T(8,128)(2,1)S(1)}, bf16[2,16,32,128]{3,2,1,0:T(8,128)(2,1)S(1)}, u32[]{:S(2)}, u32[]{:S(2)}) collective-permute-start(bf16[2,16,32,128]{3,2,1,0:T(8,128)(2,1)S(1)} %get-tuple-element.36), channel_id=1, source_target_pairs={{0,1},{1,2},{2,3},{3,0},{4,5},{5,6},{6,7},{7,4},{8,9},{9,10},{10,1... | collective-permute-start | bytes 786440 | tf_op jit(solution)/shard_map/ppermute | solution.py:23
  22.1 30.9 %collective-permute-start.5 = (bf16[4,16,32,128]{3,2,1,0:T(8,128)(2,1)S(1)}, bf16[4,16,32,128]{3,2,1,0:T(8,128)(2,1)S(1)}, u32[]{:S(2)}, u32[]{:S(2)}) collective-permute-start(bf16[4,16,32,128]{3,2,1,0:T(8,128)(2,1)S(1)} %get-tuple-element.34), channel_id=1, source_target_pairs={{0,4},{4,0},{8,12},{12,8},{16,20},{20,16},{24,28},{28,24},{32,36},... | collective-permute-start | bytes 1572872 | tf_op jit(solution)/shard_map/ppermute | solution.py:31
  22.2 24.8 %collective-permute-start.9 = (bf16[2,16,32,128]{3,2,1,0:T(8,128)(2,1)S(1)}, bf16[2,16,32,128]{3,2,1,0:T(8,128)(2,1)S(1)}, u32[]{:S(2)}, u32[]{:S(2)}) collective-permute-start(bf16[2,16,32,128]{3,2,1,0:T(8,128)(2,1)S(1)} %get-tuple-element.38), channel_id=1, source_target_pairs={{0,3},{1,0},{2,1},{3,2},{4,7},{5,4},{6,5},{7,6},{8,11},{9,8},{10,9... | collective-permute-start | bytes 786440 | tf_op jit(solution)/shard_map/ppermute | solution.py:23
  25.2 5.7 %collective-permute-start.13 = (bf16[7,32,128]{2,1,0:T(8,128)(2,1)S(1)}, bf16[7,32,128]{2,1,0:T(8,128)(2,1)S(1)}, u32[]{:S(2)}, u32[]{:S(2)}) collective-permute-start(bf16[7,32,128]{2,1,0:T(8,128)(2,1)S(1)} %copy-done.7), channel_id=1, source_target_pairs={{0,2},{1,3},{2,0},{3,1},{4,6},{5,7},{6,4},{7,5},{8,10},{9,11},{10,... | collective-permute-start | bytes 172040 | tf_op jit(solution)/shard_map/ppermute | solution.py:23
  30.9 6.1 %collective-permute-start.14 = (bf16[7,32,128]{2,1,0:T(8,128)(2,1)S(1)}, bf16[7,32,128]{2,1,0:T(8,128)(2,1)S(1)}, u32[]{:S(2)}, u32[]{:S(2)}) collective-permute-start(bf16[7,32,128]{2,1,0:T(8,128)(2,1)S(1)} %copy-done.6), channel_id=1, source_target_pairs={{0,1},{1,2},{2,3},{3,0},{4,5},{5,6},{6,7},{7,4},{8,9},{9,10},{10,1... | collective-permute-start | bytes 172040 | tf_op jit(solution)/shard_map/ppermute | solution.py:23
  37.1 24.0 %collective-permute-start.6 = (bf16[4,16,32,128]{3,2,1,0:T(8,128)(2,1)S(1)}, bf16[4,16,32,128]{3,2,1,0:T(8,128)(2,1)S(1)}, u32[]{:S(2)}, u32[]{:S(2)}) collective-permute-start(bf16[4,16,32,128]{3,2,1,0:T(8,128)(2,1)S(1)} %get-tuple-element.35), channel_id=1, source_target_pairs={{4,8},{8,4},{12,16},{16,12},{20,24},{24,20},{28,32},{32,28},{36,40... | collective-permute-start | bytes 1572872 | tf_op jit(solution)/shard_map/ppermute | solution.py:30
  43.2 9.8 %collective-permute-start.16 = (bf16[2,16,32,128]{3,2,1,0:T(8,128)(2,1)S(1)}, bf16[2,16,32,128]{3,2,1,0:T(8,128)(2,1)S(1)}, u32[]{:S(2)}, u32[]{:S(2)}) collective-permute-start(bf16[2,16,32,128]{3,2,1,0:T(8,128)(2,1)S(1)} %copy-done.5), channel_id=1, source_target_pairs={{4,8},{8,4},{12,16},{16,12},{20,24},{24,20},{28,32},{32,28},{36,40... | collective-permute-start | bytes 786440 | tf_op jit(solution)/shard_map/ppermute | solution.py:30
  45.2 18.0 %collective-permute-start.3 = (bf16[4,16,32,128]{3,2,1,0:T(8,128)(2,1)S(1)}, bf16[4,16,32,128]{3,2,1,0:T(8,128)(2,1)S(1)}, u32[]{:S(2)}, u32[]{:S(2)}) collective-permute-start(bf16[4,16,32,128]{3,2,1,0:T(8,128)(2,1)S(1)} %get-tuple-element.32), channel_id=1, source_target_pairs={{0,3},{1,0},{2,1},{3,2},{4,7},{5,4},{6,5},{7,6},{8,11},{9,8},{10,9... | collective-permute-start | bytes 1572872 | tf_op jit(solution)/shard_map/ppermute | solution.py:23
  47.0 11.8 %copy-start.2 = (bf16[27,128,32]{1,2,0:T(8,128)(2,1)S(1)}, bf16[27,128,32]{1,2,0:T(8,128)(2,1)}, u32[]{:S(2)}) copy-start(bf16[27,128,32]{1,2,0:T(8,128)(2,1)} %param.5) | copy-start | bytes 663556
  47.0 11.8 %copy-start.3 = (bf16[7,32,128]{2,1,0:T(8,128)(2,1)S(1)}, bf16[7,32,128]{2,1,0:T(8,128)(2,1)}, u32[]{:S(2)}) copy-start(bf16[7,32,128]{2,1,0:T(8,128)(2,1)} %get-tuple-element.41.refs_0_) | copy-start | bytes 172036
  47.0 16.2 %collective-permute-start.8 = (bf16[4,16,32,128]{3,2,1,0:T(8,128)(2,1)S(1)}, bf16[4,16,32,128]{3,2,1,0:T(8,128)(2,1)S(1)}, u32[]{:S(2)}, u32[]{:S(2)}) collective-permute-start(bf16[4,16,32,128]{3,2,1,0:T(8,128)(2,1)S(1)} %get-tuple-element.37), channel_id=1, source_target_pairs={{0,1},{1,2},{2,3},{3,0},{4,5},{5,6},{6,7},{7,4},{8,9},{9,10},{10,1... | collective-permute-start | bytes 1572872 | tf_op jit(solution)/shard_map/ppermute | solution.py:23
  53.0 10.1 %collective-permute-start.10 = (bf16[2,16,32,128]{3,2,1,0:T(8,128)(2,1)S(1)}, bf16[2,16,32,128]{3,2,1,0:T(8,128)(2,1)S(1)}, u32[]{:S(2)}, u32[]{:S(2)}) collective-permute-start(bf16[2,16,32,128]{3,2,1,0:T(8,128)(2,1)S(1)} %get-tuple-element.39), channel_id=1, source_target_pairs={{0,4},{4,0},{8,12},{12,8},{16,20},{20,16},{24,28},{28,24},{32,36},... | collective-permute-start | bytes 786440 | tf_op jit(solution)/shard_map/ppermute | solution.py:31
  53.0 10.1 %collective-permute-start.11 = (bf16[2,16,32,128]{3,2,1,0:T(8,128)(2,1)S(1)}, bf16[2,16,32,128]{3,2,1,0:T(8,128)(2,1)S(1)}, u32[]{:S(2)}, u32[]{:S(2)}) collective-permute-start(bf16[2,16,32,128]{3,2,1,0:T(8,128)(2,1)S(1)} %get-tuple-element.40), channel_id=1, source_target_pairs={{4,8},{8,4},{12,16},{16,12},{20,24},{24,20},{28,32},{32,28},{36,40... | collective-permute-start | bytes 786440 | tf_op jit(solution)/shard_map/ppermute | solution.py:30
  (1 other events, 0.7 us)

commit v5 on v4

--- a/solution.py
+++ b/solution.py
@@ -59,12 +59,16 @@
     )(volume, cotangent, vol_near, cot_near)
 
 
-def pack_rows(core, wholes, edges):
+def pack_rows(core, wholes, edges, pieces=()):
     planes, part, cells = edges[0].shape[1:]
     count = len(wholes) + len(edges)
+    more = 1 if pieces else 0
 
     def body(core_ref, *refs):
         *held, on_chip, off_chip = refs
+        for n, x in enumerate(held[count:]):
+            on_chip[count, pl.ds(n * x.shape[0], x.shape[0])] = x[...]
+        held = held[:count]
         side = jnp.where(core_ref[0] == 0, 1, 0)
         for n, x in enumerate(held):
             if n < len(wholes):
@@ -75,20 +79,21 @@
                 on_chip[n] = x[side]
                 off_chip[n] = x[1 - side]
 
-    out = jax.ShapeDtypeStruct((count, planes, part, cells), BF16)
-    return pl.pallas_call(
-        body,
-        out_shape=(out, out),
-        in_specs=[SMEM, *[VMEM] * count],
+    return pl.pallas_call(
+        body,
+        out_shape=tuple(
+            jax.ShapeDtypeStruct((n, planes, part, cells), BF16) for n in (count + more, count)
+        ),
+        in_specs=[SMEM, *[VMEM] * (count + len(pieces))],
         out_specs=[VMEM] * 2,
         compiler_params=pltpu.CompilerParams(vmem_limit_bytes=8 * MIB),
-    )(core, *wholes, *edges)
+    )(core, *wholes, *edges, *pieces)
 
 
 def prologue(core, place, volume, cotangent, own, bias, size):
     planes, rows, part, cells = volume.shape
     taps, outs, chans = own.shape
-    groups = -(-taps // size)
+    groups = -(-taps // (2 * size))
 
     def body(core_ref, place_ref, v, c, own_ref, bias_ref, *out_refs):
         ev, ec, on_chip, off_chip, wide_ref, *send_refs = out_refs
@@ -103,12 +108,12 @@
         column = jnp.sum(jnp.where(same, bias_ref[...], 0.0), axis=1, keepdims=True)
         wide_ref[...] = jnp.broadcast_to(column, wide_ref.shape)
         turn = lax.rem(size - place_ref[0], size) * part
-        empty = jnp.zeros((outs, chans), jnp.float32)
+        top = taps - 1 - core_ref[0] * (groups * size)
         for g in range(groups):
-            quad = [
-                pltpu.roll(own_ref[taps - 1 - t].astype(jnp.float32), turn, 1) if t < taps else empty
-                for t in range(g * size, (g + 1) * size)
-            ]
+            quad = []
+            for k in range(g * size, (g + 1) * size):
+                tile = own_ref[jnp.maximum(top - k, 0)].astype(jnp.float32)
+                quad.append(pltpu.roll(jnp.where(top >= k, tile, 0.0), turn, 1))
             for j in range(size):
                 pieces = [q[:, j * part : (j + 1) * part] for q in quad]
                 send_refs[j][g] = jnp.concatenate(pieces, axis=1).astype(BF16)
@@ -128,13 +133,15 @@
     )(core, place, volume, cotangent, own, bias.reshape(1, outs))
 
 
-def weights(place, own, received, layouts):
+def weights(core, place, own, received, others, layouts):
     taps, outs, chans = own.shape
     size, groups = len(received), received[0].shape[0]
     part = chans // size
     half = chans // 2
 
-    def body(place_ref, own_ref, *refs):
+    last = others.shape[0] - 1
+
+    def body(core_ref, place_ref, own_ref, others_ref, *refs):
         got_refs = refs[:size]
         table_refs = refs[size:]
         turn = lax.rem(size - place_ref[0] + 1, size) * part
@@ -158,9 +165,12 @@
         for n, chunks in enumerate(layouts):
             put(table_refs[2 * n], chunks, tiles)
         tiles = []
-        for g in range(groups):
-            tile = jnp.concatenate([got[g] for got in got_refs], axis=0)
-            tile = tile.astype(jnp.float32).T
+        for g in range(2 * groups):
+            at = g % groups
+            mine = jnp.concatenate([got[at] for got in got_refs], axis=0).astype(jnp.float32)
+            theirs = [others_ref[last, d * groups + at] for d in range(size)]
+            theirs = jnp.concatenate(theirs, axis=0).astype(jnp.float32)
+            tile = jnp.where(core_ref[0] == g // groups, mine, theirs).T
             tiles += [tile[t * part : (t + 1) * part] for t in range(size)]
         for n, chunks in enumerate(layouts):
             put(table_refs[2 * n + 1], chunks, tiles)
@@ -169,11 +179,11 @@
     return pl.pallas_call(
         body,
         out_shape=tuple(shape for shape in shapes for _ in range(2)),
-        in_specs=[SMEM, *[VMEM] * (size + 1)],
+        in_specs=[SMEM, SMEM, *[VMEM] * (size + 2)],
         out_specs=[VMEM] * (2 * len(layouts)),
         compiler_params=pltpu.CompilerParams(vmem_limit_bytes=8 * MIB),
         name="weights",
-    )(place, own, *received)
+    )(core, place, own, others, *received)
 
 
 def stage(core, halves, jobs, starts, shape, final):
@@ -332,10 +342,10 @@
     vol_edge, cot_edge, mid_up, mid_down = pack_forward(volume, cotangent, vol_left, cot_right)
     vol_edge, cot_edge = shifted(vol_edge, 1), shifted(cot_edge, -1)
     mid_up, mid_down = shifted(mid_up, 1), shifted(mid_down, -1)
-    near = pack_rows(core, (vol_left, cot_right), (vol_right_edge, cot_left_edge))
+    near = pack_rows(core, (vol_left, cot_right), (vol_right_edge, cot_left_edge), received)
     near = swapped_rows(*near)
 
-    tables = weights(me, own, received, (INNER_ONE, OUTER_ONE, INNER_TWO, OUTER_TWO))
+    tables = weights(core, me, own, received, near[0], (INNER_ONE, OUTER_ONE, INNER_TWO, OUTER_TWO))
     inner_one, outer_one, inner_two, outer_two = (tables[n : n + 2] for n in range(0, 8, 2))
 
     far = pack_rows(core, (), (vol_edge, cot_edge))

time: 67.5 us -> 69.9 us (1.036)
  local copies, waits for them, and re-layouts: 0.31 us -> 1.86 us
  waiting for transfers between devices: 22.2 us -> 23.3 us
    unnamed x16, local copies, waits for them, and re-layouts: 0.31 us -> 1.86 us
    ppermute x3, starting transfers between devices: 13.8 us -> 15 us  [swapped_rows(): off_chip = lax.ppermute(off_chip, 'space', far)]
    ppermute x11, waiting for transfers between devices: 16.5 us -> 17.6 us  [shifted(): lax.ppermute(x, 'chan', [(i, (i + steps) % count) for i in range(count)])]
    ppermute x11, starting transfers between devices: 18.7 us -> 17.7 us  [shifted(): lax.ppermute(x, 'chan', [(i, (i + steps) % count) for i in range(count)])]
  transfers between devices with their start and end apart: 17 -> 17, of which waited for: 6 -> 4; matrix products, arithmetic and copies ran while one was open for 0% -> 0% of each run, Pallas kernels for 11% -> 10%
where the time goes in v5:
time: 69.9 us; the launch traced here: 69.6 us
  starting transfers between devices  32.8 us (47%)
  waiting for transfers between devices  23.3 us (33%)
  Pallas kernels  10.6 us (15%)
  local copies, waits for them, and re-layouts  1.86 us (3%)
  between operations  0.99 us (1%)
    ppermute x11, starting transfers between devices, shifted(): lax.ppermute(x, 'chan', [(i, (i + steps) % count) for i in range(count)])  17.7 us
    ppermute x11, waiting for transfers between devices, shifted(): lax.ppermute(x, 'chan', [(i, (i + steps) % count) for i in range(count)])  17.6 us
    ppermute x3, starting transfers between devices, swapped_rows(): off_chip = lax.ppermute(off_chip, 'space', far)  15 us
    pallas_call x3, Pallas kernels, stage(): pl.pallas_call(body, out_shape=(out, out), in_specs=[SMEM, *[VMEM] * (len...  7.42 us
    ppermute x3, waiting for transfers between devices, swapped_rows(): off_chip = lax.ppermute(off_chip, 'space', far)  5.72 us
    pallas_call x1, Pallas kernels, prologue(): pl.pallas_call(body, out_shape=(*[two] * 4, jax.ShapeDtypeStruct((outs, c...  2.56 us
    unnamed x16, local copies, waits for them, and re-layouts  1.86 us
  transfers between devices with their start and end apart: 17, of which 4 were waited for; matrix products, arithmetic and copies ran while one was open for 0% of the time, Pallas kernels for 10%

profile of v5, /device:TPU:24, one launch (start us, length us, event | category | flops | bytes accessed | tf_op | source)
XLA Modules:
  0.0 69.6 jit_solution(14808722630358865325)
XLA Ops:
  0.6 1.6 %collective-permute-start = (bf16[16,4,32,128]{3,2,1,0:T(8,128)(2,1)}, bf16[16,4,32,128]{3,2,1,0:T(8,128)(2,1)S(1)}, u32[]{:S(2)}, u32[]{:S(2)}) collective-permute-start(bf16[16,4,32,128]{3,2,1,0:T(8,128)(2,1)} %refs_1_.3), channel_id=1, source_target_pairs={{0,1},{1,2},{2,3},{3,0},{4,5},{5,6},{6,7},{7,4},{8,9},{9,10},{10,1... | collective-permute-start | bytes 1572872 | tf_op jit(solution)/shard_map/ppermute | solution.py:23
  2.2 1.7 %collective-permute-start.1 = (bf16[16,4,32,128]{3,2,1,0:T(8,128)(2,1)}, bf16[16,4,32,128]{3,2,1,0:T(8,128)(2,1)S(1)}, u32[]{:S(2)}, u32[]{:S(2)}) collective-permute-start(bf16[16,4,32,128]{3,2,1,0:T(8,128)(2,1)} %refs_2_.3), channel_id=1, source_target_pairs={{0,3},{1,0},{2,1},{3,2},{4,7},{5,4},{6,5},{7,6},{8,11},{9,8},{10,9... | collective-permute-start | bytes 1572872 | tf_op jit(solution)/shard_map/ppermute | solution.py:23
  3.9 2.6 %prologue.1 = (bf16[2,16,32,128]{3,2,1,0:T(8,128)(2,1)}, bf16[2,16,32,128]{3,2,1,0:T(8,128)(2,1)}, bf16[2,16,32,128]{3,2,1,0:T(8,128)(2,1)}, bf16[2,16,32,128]{3...) custom-call(s32[1]{0:T(128)} %bitcast.core_ref, ...), custom_call_target="tpu_custom_call" | custom-call | tf_op jit(solution)/shard_map/prologue/pallas_call | solution.py:122
  6.5 1.6 %collective-permute-start.2 = (bf16[2,16,32,128]{3,2,1,0:T(8,128)(2,1)}, bf16[2,16,32,128]{3,2,1,0:T(8,128)(2,1)S(1)}, u32[]{:S(2)}, u32[]{:S(2)}) collective-permute-start(bf16[2,16,32,128]{3,2,1,0:T(8,128)(2,1)} %get-tuple-element.31), channel_id=1, source_target_pairs={{0,3},{1,0},{2,1},{3,2},{4,7},{5,4},{6,5},{7,6},{8,11},{9,8},{10,9... | collective-permute-start | bytes 786440 | tf_op jit(solution)/shard_map/ppermute | solution.py:23
  8.1 0.5 collective-permute-start.4
  8.5 2.8 %collective-permute-start.5 = (bf16[4,32,128]{2,1,0:T(8,128)(2,1)}, bf16[4,32,128]{2,1,0:T(8,128)(2,1)S(1)}, u32[]{:S(2)}, u32[]{:S(2)}) collective-permute-start(bf16[4,32,128]{2,1,0:T(8,128)(2,1)} %get-tuple-element.35), channel_id=1, source_target_pairs={{0,3},{1,0},{2,1},{3,2},{4,7},{5,4},{6,5},{7,6},{8,11},{9,8},{10,9... | collective-permute-start | bytes 98312 | tf_op jit(solution)/shard_map/ppermute | solution.py:23
  11.3 10.8 %collective-permute-done.5.refs_5_.refs_1_ = bf16[4,32,128]{2,1,0:T(8,128)(2,1)S(1)} collective-permute-done((bf16[4,32,128]{2,1,0:T(8,128)(2,1)}, bf16[4,32,128]{2,1,0:T(8,128)(2,1)S(1)}, u32[]{:S(2)}, u32[]{:S(2)}) %collective-permute-start.5) | collective-permute-done | bytes 32800 | tf_op jit(solution)/shard_map/ppermute | solution.py:23
  22.1 2.7 %collective-permute-start.6 = (bf16[4,32,128]{2,1,0:T(8,128)(2,1)}, bf16[4,32,128]{2,1,0:T(8,128)(2,1)S(1)}, u32[]{:S(2)}, u32[]{:S(2)}) collective-permute-start(bf16[4,32,128]{2,1,0:T(8,128)(2,1)} %get-tuple-element.36), channel_id=1, source_target_pairs={{0,2},{1,3},{2,0},{3,1},{4,6},{5,7},{6,4},{7,5},{8,10},{9,11},{10,... | collective-permute-start | bytes 98312 | tf_op jit(solution)/shard_map/ppermute | solution.py:23
  24.8 2.9 %collective-permute-done.6.refs_6_.refs_2_ = bf16[4,32,128]{2,1,0:T(8,128)(2,1)S(1)} collective-permute-done((bf16[4,32,128]{2,1,0:T(8,128)(2,1)}, bf16[4,32,128]{2,1,0:T(8,128)(2,1)S(1)}, u32[]{:S(2)}, u32[]{:S(2)}) %collective-permute-start.6) | collective-permute-done | bytes 32800 | tf_op jit(solution)/shard_map/ppermute | solution.py:23
  27.7 1.5 %collective-permute-start.7 = (bf16[4,32,128]{2,1,0:T(8,128)(2,1)}, bf16[4,32,128]{2,1,0:T(8,128)(2,1)S(1)}, u32[]{:S(2)}, u32[]{:S(2)}) collective-permute-start(bf16[4,32,128]{2,1,0:T(8,128)(2,1)} %get-tuple-element.37), channel_id=1, source_target_pairs={{0,1},{1,2},{2,3},{3,0},{4,5},{5,6},{6,7},{7,4},{8,9},{9,10},{10,1... | collective-permute-start | bytes 98312 | tf_op jit(solution)/shard_map/ppermute | solution.py:23
  29.2 3.8 %collective-permute-done.7.refs_7_.refs_3_ = bf16[4,32,128]{2,1,0:T(8,128)(2,1)S(1)} collective-permute-done((bf16[4,32,128]{2,1,0:T(8,128)(2,1)}, bf16[4,32,128]{2,1,0:T(8,128)(2,1)S(1)}, u32[]{:S(2)}, u32[]{:S(2)}) %collective-permute-start.7) | collective-permute-done | bytes 32800 | tf_op jit(solution)/shard_map/ppermute | solution.py:23
  33.1 0.7 %copy-done.3 = bf16[4,32,128]{2,1,0:T(8,128)(2,1)S(1)} copy-done((bf16[4,32,128]{2,1,0:T(8,128)(2,1)S(1)}, bf16[4,32,128]{2,1,0:T(8,128)(2,1)}, u32[]{:S(2)}) %copy-start.3) | copy-done | bytes 32792
  34.1 0.8 %copy-done.7 = bf16[2,16,32,128]{3,2,1,0:T(8,128)(2,1)S(1)} copy-done((bf16[2,16,32,128]{3,2,1,0:T(8,128)(2,1)S(1)}, bf16[2,16,32,128]{3,2,1,0:T(8,128)(2,1)}, u32[]{:S(2)}) %copy-start.7) | copy-done | bytes 262168
  35.6 3.0 %collective-permute-start.12 = (bf16[2,16,32,128]{3,2,1,0:T(8,128)(2,1)S(1)}, bf16[2,16,32,128]{3,2,1,0:T(8,128)(2,1)S(1)}, u32[]{:S(2)}, u32[]{:S(2)}) collective-permute-start(bf16[2,16,32,128]{3,2,1,0:T(8,128)(2,1)S(1)} %get-tuple-element.42), channel_id=1, source_target_pairs={{0,3},{1,0},{2,1},{3,2},{4,7},{5,4},{6,5},{7,6},{8,11},{9,8},{10,9... | collective-permute-start | bytes 786440 | tf_op jit(solution)/shard_map/ppermute | solution.py:23
  38.6 7.2 %collective-permute-start.9 = (bf16[4,16,32,128]{3,2,1,0:T(8,128)(2,1)S(1)}, bf16[4,16,32,128]{3,2,1,0:T(8,128)(2,1)S(1)}, u32[]{:S(2)}, u32[]{:S(2)}) collective-permute-start(bf16[4,16,32,128]{3,2,1,0:T(8,128)(2,1)S(1)} %get-tuple-element.39), channel_id=1, source_target_pairs={{4,8},{8,4},{12,16},{16,12},{20,24},{24,20},{28,32},{32,28},{36,40... | collective-permute-start | bytes 1572872 | tf_op jit(solution)/shard_map/ppermute | solution.py:30
  45.8 1.9 %collective-permute-start.16 = (bf16[2,16,32,128]{3,2,1,0:T(8,128)(2,1)S(1)}, bf16[2,16,32,128]{3,2,1,0:T(8,128)(2,1)S(1)}, u32[]{:S(2)}, u32[]{:S(2)}) collective-permute-start(bf16[2,16,32,128]{3,2,1,0:T(8,128)(2,1)S(1)} %copy-done.6), channel_id=1, source_target_pairs={{4,8},{8,4},{12,16},{16,12},{20,24},{24,20},{28,32},{32,28},{36,40... | collective-permute-start | bytes 786440 | tf_op jit(solution)/shard_map/ppermute | solution.py:30
  47.7 0.6 collective-permute-start.3
  48.3 1.5 %collective-permute-start.11 = (bf16[4,16,32,128]{3,2,1,0:T(8,128)(2,1)S(1)}, bf16[4,16,32,128]{3,2,1,0:T(8,128)(2,1)S(1)}, u32[]{:S(2)}, u32[]{:S(2)}) collective-permute-start(bf16[4,16,32,128]{3,2,1,0:T(8,128)(2,1)S(1)} %get-tuple-element.41), channel_id=1, source_target_pairs={{0,1},{1,2},{2,3},{3,0},{4,5},{5,6},{6,7},{7,4},{8,9},{9,10},{10,1... | collective-permute-start | bytes 1572872 | tf_op jit(solution)/shard_map/ppermute | solution.py:23
  49.9 5.7 %collective-permute-done.16.refs_5_ = bf16[2,16,32,128]{3,2,1,0:T(8,128)(2,1)S(1)} collective-permute-done((bf16[2,16,32,128]{3,2,1,0:T(8,128)(2,1)S(1)}, bf16[2,16,32,128]{3,2,1,0:T(8,128)(2,1)S(1)}, u32[]{:S(2)}, u32[]{:S(2)}) %collective-permute-start.16) | collective-permute-done | bytes 262176 | tf_op jit(solution)/shard_map/ppermute | solution.py:30
  55.6 5.9 %collective-permute-start.14 = (bf16[2,16,32,128]{3,2,1,0:T(8,128)(2,1)S(1)}, bf16[2,16,32,128]{3,2,1,0:T(8,128)(2,1)S(1)}, u32[]{:S(2)}, u32[]{:S(2)}) collective-permute-start(bf16[2,16,32,128]{3,2,1,0:T(8,128)(2,1)S(1)} %get-tuple-element.44), channel_id=1, source_target_pairs={{4,8},{8,4},{12,16},{16,12},{20,24},{24,20},{28,32},{32,28},{36,40... | collective-permute-start | bytes 786440 | tf_op jit(solution)/shard_map/ppermute | solution.py:30
  61.5 0.4 weights.1
  62.0 1.5 %shard_map.61 = (f32[16,2,32,128]{3,2,1,0:T(8,128)S(1)}, f32[16,2,32,128]{3,2,1,0:T(8,128)S(1)}) custom-call(s32[1]{0:T(128)} %bitcast.core_ref, bf16[16,4,32,128]{3,2,1,0:T(8,128)(2,1)S(1)} %collective-permute-done.vn.refs_0_, bf16[16,4,32,128]{3,2,1,0:T(8,128)(2,1)S(1)} %copy-done, bf16[16,4,32,128]{3,2,1,0:T(8,128)(2,1)S(1)} %copy-done.1, ...), custom_call_target="tpu_custom_call" | custom-call | flops 805306368 | bytes 6291456 | tf_op jit(solution)/shard_map/pallas_call | solution.py:310
  63.5 2.1 %shard_map.62 = (f32[16,2,32,128]{3,2,1,0:T(8,128)S(1)}, f32[16,2,32,128]{3,2,1,0:T(8,128)S(1)}) custom-call(s32[1]{0:T(128)} %bitcast.core_ref, bf16[16,4,32,128]{3,2,1,0:T(8,128)(2,1)S(1)} %collective-permute-done.vn.refs_0_, bf16[5,16,32,128]{3,2,1,0:T(8,128)(2,1)S(1)} %collective-permute-done.8.others_ref.refs_1_.refs_6_, ...), custom_call_target="tpu_custom_call" | custom-call | flops 1207959552 | bytes 6291456 | tf_op jit(solution)/shard_map/pallas_call | solution.py:310
  65.6 3.8 %shard_map.63 = (bf16[16,4,32,128]{3,2,1,0:T(8,128)(2,1)}, bf16[16,4,32,128]{3,2,1,0:T(8,128)(2,1)}) custom-call(s32[1]{0:T(128)} %bitcast.core_ref, bf16[16,4,32,128]{3,2,1,0:T(8,128)(2,1)S(1)} %collective-permute-done.vn.refs_0_, bf16[16,4,32,128]{3,2,1,0:T(8,128)(2,1)S(1)} %copy-done, bf16[16,4,32,128]{3,2,1,0:T(8,128)(2,1)S(1)} %copy-done.1, ...), custom_call_target="tpu_custom_call" | custom-call | flops 1610612736 | bytes 6291456 | tf_op jit(solution)/shard_map/pallas_call | solution.py:310
  (34 shorter events, 1.1 us)
Async XLA Ops:
  0.6 32.5 %collective-permute-start = (bf16[16,4,32,128]{3,2,1,0:T(8,128)(2,1)}, bf16[16,4,32,128]{3,2,1,0:T(8,128)(2,1)S(1)}, u32[]{:S(2)}, u32[]{:S(2)}) collective-permute-start(bf16[16,4,32,128]{3,2,1,0:T(8,128)(2,1)} %refs_1_.3), channel_id=1, source_target_pairs={{0,1},{1,2},{2,3},{3,0},{4,5},{5,6},{6,7},{7,4},{8,9},{9,10},{10,1... | collective-permute-start | bytes 1572872 | tf_op jit(solution)/shard_map/ppermute | solution.py:23
  2.2 30.9 %collective-permute-start.1 = (bf16[16,4,32,128]{3,2,1,0:T(8,128)(2,1)}, bf16[16,4,32,128]{3,2,1,0:T(8,128)(2,1)S(1)}, u32[]{:S(2)}, u32[]{:S(2)}) collective-permute-start(bf16[16,4,32,128]{3,2,1,0:T(8,128)(2,1)} %refs_2_.3), channel_id=1, source_target_pairs={{0,3},{1,0},{2,1},{3,2},{4,7},{5,4},{6,5},{7,6},{8,11},{9,8},{10,9... | collective-permute-start | bytes 1572872 | tf_op jit(solution)/shard_map/ppermute | solution.py:23
  6.5 26.6 %collective-permute-start.2 = (bf16[2,16,32,128]{3,2,1,0:T(8,128)(2,1)}, bf16[2,16,32,128]{3,2,1,0:T(8,128)(2,1)S(1)}, u32[]{:S(2)}, u32[]{:S(2)}) collective-permute-start(bf16[2,16,32,128]{3,2,1,0:T(8,128)(2,1)} %get-tuple-element.31), channel_id=1, source_target_pairs={{0,3},{1,0},{2,1},{3,2},{4,7},{5,4},{6,5},{7,6},{8,11},{9,8},{10,9... | collective-permute-start | bytes 786440 | tf_op jit(solution)/shard_map/ppermute | solution.py:23
  8.1 25.0 %collective-permute-start.4 = (bf16[2,16,32,128]{3,2,1,0:T(8,128)(2,1)}, bf16[2,16,32,128]{3,2,1,0:T(8,128)(2,1)S(1)}, u32[]{:S(2)}, u32[]{:S(2)}) collective-permute-start(bf16[2,16,32,128]{3,2,1,0:T(8,128)(2,1)} %get-tuple-element.33), channel_id=1, source_target_pairs={{0,1},{1,2},{2,3},{3,0},{4,5},{5,6},{6,7},{7,4},{8,9},{9,10},{10,1... | collective-permute-start | bytes 786440 | tf_op jit(solution)/shard_map/ppermute | solution.py:23
  8.5 13.6 %collective-permute-start.5 = (bf16[4,32,128]{2,1,0:T(8,128)(2,1)}, bf16[4,32,128]{2,1,0:T(8,128)(2,1)S(1)}, u32[]{:S(2)}, u32[]{:S(2)}) collective-permute-start(bf16[4,32,128]{2,1,0:T(8,128)(2,1)} %get-tuple-element.35), channel_id=1, source_target_pairs={{0,3},{1,0},{2,1},{3,2},{4,7},{5,4},{6,5},{7,6},{8,11},{9,8},{10,9... | collective-permute-start | bytes 98312 | tf_op jit(solution)/shard_map/ppermute | solution.py:23
  22.1 5.6 %collective-permute-start.6 = (bf16[4,32,128]{2,1,0:T(8,128)(2,1)}, bf16[4,32,128]{2,1,0:T(8,128)(2,1)S(1)}, u32[]{:S(2)}, u32[]{:S(2)}) collective-permute-start(bf16[4,32,128]{2,1,0:T(8,128)(2,1)} %get-tuple-element.36), channel_id=1, source_target_pairs={{0,2},{1,3},{2,0},{3,1},{4,6},{5,7},{6,4},{7,5},{8,10},{9,11},{10,... | collective-permute-start | bytes 98312 | tf_op jit(solution)/shard_map/ppermute | solution.py:23
  27.7 5.3 %collective-permute-start.7 = (bf16[4,32,128]{2,1,0:T(8,128)(2,1)}, bf16[4,32,128]{2,1,0:T(8,128)(2,1)S(1)}, u32[]{:S(2)}, u32[]{:S(2)}) collective-permute-start(bf16[4,32,128]{2,1,0:T(8,128)(2,1)} %get-tuple-element.37), channel_id=1, source_target_pairs={{0,1},{1,2},{2,3},{3,0},{4,5},{5,6},{6,7},{7,4},{8,9},{9,10},{10,1... | collective-permute-start | bytes 98312 | tf_op jit(solution)/shard_map/ppermute | solution.py:23
  33.9 0.9 %copy-start.7 = (bf16[2,16,32,128]{3,2,1,0:T(8,128)(2,1)S(1)}, bf16[2,16,32,128]{3,2,1,0:T(8,128)(2,1)}, u32[]{:S(2)}) copy-start(bf16[2,16,32,128]{3,2,1,0:T(8,128)(2,1)} %get-tuple-element.53) | copy-start | bytes 786436
  33.9 1.1 %copy-start = (bf16[16,4,32,128]{3,2,1,0:T(8,128)(2,1)S(1)}, bf16[16,4,32,128]{3,2,1,0:T(8,128)(2,1)}, u32[]{:S(2)}) copy-start(bf16[16,4,32,128]{3,2,1,0:T(8,128)(2,1)} %refs_1_.3) | copy-start | bytes 1572868
  33.9 1.3 %copy-start.1 = (bf16[16,4,32,128]{3,2,1,0:T(8,128)(2,1)S(1)}, bf16[16,4,32,128]{3,2,1,0:T(8,128)(2,1)}, u32[]{:S(2)}) copy-start(bf16[16,4,32,128]{3,2,1,0:T(8,128)(2,1)} %refs_2_.3) | copy-start | bytes 1572868
  34.0 21.6 %collective-permute-start.8 = (bf16[5,16,32,128]{3,2,1,0:T(8,128)(2,1)S(1)}, bf16[5,16,32,128]{3,2,1,0:T(8,128)(2,1)S(1)}, u32[]{:S(2)}, u32[]{:S(2)}) collective-permute-start(bf16[5,16,32,128]{3,2,1,0:T(8,128)(2,1)S(1)} %get-tuple-element.38), channel_id=1, source_target_pairs={{0,4},{4,0},{8,12},{12,8},{16,20},{20,16},{24,28},{28,24},{32,36},... | collective-permute-start | bytes 1966088 | tf_op jit(solution)/shard_map/ppermute | solution.py:31
  34.8 10.9 %copy-start.6 = (bf16[2,16,32,128]{3,2,1,0:T(8,128)(2,1)S(1)}, bf16[2,16,32,128]{3,2,1,0:T(8,128)(2,1)}, u32[]{:S(2)}) copy-start(bf16[2,16,32,128]{3,2,1,0:T(8,128)(2,1)} %get-tuple-element.54) | copy-start | bytes 786436
  34.8 10.9 %collective-permute-start.15 = (bf16[2,16,32,128]{3,2,1,0:T(8,128)(2,1)S(1)}, bf16[2,16,32,128]{3,2,1,0:T(8,128)(2,1)S(1)}, u32[]{:S(2)}, u32[]{:S(2)}) collective-permute-start(bf16[2,16,32,128]{3,2,1,0:T(8,128)(2,1)S(1)} %copy-done.7), channel_id=1, source_target_pairs={{0,4},{4,0},{8,12},{12,8},{16,20},{20,16},{24,28},{28,24},{32,36},... | collective-permute-start | bytes 786440 | tf_op jit(solution)/shard_map/ppermute | solution.py:31
  35.3 12.4 %collective-permute-start.10 = (bf16[2,16,32,128]{3,2,1,0:T(8,128)(2,1)S(1)}, bf16[2,16,32,128]{3,2,1,0:T(8,128)(2,1)S(1)}, u32[]{:S(2)}, u32[]{:S(2)}) collective-permute-start(bf16[2,16,32,128]{3,2,1,0:T(8,128)(2,1)S(1)} %get-tuple-element.40), channel_id=1, source_target_pairs={{0,1},{1,2},{2,3},{3,0},{4,5},{5,6},{6,7},{7,4},{8,9},{9,10},{10,1... | collective-permute-start | bytes 786440 | tf_op jit(solution)/shard_map/ppermute | solution.py:23
  35.6 12.7 %collective-permute-start.12 = (bf16[2,16,32,128]{3,2,1,0:T(8,128)(2,1)S(1)}, bf16[2,16,32,128]{3,2,1,0:T(8,128)(2,1)S(1)}, u32[]{:S(2)}, u32[]{:S(2)}) collective-permute-start(bf16[2,16,32,128]{3,2,1,0:T(8,128)(2,1)S(1)} %get-tuple-element.42), channel_id=1, source_target_pairs={{0,3},{1,0},{2,1},{3,2},{4,7},{5,4},{6,5},{7,6},{8,11},{9,8},{10,9... | collective-permute-start | bytes 786440 | tf_op jit(solution)/shard_map/ppermute | solution.py:23
  38.6 24.9 %collective-permute-start.9 = (bf16[4,16,32,128]{3,2,1,0:T(8,128)(2,1)S(1)}, bf16[4,16,32,128]{3,2,1,0:T(8,128)(2,1)S(1)}, u32[]{:S(2)}, u32[]{:S(2)}) collective-permute-start(bf16[4,16,32,128]{3,2,1,0:T(8,128)(2,1)S(1)} %get-tuple-element.39), channel_id=1, source_target_pairs={{4,8},{8,4},{12,16},{16,12},{20,24},{24,20},{28,32},{32,28},{36,40... | collective-permute-start | bytes 1572872 | tf_op jit(solution)/shard_map/ppermute | solution.py:30
  45.8 9.8 %collective-permute-start.16 = (bf16[2,16,32,128]{3,2,1,0:T(8,128)(2,1)S(1)}, bf16[2,16,32,128]{3,2,1,0:T(8,128)(2,1)S(1)}, u32[]{:S(2)}, u32[]{:S(2)}) collective-permute-start(bf16[2,16,32,128]{3,2,1,0:T(8,128)(2,1)S(1)} %copy-done.6), channel_id=1, source_target_pairs={{4,8},{8,4},{12,16},{16,12},{20,24},{24,20},{28,32},{32,28},{36,40... | collective-permute-start | bytes 786440 | tf_op jit(solution)/shard_map/ppermute | solution.py:30
  47.7 17.9 %collective-permute-start.3 = (bf16[4,16,32,128]{3,2,1,0:T(8,128)(2,1)S(1)}, bf16[4,16,32,128]{3,2,1,0:T(8,128)(2,1)S(1)}, u32[]{:S(2)}, u32[]{:S(2)}) collective-permute-start(bf16[4,16,32,128]{3,2,1,0:T(8,128)(2,1)S(1)} %get-tuple-element.32), channel_id=1, source_target_pairs={{0,3},{1,0},{2,1},{3,2},{4,7},{5,4},{6,5},{7,6},{8,11},{9,8},{10,9... | collective-permute-start | bytes 1572872 | tf_op jit(solution)/shard_map/ppermute | solution.py:23
  48.3 13.2 %copy-start.2 = (bf16[27,128,32]{1,2,0:T(8,128)(2,1)S(1)}, bf16[27,128,32]{1,2,0:T(8,128)(2,1)}, u32[]{:S(2)}) copy-start(bf16[27,128,32]{1,2,0:T(8,128)(2,1)} %param.5) | copy-start | bytes 663556
  48.3 13.2 %copy-start.4 = (bf16[4,32,128]{2,1,0:T(8,128)(2,1)S(1)}, bf16[4,32,128]{2,1,0:T(8,128)(2,1)}, u32[]{:S(2)}) copy-start(bf16[4,32,128]{2,1,0:T(8,128)(2,1)} %get-tuple-element.34.refs_4_.refs_0_) | copy-start | bytes 98308
  48.3 17.3 %collective-permute-start.11 = (bf16[4,16,32,128]{3,2,1,0:T(8,128)(2,1)S(1)}, bf16[4,16,32,128]{3,2,1,0:T(8,128)(2,1)S(1)}, u32[]{:S(2)}, u32[]{:S(2)}) collective-permute-start(bf16[4,16,32,128]{3,2,1,0:T(8,128)(2,1)S(1)} %get-tuple-element.41), channel_id=1, source_target_pairs={{0,1},{1,2},{2,3},{3,0},{4,5},{5,6},{6,7},{7,4},{8,9},{9,10},{10,1... | collective-permute-start | bytes 1572872 | tf_op jit(solution)/shard_map/ppermute | solution.py:23
  55.6 10.0 %collective-permute-start.13 = (bf16[2,16,32,128]{3,2,1,0:T(8,128)(2,1)S(1)}, bf16[2,16,32,128]{3,2,1,0:T(8,128)(2,1)S(1)}, u32[]{:S(2)}, u32[]{:S(2)}) collective-permute-start(bf16[2,16,32,128]{3,2,1,0:T(8,128)(2,1)S(1)} %get-tuple-element.43), channel_id=1, source_target_pairs={{0,4},{4,0},{8,12},{12,8},{16,20},{20,16},{24,28},{28,24},{32,36},... | collective-permute-start | bytes 786440 | tf_op jit(solution)/shard_map/ppermute | solution.py:31
  55.6 6.4 %copy-start.5 = (f32[32,128]{1,0:T(8,128)S(1)}, f32[32,128]{1,0:T(8,128)}, u32[]{:S(2)}) copy-start(f32[32,128]{1,0:T(8,128)} %get-tuple-element.51.refs_6_.refs_14_) | copy-start | bytes 49156
  55.6 10.0 %collective-permute-start.14 = (bf16[2,16,32,128]{3,2,1,0:T(8,128)(2,1)S(1)}, bf16[2,16,32,128]{3,2,1,0:T(8,128)(2,1)S(1)}, u32[]{:S(2)}, u32[]{:S(2)}) collective-permute-start(bf16[2,16,32,128]{3,2,1,0:T(8,128)(2,1)S(1)} %get-tuple-element.44), channel_id=1, source_target_pairs={{4,8},{8,4},{12,16},{16,12},{20,24},{24,20},{28,32},{32,28},{36,40... | collective-permute-start | bytes 786440 | tf_op jit(solution)/shard_map/ppermute | solution.py:30
  (1 other events, 0.8 us)

commit v6 on v5

--- a/solution.py
+++ b/solution.py
@@ -16,6 +16,7 @@
 INNER_TWO = (*[(1, at) for at in range(9)], (0, 8))
 OUTER_ONE = (*[(0, at) for at in range(9)], (1, 1), (1, 4), (1, 7))
 OUTER_TWO = tuple((1, at) for at in (0, 2, 3, 5, 6, 8))
+LAYOUTS = (INNER_ONE, OUTER_ONE, INNER_TWO, OUTER_TWO)
 
 
 def shifted(x, steps):
@@ -133,18 +134,17 @@
     )(core, place, volume, cotangent, own, bias.reshape(1, outs))
 
 
-def weights(core, place, own, received, others, layouts):
-    taps, outs, chans = own.shape
-    size, groups = len(received), received[0].shape[0]
+def weights_back(core, received, others, layouts):
+    size = len(received)
+    groups, outs, chans = received[0].shape
     part = chans // size
     half = chans // 2
 
     last = others.shape[0] - 1
 
-    def body(core_ref, place_ref, own_ref, others_ref, *refs):
+    def body(core_ref, others_ref, *refs):
         got_refs = refs[:size]
         table_refs = refs[size:]
-        turn = lax.rem(size - place_ref[0] + 1, size) * part
         low = lax.broadcasted_iota(jnp.int32, (outs, chans), 1) < half
 
         def put(ref, chunks, tiles):
@@ -161,9 +161,6 @@
                     else:
                         ref[here, k * half :] = found[0][:, :half].astype(BF16)
 
-        tiles = [pltpu.roll(own_ref[t].astype(jnp.float32), turn, 1) for t in range(taps)]
-        for n, chunks in enumerate(layouts):
-            put(table_refs[2 * n], chunks, tiles)
         tiles = []
         for g in range(2 * groups):
             at = g % groups
@@ -173,17 +170,56 @@
             tile = jnp.where(core_ref[0] == g // groups, mine, theirs).T
             tiles += [tile[t * part : (t + 1) * part] for t in range(size)]
         for n, chunks in enumerate(layouts):
-            put(table_refs[2 * n + 1], chunks, tiles)
+            put(table_refs[n], chunks, tiles)
 
     shapes = [jax.ShapeDtypeStruct((3 * outs, len(chunks) * half), BF16) for chunks in layouts]
     return pl.pallas_call(
         body,
-        out_shape=tuple(shape for shape in shapes for _ in range(2)),
-        in_specs=[SMEM, SMEM, *[VMEM] * (size + 2)],
-        out_specs=[VMEM] * (2 * len(layouts)),
+        out_shape=tuple(shapes),
+        in_specs=[SMEM, *[VMEM] * (size + 1)],
+        out_specs=[VMEM] * len(layouts),
         compiler_params=pltpu.CompilerParams(vmem_limit_bytes=8 * MIB),
-        name="weights",
-    )(core, place, own, others, *received)
+        name="weights_back",
+    )(core, others, *received)
+
+
+def weights_ahead(place, own, size, layouts):
+    taps, outs, chans = own.shape
+    part = chans // size
+    half = chans // 2
+
+    def body(place_ref, own_ref, *table_refs):
+        turn = lax.rem(size - place_ref[0] + 1, size) * part
+        low = lax.broadcasted_iota(jnp.int32, (outs, chans), 1) < half
+
+        def put(ref, chunks, tiles):
+            for c in range(3):
+                here = slice(c * outs, (c + 1) * outs)
+                for k in range(0, len(chunks), 2):
+                    found = []
+                    for side, (n, at) in enumerate(chunks[k : k + 2]):
+                        tile = tiles[3 * at + c]
+                        found.append(tile if n == side else pltpu.roll(tile, half, 1))
+                    if len(found) == 2:
+                        both = jnp.where(low, *found)
+                        ref[here, k * half : (k + 2) * half] = both.astype(BF16)
+                    else:
+                        ref[here, k * half :] = found[0][:, :half].astype(BF16)
+
+        tiles = [pltpu.roll(own_ref[t].astype(jnp.float32), turn, 1) for t in range(taps)]
+        for n, chunks in enumerate(layouts):
+            put(table_refs[n], chunks, tiles)
+
+    return pl.pallas_call(
+        body,
+        out_shape=tuple(
+            jax.ShapeDtypeStruct((3 * outs, len(chunks) * half), BF16) for chunks in layouts
+        ),
+        in_specs=[SMEM, VMEM],
+        out_specs=[VMEM] * len(layouts),
+        compiler_params=pltpu.CompilerParams(vmem_limit_bytes=8 * MIB),
+        name="weights_ahead",
+    )(place, own)
 
 
 def stage(core, halves, jobs, starts, shape, final):
@@ -334,6 +370,7 @@
     vol_edge, cot_edge, on_chip, off_chip, wide, *sent = prologue(
         core, me, volume, cotangent, own, bias, size
     )
+    ahead = weights_ahead(me, own, size, LAYOUTS)
     received = [sent[0], *[shifted(sent[size - d], -d) for d in range(1, size)]]
     cot_left_edge = shifted(cot_edge, 1)
     vol_right_edge = shifted(vol_edge, -1)
@@ -345,8 +382,8 @@
     near = pack_rows(core, (vol_left, cot_right), (vol_right_edge, cot_left_edge), received)
     near = swapped_rows(*near)
 
-    tables = weights(core, me, own, received, near[0], (INNER_ONE, OUTER_ONE, INNER_TWO, OUTER_TWO))
-    inner_one, outer_one, inner_two, outer_two = (tables[n : n + 2] for n in range(0, 8, 2))
+    back = weights_back(core, received, near[0], LAYOUTS)
+    inner_one, outer_one, inner_two, outer_two = zip(ahead, back)
 
     far = pack_rows(core, (), (vol_edge, cot_edge))
     far = swapped_rows(*far)

time: 69.9 us -> 70.5 us (level)
  no operation moved by 1% of the time
where the time goes in v6:
time: 70.5 us; the launch traced here: 70.1 us
  starting transfers between devices  32.8 us (47%)
  waiting for transfers between devices  23.3 us (33%)
  Pallas kernels  10.7 us (15%)
  local copies, waits for them, and re-layouts  2.3 us (3%)
  between operations  0.99 us (1%)
    ppermute x11, starting transfers between devices, shifted(): lax.ppermute(x, 'chan', [(i, (i + steps) % count) for i in range(count)])  17.7 us
    ppermute x11, waiting for transfers between devices, shifted(): lax.ppermute(x, 'chan', [(i, (i + steps) % count) for i in range(count)])  17.6 us
    ppermute x3, starting transfers between devices, swapped_rows(): off_chip = lax.ppermute(off_chip, 'space', far)  15 us
    pallas_call x3, Pallas kernels, stage(): pl.pallas_call(body, out_shape=(out, out), in_specs=[SMEM, *[VMEM] * (len...  7.41 us
    ppermute x3, waiting for transfers between devices, swapped_rows(): off_chip = lax.ppermute(off_chip, 'space', far)  5.72 us
    pallas_call x1, Pallas kernels, prologue(): pl.pallas_call(body, out_shape=(*[two] * 4, jax.ShapeDtypeStruct((outs, c...  2.57 us
    unnamed x16, local copies, waits for them, and re-layouts  2.3 us
  transfers between devices with their start and end apart: 17, of which 4 were waited for; matrix products, arithmetic and copies ran while one was open for 0% of the time, Pallas kernels for 10%

profile of v6, /device:TPU:24, one launch (start us, length us, event | category | flops | bytes accessed | tf_op | source)
XLA Modules:
  0.0 70.1 jit_solution(17777689009071608550)
XLA Ops:
  0.6 1.6 %collective-permute-start = (bf16[16,4,32,128]{3,2,1,0:T(8,128)(2,1)}, bf16[16,4,32,128]{3,2,1,0:T(8,128)(2,1)S(1)}, u32[]{:S(2)}, u32[]{:S(2)}) collective-permute-start(bf16[16,4,32,128]{3,2,1,0:T(8,128)(2,1)} %refs_1_.3), channel_id=1, source_target_pairs={{0,1},{1,2},{2,3},{3,0},{4,5},{5,6},{6,7},{7,4},{8,9},{9,10},{10,1... | collective-permute-start | bytes 1572872 | tf_op jit(solution)/shard_map/ppermute | solution.py:24
  2.2 1.7 %collective-permute-start.1 = (bf16[16,4,32,128]{3,2,1,0:T(8,128)(2,1)}, bf16[16,4,32,128]{3,2,1,0:T(8,128)(2,1)S(1)}, u32[]{:S(2)}, u32[]{:S(2)}) collective-permute-start(bf16[16,4,32,128]{3,2,1,0:T(8,128)(2,1)} %refs_2_.3), channel_id=1, source_target_pairs={{0,3},{1,0},{2,1},{3,2},{4,7},{5,4},{6,5},{7,6},{8,11},{9,8},{10,9... | collective-permute-start | bytes 1572872 | tf_op jit(solution)/shard_map/ppermute | solution.py:24
  3.9 2.6 %prologue.1 = (bf16[2,16,32,128]{3,2,1,0:T(8,128)(2,1)}, bf16[2,16,32,128]{3,2,1,0:T(8,128)(2,1)}, bf16[2,16,32,128]{3,2,1,0:T(8,128)(2,1)}, bf16[2,16,32,128]{3...) custom-call(s32[1]{0:T(128)} %bitcast.core_ref, ...), custom_call_target="tpu_custom_call" | custom-call | tf_op jit(solution)/shard_map/prologue/pallas_call | solution.py:123
  6.5 1.5 %collective-permute-start.2 = (bf16[2,16,32,128]{3,2,1,0:T(8,128)(2,1)}, bf16[2,16,32,128]{3,2,1,0:T(8,128)(2,1)S(1)}, u32[]{:S(2)}, u32[]{:S(2)}) collective-permute-start(bf16[2,16,32,128]{3,2,1,0:T(8,128)(2,1)} %get-tuple-element.31), channel_id=1, source_target_pairs={{0,3},{1,0},{2,1},{3,2},{4,7},{5,4},{6,5},{7,6},{8,11},{9,8},{10,9... | collective-permute-start | bytes 786440 | tf_op jit(solution)/shard_map/ppermute | solution.py:24
  8.1 0.5 collective-permute-start.4
  8.5 2.8 %collective-permute-start.5 = (bf16[4,32,128]{2,1,0:T(8,128)(2,1)}, bf16[4,32,128]{2,1,0:T(8,128)(2,1)S(1)}, u32[]{:S(2)}, u32[]{:S(2)}) collective-permute-start(bf16[4,32,128]{2,1,0:T(8,128)(2,1)} %get-tuple-element.35), channel_id=1, source_target_pairs={{0,3},{1,0},{2,1},{3,2},{4,7},{5,4},{6,5},{7,6},{8,11},{9,8},{10,9... | collective-permute-start | bytes 98312 | tf_op jit(solution)/shard_map/ppermute | solution.py:24
  11.3 10.8 %collective-permute-done.5.refs_5_.refs_1_ = bf16[4,32,128]{2,1,0:T(8,128)(2,1)S(1)} collective-permute-done((bf16[4,32,128]{2,1,0:T(8,128)(2,1)}, bf16[4,32,128]{2,1,0:T(8,128)(2,1)S(1)}, u32[]{:S(2)}, u32[]{:S(2)}) %collective-permute-start.5) | collective-permute-done | bytes 32800 | tf_op jit(solution)/shard_map/ppermute | solution.py:24
  22.1 2.7 %collective-permute-start.6 = (bf16[4,32,128]{2,1,0:T(8,128)(2,1)}, bf16[4,32,128]{2,1,0:T(8,128)(2,1)S(1)}, u32[]{:S(2)}, u32[]{:S(2)}) collective-permute-start(bf16[4,32,128]{2,1,0:T(8,128)(2,1)} %get-tuple-element.36), channel_id=1, source_target_pairs={{0,2},{1,3},{2,0},{3,1},{4,6},{5,7},{6,4},{7,5},{8,10},{9,11},{10,... | collective-permute-start | bytes 98312 | tf_op jit(solution)/shard_map/ppermute | solution.py:24
  24.8 2.9 %collective-permute-done.6.refs_6_.refs_2_ = bf16[4,32,128]{2,1,0:T(8,128)(2,1)S(1)} collective-permute-done((bf16[4,32,128]{2,1,0:T(8,128)(2,1)}, bf16[4,32,128]{2,1,0:T(8,128)(2,1)S(1)}, u32[]{:S(2)}, u32[]{:S(2)}) %collective-permute-start.6) | collective-permute-done | bytes 32800 | tf_op jit(solution)/shard_map/ppermute | solution.py:24
  27.7 1.5 %collective-permute-start.7 = (bf16[4,32,128]{2,1,0:T(8,128)(2,1)}, bf16[4,32,128]{2,1,0:T(8,128)(2,1)S(1)}, u32[]{:S(2)}, u32[]{:S(2)}) collective-permute-start(bf16[4,32,128]{2,1,0:T(8,128)(2,1)} %get-tuple-element.37), channel_id=1, source_target_pairs={{0,1},{1,2},{2,3},{3,0},{4,5},{5,6},{6,7},{7,4},{8,9},{9,10},{10,1... | collective-permute-start | bytes 98312 | tf_op jit(solution)/shard_map/ppermute | solution.py:24
  29.2 3.8 %collective-permute-done.7.refs_7_.refs_3_ = bf16[4,32,128]{2,1,0:T(8,128)(2,1)S(1)} collective-permute-done((bf16[4,32,128]{2,1,0:T(8,128)(2,1)}, bf16[4,32,128]{2,1,0:T(8,128)(2,1)S(1)}, u32[]{:S(2)}, u32[]{:S(2)}) %collective-permute-start.7) | collective-permute-done | bytes 32800 | tf_op jit(solution)/shard_map/ppermute | solution.py:24
  33.1 0.7 %copy-done.3 = bf16[4,32,128]{2,1,0:T(8,128)(2,1)S(1)} copy-done((bf16[4,32,128]{2,1,0:T(8,128)(2,1)S(1)}, bf16[4,32,128]{2,1,0:T(8,128)(2,1)}, u32[]{:S(2)}) %copy-start.3) | copy-done | bytes 32792
  34.1 0.8 %copy-done.7 = bf16[2,16,32,128]{3,2,1,0:T(8,128)(2,1)S(1)} copy-done((bf16[2,16,32,128]{3,2,1,0:T(8,128)(2,1)S(1)}, bf16[2,16,32,128]{3,2,1,0:T(8,128)(2,1)}, u32[]{:S(2)}) %copy-start.7) | copy-done | bytes 262168
  35.6 3.0 %collective-permute-start.12 = (bf16[2,16,32,128]{3,2,1,0:T(8,128)(2,1)S(1)}, bf16[2,16,32,128]{3,2,1,0:T(8,128)(2,1)S(1)}, u32[]{:S(2)}, u32[]{:S(2)}) collective-permute-start(bf16[2,16,32,128]{3,2,1,0:T(8,128)(2,1)S(1)} %get-tuple-element.42), channel_id=1, source_target_pairs={{0,3},{1,0},{2,1},{3,2},{4,7},{5,4},{6,5},{7,6},{8,11},{9,8},{10,9... | collective-permute-start | bytes 786440 | tf_op jit(solution)/shard_map/ppermute | solution.py:24
  38.6 7.2 %collective-permute-start.9 = (bf16[4,16,32,128]{3,2,1,0:T(8,128)(2,1)S(1)}, bf16[4,16,32,128]{3,2,1,0:T(8,128)(2,1)S(1)}, u32[]{:S(2)}, u32[]{:S(2)}) collective-permute-start(bf16[4,16,32,128]{3,2,1,0:T(8,128)(2,1)S(1)} %get-tuple-element.39), channel_id=1, source_target_pairs={{4,8},{8,4},{12,16},{16,12},{20,24},{24,20},{28,32},{32,28},{36,40... | collective-permute-start | bytes 1572872 | tf_op jit(solution)/shard_map/ppermute | solution.py:31
  45.8 1.9 %collective-permute-start.16 = (bf16[2,16,32,128]{3,2,1,0:T(8,128)(2,1)S(1)}, bf16[2,16,32,128]{3,2,1,0:T(8,128)(2,1)S(1)}, u32[]{:S(2)}, u32[]{:S(2)}) collective-permute-start(bf16[2,16,32,128]{3,2,1,0:T(8,128)(2,1)S(1)} %copy-done.6), channel_id=1, source_target_pairs={{4,8},{8,4},{12,16},{16,12},{20,24},{24,20},{28,32},{32,28},{36,40... | collective-permute-start | bytes 786440 | tf_op jit(solution)/shard_map/ppermute | solution.py:31
  47.7 0.6 collective-permute-start.3
  48.3 1.5 %collective-permute-start.11 = (bf16[4,16,32,128]{3,2,1,0:T(8,128)(2,1)S(1)}, bf16[4,16,32,128]{3,2,1,0:T(8,128)(2,1)S(1)}, u32[]{:S(2)}, u32[]{:S(2)}) collective-permute-start(bf16[4,16,32,128]{3,2,1,0:T(8,128)(2,1)S(1)} %get-tuple-element.41), channel_id=1, source_target_pairs={{0,1},{1,2},{2,3},{3,0},{4,5},{5,6},{6,7},{7,4},{8,9},{9,10},{10,1... | collective-permute-start | bytes 1572872 | tf_op jit(solution)/shard_map/ppermute | solution.py:24
  49.9 5.7 %collective-permute-done.16.refs_5_ = bf16[2,16,32,128]{3,2,1,0:T(8,128)(2,1)S(1)} collective-permute-done((bf16[2,16,32,128]{3,2,1,0:T(8,128)(2,1)S(1)}, bf16[2,16,32,128]{3,2,1,0:T(8,128)(2,1)S(1)}, u32[]{:S(2)}, u32[]{:S(2)}) %collective-permute-start.16) | collective-permute-done | bytes 262176 | tf_op jit(solution)/shard_map/ppermute | solution.py:31
  55.6 5.9 %collective-permute-start.14 = (bf16[2,16,32,128]{3,2,1,0:T(8,128)(2,1)S(1)}, bf16[2,16,32,128]{3,2,1,0:T(8,128)(2,1)S(1)}, u32[]{:S(2)}, u32[]{:S(2)}) collective-permute-start(bf16[2,16,32,128]{3,2,1,0:T(8,128)(2,1)S(1)} %get-tuple-element.44), channel_id=1, source_target_pairs={{4,8},{8,4},{12,16},{16,12},{20,24},{24,20},{28,32},{32,28},{36,40... | collective-permute-start | bytes 786440 | tf_op jit(solution)/shard_map/ppermute | solution.py:31
  62.0 0.4 copy-done.5
  62.5 1.5 %shard_map.61 = (f32[16,2,32,128]{3,2,1,0:T(8,128)S(1)}, f32[16,2,32,128]{3,2,1,0:T(8,128)S(1)}) custom-call(s32[1]{0:T(128)} %bitcast.core_ref, bf16[16,4,32,128]{3,2,1,0:T(8,128)(2,1)S(1)} %collective-permute-done.vn.refs_0_, bf16[16,4,32,128]{3,2,1,0:T(8,128)(2,1)S(1)} %copy-done, bf16[16,4,32,128]{3,2,1,0:T(8,128)(2,1)S(1)} %copy-done.1, ...), custom_call_target="tpu_custom_call" | custom-call | flops 805306368 | bytes 6291456 | tf_op jit(solution)/shard_map/pallas_call | solution.py:346
  64.0 2.1 %shard_map.62 = (f32[16,2,32,128]{3,2,1,0:T(8,128)S(1)}, f32[16,2,32,128]{3,2,1,0:T(8,128)S(1)}) custom-call(s32[1]{0:T(128)} %bitcast.core_ref, bf16[16,4,32,128]{3,2,1,0:T(8,128)(2,1)S(1)} %collective-permute-done.vn.refs_0_, bf16[5,16,32,128]{3,2,1,0:T(8,128)(2,1)S(1)} %collective-permute-done.8.others_ref.refs_1_.refs_6_, ...), custom_call_target="tpu_custom_call" | custom-call | flops 1207959552 | bytes 6291456 | tf_op jit(solution)/shard_map/pallas_call | solution.py:346
  66.2 3.8 %shard_map.63 = (bf16[16,4,32,128]{3,2,1,0:T(8,128)(2,1)}, bf16[16,4,32,128]{3,2,1,0:T(8,128)(2,1)}) custom-call(s32[1]{0:T(128)} %bitcast.core_ref, bf16[16,4,32,128]{3,2,1,0:T(8,128)(2,1)S(1)} %collective-permute-done.vn.refs_0_, bf16[16,4,32,128]{3,2,1,0:T(8,128)(2,1)S(1)} %copy-done, bf16[16,4,32,128]{3,2,1,0:T(8,128)(2,1)S(1)} %copy-done.1, ...), custom_call_target="tpu_custom_call" | custom-call | flops 1610612736 | bytes 6291456 | tf_op jit(solution)/shard_map/pallas_call | solution.py:346
  (35 shorter events, 1.6 us)
Async XLA Ops:
  0.6 32.5 %collective-permute-start = (bf16[16,4,32,128]{3,2,1,0:T(8,128)(2,1)}, bf16[16,4,32,128]{3,2,1,0:T(8,128)(2,1)S(1)}, u32[]{:S(2)}, u32[]{:S(2)}) collective-permute-start(bf16[16,4,32,128]{3,2,1,0:T(8,128)(2,1)} %refs_1_.3), channel_id=1, source_target_pairs={{0,1},{1,2},{2,3},{3,0},{4,5},{5,6},{6,7},{7,4},{8,9},{9,10},{10,1... | collective-permute-start | bytes 1572872 | tf_op jit(solution)/shard_map/ppermute | solution.py:24
  2.2 30.9 %collective-permute-start.1 = (bf16[16,4,32,128]{3,2,1,0:T(8,128)(2,1)}, bf16[16,4,32,128]{3,2,1,0:T(8,128)(2,1)S(1)}, u32[]{:S(2)}, u32[]{:S(2)}) collective-permute-start(bf16[16,4,32,128]{3,2,1,0:T(8,128)(2,1)} %refs_2_.3), channel_id=1, source_target_pairs={{0,3},{1,0},{2,1},{3,2},{4,7},{5,4},{6,5},{7,6},{8,11},{9,8},{10,9... | collective-permute-start | bytes 1572872 | tf_op jit(solution)/shard_map/ppermute | solution.py:24
  6.5 26.6 %collective-permute-start.2 = (bf16[2,16,32,128]{3,2,1,0:T(8,128)(2,1)}, bf16[2,16,32,128]{3,2,1,0:T(8,128)(2,1)S(1)}, u32[]{:S(2)}, u32[]{:S(2)}) collective-permute-start(bf16[2,16,32,128]{3,2,1,0:T(8,128)(2,1)} %get-tuple-element.31), channel_id=1, source_target_pairs={{0,3},{1,0},{2,1},{3,2},{4,7},{5,4},{6,5},{7,6},{8,11},{9,8},{10,9... | collective-permute-start | bytes 786440 | tf_op jit(solution)/shard_map/ppermute | solution.py:24
  8.1 25.0 %collective-permute-start.4 = (bf16[2,16,32,128]{3,2,1,0:T(8,128)(2,1)}, bf16[2,16,32,128]{3,2,1,0:T(8,128)(2,1)S(1)}, u32[]{:S(2)}, u32[]{:S(2)}) collective-permute-start(bf16[2,16,32,128]{3,2,1,0:T(8,128)(2,1)} %get-tuple-element.33), channel_id=1, source_target_pairs={{0,1},{1,2},{2,3},{3,0},{4,5},{5,6},{6,7},{7,4},{8,9},{9,10},{10,1... | collective-permute-start | bytes 786440 | tf_op jit(solution)/shard_map/ppermute | solution.py:24
  8.5 13.6 %collective-permute-start.5 = (bf16[4,32,128]{2,1,0:T(8,128)(2,1)}, bf16[4,32,128]{2,1,0:T(8,128)(2,1)S(1)}, u32[]{:S(2)}, u32[]{:S(2)}) collective-permute-start(bf16[4,32,128]{2,1,0:T(8,128)(2,1)} %get-tuple-element.35), channel_id=1, source_target_pairs={{0,3},{1,0},{2,1},{3,2},{4,7},{5,4},{6,5},{7,6},{8,11},{9,8},{10,9... | collective-permute-start | bytes 98312 | tf_op jit(solution)/shard_map/ppermute | solution.py:24
  22.1 5.6 %collective-permute-start.6 = (bf16[4,32,128]{2,1,0:T(8,128)(2,1)}, bf16[4,32,128]{2,1,0:T(8,128)(2,1)S(1)}, u32[]{:S(2)}, u32[]{:S(2)}) collective-permute-start(bf16[4,32,128]{2,1,0:T(8,128)(2,1)} %get-tuple-element.36), channel_id=1, source_target_pairs={{0,2},{1,3},{2,0},{3,1},{4,6},{5,7},{6,4},{7,5},{8,10},{9,11},{10,... | collective-permute-start | bytes 98312 | tf_op jit(solution)/shard_map/ppermute | solution.py:24
  27.7 5.3 %collective-permute-start.7 = (bf16[4,32,128]{2,1,0:T(8,128)(2,1)}, bf16[4,32,128]{2,1,0:T(8,128)(2,1)S(1)}, u32[]{:S(2)}, u32[]{:S(2)}) collective-permute-start(bf16[4,32,128]{2,1,0:T(8,128)(2,1)} %get-tuple-element.37), channel_id=1, source_target_pairs={{0,1},{1,2},{2,3},{3,0},{4,5},{5,6},{6,7},{7,4},{8,9},{9,10},{10,1... | collective-permute-start | bytes 98312 | tf_op jit(solution)/shard_map/ppermute | solution.py:24
  33.1 0.8 %copy-start.3 = (bf16[4,32,128]{2,1,0:T(8,128)(2,1)S(1)}, bf16[4,32,128]{2,1,0:T(8,128)(2,1)}, u32[]{:S(2)}) copy-start(bf16[4,32,128]{2,1,0:T(8,128)(2,1)} %get-tuple-element.34.refs_4_.refs_0_) | copy-start | bytes 98308
  33.9 0.9 %copy-start.7 = (bf16[2,16,32,128]{3,2,1,0:T(8,128)(2,1)S(1)}, bf16[2,16,32,128]{3,2,1,0:T(8,128)(2,1)}, u32[]{:S(2)}) copy-start(bf16[2,16,32,128]{3,2,1,0:T(8,128)(2,1)} %get-tuple-element.53) | copy-start | bytes 786436
  33.9 1.1 %copy-start = (bf16[16,4,32,128]{3,2,1,0:T(8,128)(2,1)S(1)}, bf16[16,4,32,128]{3,2,1,0:T(8,128)(2,1)}, u32[]{:S(2)}) copy-start(bf16[16,4,32,128]{3,2,1,0:T(8,128)(2,1)} %refs_1_.3) | copy-start | bytes 1572868
  33.9 1.3 %copy-start.1 = (bf16[16,4,32,128]{3,2,1,0:T(8,128)(2,1)S(1)}, bf16[16,4,32,128]{3,2,1,0:T(8,128)(2,1)}, u32[]{:S(2)}) copy-start(bf16[16,4,32,128]{3,2,1,0:T(8,128)(2,1)} %refs_2_.3) | copy-start | bytes 1572868
  34.0 21.6 %collective-permute-start.8 = (bf16[5,16,32,128]{3,2,1,0:T(8,128)(2,1)S(1)}, bf16[5,16,32,128]{3,2,1,0:T(8,128)(2,1)S(1)}, u32[]{:S(2)}, u32[]{:S(2)}) collective-permute-start(bf16[5,16,32,128]{3,2,1,0:T(8,128)(2,1)S(1)} %get-tuple-element.38), channel_id=1, source_target_pairs={{0,4},{4,0},{8,12},{12,8},{16,20},{20,16},{24,28},{28,24},{32,36},... | collective-permute-start | bytes 1966088 | tf_op jit(solution)/shard_map/ppermute | solution.py:32
  34.8 10.9 %copy-start.6 = (bf16[2,16,32,128]{3,2,1,0:T(8,128)(2,1)S(1)}, bf16[2,16,32,128]{3,2,1,0:T(8,128)(2,1)}, u32[]{:S(2)}) copy-start(bf16[2,16,32,128]{3,2,1,0:T(8,128)(2,1)} %get-tuple-element.54) | copy-start | bytes 786436
  34.8 10.9 %collective-permute-start.15 = (bf16[2,16,32,128]{3,2,1,0:T(8,128)(2,1)S(1)}, bf16[2,16,32,128]{3,2,1,0:T(8,128)(2,1)S(1)}, u32[]{:S(2)}, u32[]{:S(2)}) collective-permute-start(bf16[2,16,32,128]{3,2,1,0:T(8,128)(2,1)S(1)} %copy-done.7), channel_id=1, source_target_pairs={{0,4},{4,0},{8,12},{12,8},{16,20},{20,16},{24,28},{28,24},{32,36},... | collective-permute-start | bytes 786440 | tf_op jit(solution)/shard_map/ppermute | solution.py:32
  35.3 12.4 %collective-permute-start.10 = (bf16[2,16,32,128]{3,2,1,0:T(8,128)(2,1)S(1)}, bf16[2,16,32,128]{3,2,1,0:T(8,128)(2,1)S(1)}, u32[]{:S(2)}, u32[]{:S(2)}) collective-permute-start(bf16[2,16,32,128]{3,2,1,0:T(8,128)(2,1)S(1)} %get-tuple-element.40), channel_id=1, source_target_pairs={{0,1},{1,2},{2,3},{3,0},{4,5},{5,6},{6,7},{7,4},{8,9},{9,10},{10,1... | collective-permute-start | bytes 786440 | tf_op jit(solution)/shard_map/ppermute | solution.py:24
  35.6 12.7 %collective-permute-start.12 = (bf16[2,16,32,128]{3,2,1,0:T(8,128)(2,1)S(1)}, bf16[2,16,32,128]{3,2,1,0:T(8,128)(2,1)S(1)}, u32[]{:S(2)}, u32[]{:S(2)}) collective-permute-start(bf16[2,16,32,128]{3,2,1,0:T(8,128)(2,1)S(1)} %get-tuple-element.42), channel_id=1, source_target_pairs={{0,3},{1,0},{2,1},{3,2},{4,7},{5,4},{6,5},{7,6},{8,11},{9,8},{10,9... | collective-permute-start | bytes 786440 | tf_op jit(solution)/shard_map/ppermute | solution.py:24
  38.6 25.4 %collective-permute-start.9 = (bf16[4,16,32,128]{3,2,1,0:T(8,128)(2,1)S(1)}, bf16[4,16,32,128]{3,2,1,0:T(8,128)(2,1)S(1)}, u32[]{:S(2)}, u32[]{:S(2)}) collective-permute-start(bf16[4,16,32,128]{3,2,1,0:T(8,128)(2,1)S(1)} %get-tuple-element.39), channel_id=1, source_target_pairs={{4,8},{8,4},{12,16},{16,12},{20,24},{24,20},{28,32},{32,28},{36,40... | collective-permute-start | bytes 1572872 | tf_op jit(solution)/shard_map/ppermute | solution.py:31
  45.8 9.8 %collective-permute-start.16 = (bf16[2,16,32,128]{3,2,1,0:T(8,128)(2,1)S(1)}, bf16[2,16,32,128]{3,2,1,0:T(8,128)(2,1)S(1)}, u32[]{:S(2)}, u32[]{:S(2)}) collective-permute-start(bf16[2,16,32,128]{3,2,1,0:T(8,128)(2,1)S(1)} %copy-done.6), channel_id=1, source_target_pairs={{4,8},{8,4},{12,16},{16,12},{20,24},{24,20},{28,32},{32,28},{36,40... | collective-permute-start | bytes 786440 | tf_op jit(solution)/shard_map/ppermute | solution.py:31
  47.7 18.4 %collective-permute-start.3 = (bf16[4,16,32,128]{3,2,1,0:T(8,128)(2,1)S(1)}, bf16[4,16,32,128]{3,2,1,0:T(8,128)(2,1)S(1)}, u32[]{:S(2)}, u32[]{:S(2)}) collective-permute-start(bf16[4,16,32,128]{3,2,1,0:T(8,128)(2,1)S(1)} %get-tuple-element.32), channel_id=1, source_target_pairs={{0,3},{1,0},{2,1},{3,2},{4,7},{5,4},{6,5},{7,6},{8,11},{9,8},{10,9... | collective-permute-start | bytes 1572872 | tf_op jit(solution)/shard_map/ppermute | solution.py:24
  48.3 13.2 %copy-start.2 = (bf16[27,128,32]{1,2,0:T(8,128)(2,1)S(1)}, bf16[27,128,32]{1,2,0:T(8,128)(2,1)}, u32[]{:S(2)}) copy-start(bf16[27,128,32]{1,2,0:T(8,128)(2,1)} %param.5) | copy-start | bytes 663556
  48.3 17.8 %collective-permute-start.11 = (bf16[4,16,32,128]{3,2,1,0:T(8,128)(2,1)S(1)}, bf16[4,16,32,128]{3,2,1,0:T(8,128)(2,1)S(1)}, u32[]{:S(2)}, u32[]{:S(2)}) collective-permute-start(bf16[4,16,32,128]{3,2,1,0:T(8,128)(2,1)S(1)} %get-tuple-element.41), channel_id=1, source_target_pairs={{0,1},{1,2},{2,3},{3,0},{4,5},{5,6},{6,7},{7,4},{8,9},{9,10},{10,1... | collective-permute-start | bytes 1572872 | tf_op jit(solution)/shard_map/ppermute | solution.py:24
  55.6 10.6 %collective-permute-start.13 = (bf16[2,16,32,128]{3,2,1,0:T(8,128)(2,1)S(1)}, bf16[2,16,32,128]{3,2,1,0:T(8,128)(2,1)S(1)}, u32[]{:S(2)}, u32[]{:S(2)}) collective-permute-start(bf16[2,16,32,128]{3,2,1,0:T(8,128)(2,1)S(1)} %get-tuple-element.43), channel_id=1, source_target_pairs={{0,4},{4,0},{8,12},{12,8},{16,20},{20,16},{24,28},{28,24},{32,36},... | collective-permute-start | bytes 786440 | tf_op jit(solution)/shard_map/ppermute | solution.py:32
  55.6 6.2 %copy-start.4 = (bf16[4,32,128]{2,1,0:T(8,128)(2,1)S(1)}, bf16[4,32,128]{2,1,0:T(8,128)(2,1)}, u32[]{:S(2)}) copy-start(bf16[4,32,128]{2,1,0:T(8,128)(2,1)} %get-tuple-element.34.refs_4_.refs_0_) | copy-start | bytes 98308
  55.6 10.6 %collective-permute-start.14 = (bf16[2,16,32,128]{3,2,1,0:T(8,128)(2,1)S(1)}, bf16[2,16,32,128]{3,2,1,0:T(8,128)(2,1)S(1)}, u32[]{:S(2)}, u32[]{:S(2)}) collective-permute-start(bf16[2,16,32,128]{3,2,1,0:T(8,128)(2,1)S(1)} %get-tuple-element.44), channel_id=1, source_target_pairs={{4,8},{8,4},{12,16},{16,12},{20,24},{24,20},{28,32},{32,28},{36,40... | collective-permute-start | bytes 786440 | tf_op jit(solution)/shard_map/ppermute | solution.py:31
  (1 other events, 0.7 us)
